TPU v7x, 512 devices: a whole 4x8x8 slice. The times are simulated.
512 devices in a mesh: wide: 64 (over y, z), narrow: 8 (over x, core).
Axes of the slice: x: 4, y: 8, z: 8, core: 2. Of those that a mesh axis runs over, the one named last changes fastest.
Arguments:
- node_rows: bfloat16 [1048576, 128], P(('wide', 'narrow')), may hold values from -6 to 6
- tile_values: bfloat16 [8192, 128, 128], P(('wide', 'narrow')), may hold values from -0.25 to 0.25
- tile_owner: int32 [8192, 1], P(('wide', 'narrow')), may hold values from 0 to 63; in each aligned block of 16 rows (0 to 15, 16 to 31, ...) at most 2 rows name the same one
- tile_block: int32 [8192], P(('wide', 'narrow')), may hold values from 0 to 15
- edge_degree: int32 [65536], P('wide'), may hold values from 1 to 4
- w_in: bfloat16 [128, 512], replicated, may hold values from -0.5 to 0.5
- w_out: bfloat16 [512, 128], replicated, may hold values from -0.25 to 0.25
Outputs:
- node_out: bfloat16 [1048576, 128], P(('wide', 'narrow'))
Inputs may be any that keep to these rules, and one draw needn't show every extreme that they name: `tile_owner`: among the 16 tiles of one device at most 2 name the same owner, and in every draw some device has 2 tiles that name one owner.
All inputs are finite; a program needn't handle non-finite values.
Results may differ from a plain program's by a relative error of at most 0.0038.
Values may be sent and summed in bfloat16 or wider, within the bound.
A program may use at most 192 MiB of HBM per device.

v0:
```python
import jax
import jax.numpy as jnp
from jax import lax
from jax.sharding import PartitionSpec as P


def edge_network(summed, degrees, w_in, w_out):
    edge_in = (summed / degrees.astype(jnp.float32)[:, None]).astype(jnp.bfloat16)
    pre_act = jnp.dot(edge_in, w_in, preferred_element_type=jnp.float32)
    hidden = jax.nn.silu(pre_act).astype(jnp.bfloat16)
    return jnp.dot(hidden, w_out, preferred_element_type=jnp.float32).astype(jnp.bfloat16)


def body(node_rows, tile_values, tile_owner, tile_block, edge_degree, w_in, w_out):
    owners = lax.axis_size("wide")
    tile_count, block_size, _ = tile_values.shape
    channels = node_rows.shape[1]
    node_block_count = node_rows.shape[0] // block_size
    edge_row_count = edge_degree.shape[0]
    edge_blocks = edge_row_count // block_size
    per_block = tile_count // edge_blocks
    capacity = max(2, 2 * tile_count // owners)
    slot_count = owners * capacity
    target = tile_owner[:, 0]
    positions = jnp.arange(tile_count, dtype=jnp.int32)
    earlier = (target[:, None] == target[None, :]) & (positions[None, :] < positions[:, None])
    order_in = jnp.sum(earlier.astype(jnp.int32), axis=1)
    slot_of = target * capacity + order_in
    slot_ids = jnp.arange(slot_count, dtype=jnp.int32)
    matches = slot_of[:, None] == slot_ids[None, :]
    wanted_out = jnp.sum(jnp.where(matches, tile_block[:, None] + 1, 0), axis=0) - 1
    wanted = lax.all_to_all(
        wanted_out.reshape(owners, capacity), "wide", split_axis=0, concat_axis=0, tiled=True
    ).reshape(slot_count)
    filled = wanted >= 0
    block_ids = jnp.arange(node_block_count, dtype=jnp.int32)
    selector = (wanted[None, :] == block_ids[:, None]).astype(jnp.bfloat16)
    grouped = tile_values.reshape(edge_blocks, per_block, block_size, block_size)
    current = node_rows
    node_blocks = current.reshape(node_block_count, block_size, channels)
    picked = jnp.where(
        filled[:, None, None], node_blocks[jnp.maximum(wanted, 0)], jnp.zeros((), jnp.bfloat16)
    )
    arrived = lax.all_to_all(
        picked.reshape(owners, capacity, block_size, channels),
        "wide",
        split_axis=0,
        concat_axis=0,
        tiled=True,
    )
    tile_rows = arrived.reshape(slot_count, block_size, channels)[slot_of]
    partial_value = jnp.einsum(
        "tij,tjc->tic", tile_values, tile_rows, preferred_element_type=jnp.float32
    )
    partial_value = jnp.sum(
        partial_value.reshape(edge_blocks, per_block, block_size, channels), axis=1
    )
    partial_value = partial_value.reshape(edge_row_count, channels)
    summed = lax.psum(partial_value, "narrow")
    edge_out = edge_network(summed, edge_degree, w_in, w_out)
    blocks_out = edge_out.reshape(edge_blocks, block_size, channels)
    tile_terms = jnp.einsum(
        "ekji,ejc->ekic", grouped, blocks_out, preferred_element_type=jnp.float32
    ).astype(jnp.bfloat16)
    outgoing = jnp.zeros((slot_count, block_size, channels), jnp.bfloat16)
    outgoing = outgoing.at[slot_of].set(tile_terms.reshape(tile_count, block_size, channels))
    returned = lax.all_to_all(
        outgoing.reshape(owners, capacity, block_size, channels),
        "wide",
        split_axis=0,
        concat_axis=0,
        tiled=True,
    )
    gathered = jnp.dot(
        selector,
        returned.reshape(slot_count, block_size * channels),
        preferred_element_type=jnp.float32,
    )
    current = (
        current.astype(jnp.float32) + gathered.reshape(node_block_count * block_size, channels)
    ).astype(jnp.bfloat16)
    return current


def solution(mesh):
    return jax.shard_map(
        body,
        mesh=mesh,
        in_specs=(
            P(("wide", "narrow"), None),
            P(("wide", "narrow"), None, None),
            P(("wide", "narrow"), None),
            P(("wide", "narrow")),
            P("wide"),
            P(),
            P(),
        ),
        out_specs=P(("wide", "narrow"), None),
        check_vma=False,
    )
```

profile of v0, /device:TPU:78, one launch (start us, length us, event | category | flops | bytes accessed | tf_op | source)
XLA Modules:
  0.0 432.3 jit_solution(3052882399509095070)
XLA Ops:
  6.5 0.0 copy-start
  6.5 0.7 broadcast_add_fusion.1
  7.3 0.9 convert_reduce_fusion
  8.2 0.7 fusion.12
  8.8 0.1 select_reduce_fusion
  8.9 0.1 sub.7
  9.1 25.6 %all_to_all.16 = s32[64,1,2]{2,1,0:T(1,128)S(1)} all-to-all(s32[64,1,2]{2,1,0:T(1,128)S(1)} %bitcast.50), channel_id=1, replica_groups=mesh['wide'=64,'narrow'=8] {'wide'}, dimensions={0} | all-to-all | bytes 1024 | tf_op jit(solution)/shard_map/all_to_all | solution.py:32
  34.7 0.1 copy.30
  34.8 0.1 copy.31
  35.0 0.5 broadcast.86
  35.5 0.8 fusion.13
  36.3 0.1 reshape.92
  36.5 4.1 gather_fusion
  40.6 4.5 %broadcast_select_fusion = bf16[64,2,128,128]{3,2,1,0:T(8,128)(2,1)} fusion(bf16[64,2,128,128]{3,2,1,0:T(8,128)(2,1)} %bitcast.46, pred[64,2]{1,0:T(8,128)(4,1)S(1)} %copy.31), kind=kLoop, calls=%fused_computation.6 | loop fusion | flops 2097152 | bytes 8388736 | tf_op jit(solution)/shard_map/jit(_where)/select_n | solution.py:41
  45.0 7.4 %all-to-all-start.1 = ((bf16[64,2,128,128]{3,2,1,0:T(8,128)(2,1)}), bf16[64,2,128,128]{3,2,1,0:T(8,128)(2,1)}, u32[]{:S(2)}, u32[]{:S(2)}) async-start(bf16[64,2,128,128]{3,2,1,0:T(8,128)(2,1)} %broadcast_select_fusion), calls=%async_computation.1 | async-start | bytes 8388608 | tf_op jit(solution)/shard_map/all_to_all | solution.py:44
  52.4 0.0 copy-start.2
  52.4 0.0 copy-start.3
  52.4 0.0 copy-start.4
  52.4 0.0 all-reduce.2.cloned.1.call-start
  52.5 118.3 %all-to-all-done.1 = bf16[64,2,128,128]{3,2,1,0:T(8,128)(2,1)} async-done(((bf16[64,2,128,128]{3,2,1,0:T(8,128)(2,1)}), bf16[64,2,128,128]{3,2,1,0:T(8,128)(2,1)}, u32[]{:S(2)}, u32[]{:S(2)}) %all-to-all-start.1) | async-done | bytes 4194336 | tf_op jit(solution)/shard_map/all_to_all | solution.py:44
  170.8 2.8 gather_fusion.1
  173.7 0.0 copy-done
  173.7 0.5 bitcast_reduce_fusion
  174.2 1.0 copy.33
  175.2 0.0 all-reduce.2.cloned.1.call-update
  175.2 0.0 copy-done.2
  175.2 77.9 %all-reduce.2.cloned.1.call-done = f32[1024,128]{1,0:T(8,128)} async-done(((f32[1024,128]{1,0:T(8,128)}), f32[1024,128]{1,0:T(8,128)}) %all-reduce.2.cloned.1.call-update) | async-done | bytes 524304 | tf_op jit(solution)/shard_map/psum | solution.py:59
  253.2 0.0 copy-done.3
  253.2 0.0 copy-done.4
  253.2 2.0 fusion.4
  255.2 0.4 convolution_convert_fusion
  255.6 0.3 copy.35
  255.9 3.0 broadcast_in_dim.40
  258.9 2.6 scatter_fusion
  261.5 13.4 %all-to-all-start.2 = ((bf16[64,2,128,128]{3,2,1,0:T(8,128)(2,1)}), bf16[64,2,128,128]{3,2,1,0:T(8,128)(2,1)}, u32[]{:S(2)}, u32[]{:S(2)}) async-start(bf16[64,2,128,128]{3,2,1,0:T(8,128)(2,1)} %bitcast.45), calls=%async_computation.2 | async-start | bytes 8388608 | tf_op jit(solution)/shard_map/all_to_all | solution.py:67
  274.8 0.0 copy-start.1
  274.9 0.1 eq.53
  275.0 144.9 %all-to-all-done.2 = bf16[64,2,128,128]{3,2,1,0:T(8,128)(2,1)} async-done(((bf16[64,2,128,128]{3,2,1,0:T(8,128)(2,1)}), bf16[64,2,128,128]{3,2,1,0:T(8,128)(2,1)}, u32[]{:S(2)}, u32[]{:S(2)}) %all-to-all-start.2) | async-done | bytes 4194336 | tf_op jit(solution)/shard_map/all_to_all | solution.py:67
  419.9 4.5 %fusion = f32[16,16384]{1,0:T(8,128)S(1)} fusion(bf16[16,8,128,128]{3,2,1,0:T(8,128)(2,1)} %bitcast.24, s32[128]{0:T(128)S(1)} %eq.53), kind=kOutput, calls=%fused_computation.3 | convolution fusion | flops 67110912 | bytes 5243392 | tf_op jit(solution)/shard_map/dot_general | solution.py:74
  424.4 0.2 reshape.89
  424.6 0.0 copy-done.1
  424.6 0.9 add_convert_fusion
  (5 shorter events, 0.1 us)
Async XLA Ops:
  6.5 167.1 %copy-start = (bf16[16,128,128]{2,1,0:T(8,128)(2,1)S(1)}, bf16[16,128,128]{2,1,0:T(8,128)(2,1)}, u32[]{:S(2)}) copy-start(bf16[16,128,128]{2,1,0:T(8,128)(2,1)} %param.8) | copy-start | bytes 1572868
  45.0 125.8 %all-to-all-start.1 = ((bf16[64,2,128,128]{3,2,1,0:T(8,128)(2,1)}), bf16[64,2,128,128]{3,2,1,0:T(8,128)(2,1)}, u32[]{:S(2)}, u32[]{:S(2)}) async-start(bf16[64,2,128,128]{3,2,1,0:T(8,128)(2,1)} %broadcast_select_fusion), calls=%async_computation.1 | async-start | bytes 8388608 | tf_op jit(solution)/shard_map/all_to_all | solution.py:44
  52.4 122.8 %copy-start.2 = (s32[1024]{0:T(1024)S(1)}, s32[1024]{0:T(1024)}, u32[]{:S(2)}) copy-start(s32[1024]{0:T(1024)} %param.11) | copy-start | bytes 12292
  52.4 200.8 %copy-start.3 = (bf16[512,128]{1,0:T(8,128)(2,1)S(1)}, bf16[512,128]{1,0:T(8,128)(2,1)}, u32[]{:S(2)}) copy-start(bf16[512,128]{1,0:T(8,128)(2,1)} %param.13) | copy-start | bytes 393220
  52.4 200.8 %copy-start.4 = (bf16[128,512]{1,0:T(8,128)(2,1)S(1)}, bf16[128,512]{1,0:T(8,128)(2,1)}, u32[]{:S(2)}) copy-start(bf16[128,512]{1,0:T(8,128)(2,1)} %param.12) | copy-start | bytes 393220
  52.4 200.8 %all-reduce.2.cloned.1.call-start = ((), (), s32[]{:S(2)}) async-start(), calls=%async_computation.3 | async-start | bytes 1048576 | tf_op jit(solution)/shard_map/psum | solution.py:59
  261.5 158.4 %all-to-all-start.2 = ((bf16[64,2,128,128]{3,2,1,0:T(8,128)(2,1)}), bf16[64,2,128,128]{3,2,1,0:T(8,128)(2,1)}, u32[]{:S(2)}, u32[]{:S(2)}) async-start(bf16[64,2,128,128]{3,2,1,0:T(8,128)(2,1)} %bitcast.45), calls=%async_computation.2 | async-start | bytes 8388608 | tf_op jit(solution)/shard_map/all_to_all | solution.py:67
  274.8 149.7 %copy-start.1 = (bf16[2048,128]{1,0:T(8,128)(2,1)S(1)}, bf16[2048,128]{1,0:T(8,128)(2,1)}, u32[]{:S(2)}) copy-start(bf16[2048,128]{1,0:T(8,128)(2,1)} %param.7) | copy-start | bytes 1572868
Sparse Core Ops, SparseCore 0:
  175.3 77.7 all-reduce.1
where the time goes:
time: 433 us; the launch traced here: 432 us
  waiting for transfers between devices  341 us (79%)
  blocking collectives  25.6 us (6%)
  starting transfers between devices  20.8 us (5%)
  local copies, waits for them, and re-layouts  15.1 us (3%)
  between operations  13.6 us (3%)
  other arithmetic  8.63 us (2%)
  matrix products  7.4 us (2%)
    all_to_all x1, waiting for transfers between devices, body(): lax.all_to_all(outgoing.reshape(owners, capacity, block_size, channels),...  145 us
    all_to_all x1, waiting for transfers between devices, body(): lax.all_to_all(picked.reshape(owners, capacity, block_size, channels), 'w...  118 us
    psum x1, waiting for transfers between devices, body(): summed = lax.psum(partial_value, 'narrow')  77.9 us
    all_to_all x1, blocking collectives, body(): lax.all_to_all(wanted_out.reshape(owners, capacity), 'wide', split_axis=0...  25.6 us
    all_to_all x1, starting transfers between devices, body(): lax.all_to_all(outgoing.reshape(owners, capacity, block_size, channels),...  13.4 us
  transfers between devices with their start and end apart: 3, of which 3 were waited for; matrix products, arithmetic and copies ran while one was open for 0% of the time, Pallas kernels for 0%

commit v1 on v0

--- a/solution.py
+++ b/solution.py
@@ -55,9 +55,18 @@
     partial_value = jnp.sum(
         partial_value.reshape(edge_blocks, per_block, block_size, channels), axis=1
     )
-    partial_value = partial_value.reshape(edge_row_count, channels)
-    summed = lax.psum(partial_value, "narrow")
-    edge_out = edge_network(summed, edge_degree, w_in, w_out)
+    groups = lax.axis_size("narrow")
+    me = lax.axis_index("narrow")
+    own_rows = edge_row_count // groups
+    pieces = lax.all_to_all(
+        partial_value.reshape(groups, own_rows, channels), "narrow", 0, 0, tiled=True
+    )
+    summed = jnp.sum(pieces, axis=0)
+    own_degree = lax.dynamic_slice_in_dim(edge_degree, me * own_rows, own_rows)
+    own_out = edge_network(summed, own_degree, w_in, w_out)
+    edge_out = lax.all_to_all(
+        jnp.broadcast_to(own_out[None], (groups, own_rows, channels)), "narrow", 0, 0, tiled=True
+    )
     blocks_out = edge_out.reshape(edge_blocks, block_size, channels)
     tile_terms = jnp.einsum(
         "ekji,ejc->ekic", grouped, blocks_out, preferred_element_type=jnp.float32

time: 433 us -> 365 us (0.84)
  the two profiles are of different devices: /device:TPU:78 before, /device:TPU:86 now
where the time goes in v1:
time: 365 us; the launch traced here: 364 us
  waiting for transfers between devices  264 us (72%)
  starting transfers between devices  35.5 us (10%)
  blocking collectives  34.6 us (9%)
  local copies, waits for them, and re-layouts  14.3 us (4%)
  other arithmetic  9.41 us (3%)
  matrix products  6.49 us (2%)
    all_to_all x1, waiting for transfers between devices, body(): lax.all_to_all(outgoing.reshape(owners, capacity, block_size, channels),...  140 us
    all_to_all x1, waiting for transfers between devices, body(): lax.all_to_all(picked.reshape(owners, capacity, block_size, channels), 'w...  117 us
    all_to_all x1, blocking collectives, body(): lax.all_to_all(wanted_out.reshape(owners, capacity), 'wide', split_axis=0...  24.7 us
    all_to_all x1, starting transfers between devices, body(): lax.all_to_all(outgoing.reshape(owners, capacity, block_size, channels),...  22.4 us
    all_to_all x1, blocking collectives, body(): lax.all_to_all(jnp.broadcast_to(own_out[None], (groups, own_rows, channel...  9.94 us
    all_to_all x1, starting transfers between devices, body(): lax.all_to_all(picked.reshape(owners, capacity, block_size, channels), 'w...  8.26 us
    all_to_all x1, waiting for transfers between devices, body(): lax.all_to_all(partial_value.reshape(groups, own_rows, channels), 'narrow...  7.52 us
  transfers between devices with their start and end apart: 3, of which 3 were waited for; matrix products, arithmetic and copies ran while one was open for 0% of the time, Pallas kernels for 0%

profile of v1, /device:TPU:86, one launch (start us, length us, event | category | flops | bytes accessed | tf_op | source)
XLA Modules:
  0.0 364.2 jit_solution(5281973286511648934)
XLA Ops:
  0.0 0.0 copy-start
  0.0 0.7 broadcast_add_fusion.1
  0.7 0.9 convert_reduce_fusion
  1.6 0.7 fusion.11
  2.3 0.1 select_reduce_fusion
  2.4 0.1 sub.7
  2.5 24.7 %all_to_all.26 = s32[64,1,2]{2,1,0:T(1,128)S(1)} all-to-all(s32[64,1,2]{2,1,0:T(1,128)S(1)} %bitcast.46), channel_id=1, replica_groups=mesh['wide'=64,'narrow'=8] {'wide'}, dimensions={0} | all-to-all | bytes 1024 | tf_op jit(solution)/shard_map/all_to_all | solution.py:32
  27.2 0.1 copy.27
  27.3 0.1 copy.28
  27.5 0.5 broadcast.87
  28.0 0.8 fusion.12
  28.8 0.1 reshape.85
  29.0 4.1 %gather_fusion = bf16[128,128,128]{2,1,0:T(8,128)(2,1)} fusion(bf16[16,128,128]{2,1,0:T(8,128)(2,1)} %bitcast.42, s32[1024]{0:T(1024)S(1)} %pad_clamp_fusion.1), kind=kCustom, calls=%fused_computation | custom fusion | bytes 8389120 | tf_op jit(solution)/shard_map/gather | solution.py:42
  33.1 4.5 %broadcast_select_fusion = bf16[64,2,128,128]{3,2,1,0:T(8,128)(2,1)} fusion(bf16[64,2,128,128]{3,2,1,0:T(8,128)(2,1)} %bitcast.44, pred[64,2]{1,0:T(8,128)(4,1)S(1)} %copy.28), kind=kLoop, calls=%fused_computation.6 | loop fusion | flops 2097152 | bytes 8388736 | tf_op jit(solution)/shard_map/jit(_where)/select_n | solution.py:41
  37.5 8.3 %all-to-all-start.1 = ((bf16[64,2,128,128]{3,2,1,0:T(8,128)(2,1)}), bf16[64,2,128,128]{3,2,1,0:T(8,128)(2,1)}, u32[]{:S(2)}, u32[]{:S(2)}) async-start(bf16[64,2,128,128]{3,2,1,0:T(8,128)(2,1)} %broadcast_select_fusion), calls=%async_computation.1 | async-start | bytes 8388608 | tf_op jit(solution)/shard_map/all_to_all | solution.py:44
  45.8 0.0 copy-start.2
  45.8 0.0 copy-start.3
  45.8 116.6 %all-to-all-done.1 = bf16[64,2,128,128]{3,2,1,0:T(8,128)(2,1)} async-done(((bf16[64,2,128,128]{3,2,1,0:T(8,128)(2,1)}), bf16[64,2,128,128]{3,2,1,0:T(8,128)(2,1)}, u32[]{:S(2)}, u32[]{:S(2)}) %all-to-all-start.1) | async-done | bytes 4194336 | tf_op jit(solution)/shard_map/all_to_all | solution.py:44
  162.5 2.8 gather_fusion.1
  165.3 0.0 copy-done
  165.3 1.3 bitcast_reduce_fusion
  166.6 4.8 %all-to-all-start.2 = ((f32[8,128,128]{1,2,0:T(8,128)}), f32[8,128,128]{1,2,0:T(8,128)S(1)}, u32[]{:S(2)}, u32[]{:S(2)}) async-start(f32[8,128,128]{1,2,0:T(8,128)} %bitcast_reduce_fusion), calls=%async_computation.2 | async-start | bytes 1048576 | tf_op jit(solution)/shard_map/all_to_all | solution.py:61
  171.4 0.8 dynamic-slice_convert_fusion
  172.2 7.5 %all-to-all-done.2 = f32[8,128,128]{1,2,0:T(8,128)S(1)} async-done(((f32[8,128,128]{1,2,0:T(8,128)}), f32[8,128,128]{1,2,0:T(8,128)S(1)}, u32[]{:S(2)}, u32[]{:S(2)}) %all-to-all-start.2) | async-done | bytes 524320 | tf_op jit(solution)/shard_map/all_to_all | solution.py:61
  179.7 0.0 copy-done.2
  179.7 0.0 copy-done.3
  179.7 0.4 convolution_convert_fusion.1
  180.1 0.1 copy.30
  180.3 9.9 %all_to_all.27 = bf16[8,128,128]{1,2,0:T(8,128)(2,1)S(1)} all-to-all(bf16[8,128,128]{1,2,0:T(8,128)(2,1)S(1)} %broadcast_in_dim.49), channel_id=1, replica_groups=mesh['wide'=64,'narrow'=8] {'narrow'}, dimensions={0} | all-to-all | bytes 524288 | tf_op jit(solution)/shard_map/all_to_all | solution.py:67
  190.2 0.3 convolution_convert_fusion
  190.5 0.3 copy.31
  190.8 3.0 broadcast_in_dim.30
  193.8 2.6 scatter_fusion
  196.4 22.4 %all-to-all-start.4 = ((bf16[64,2,128,128]{3,2,1,0:T(8,128)(2,1)}), bf16[64,2,128,128]{3,2,1,0:T(8,128)(2,1)}, u32[]{:S(2)}, u32[]{:S(2)}) async-start(bf16[64,2,128,128]{3,2,1,0:T(8,128)(2,1)} %bitcast.43), calls=%async_computation.4 | async-start | bytes 8388608 | tf_op jit(solution)/shard_map/all_to_all | solution.py:76
  218.9 0.0 copy-start.1
  218.9 0.1 eq.53
  219.0 139.6 %all-to-all-done.4 = bf16[64,2,128,128]{3,2,1,0:T(8,128)(2,1)} async-done(((bf16[64,2,128,128]{3,2,1,0:T(8,128)(2,1)}), bf16[64,2,128,128]{3,2,1,0:T(8,128)(2,1)}, u32[]{:S(2)}, u32[]{:S(2)}) %all-to-all-start.4) | async-done | bytes 4194336 | tf_op jit(solution)/shard_map/all_to_all | solution.py:76
  358.6 4.5 %fusion = f32[16,16384]{1,0:T(8,128)S(1)} fusion(bf16[16,8,128,128]{3,2,1,0:T(8,128)(2,1)} %bitcast.21, s32[128]{0:T(128)S(1)} %eq.53), kind=kOutput, calls=%fused_computation.3 | convolution fusion | flops 67110912 | bytes 5243392 | tf_op jit(solution)/shard_map/dot_general | solution.py:83
  363.1 0.2 reshape.82
  363.3 0.0 copy-done.1
  363.3 0.9 add_convert_fusion
  (6 shorter events, 0.1 us)
Async XLA Ops:
  0.0 165.3 %copy-start = (bf16[16,128,128]{2,1,0:T(8,128)(2,1)S(1)}, bf16[16,128,128]{2,1,0:T(8,128)(2,1)}, u32[]{:S(2)}) copy-start(bf16[16,128,128]{2,1,0:T(8,128)(2,1)} %param.8) | copy-start | bytes 1572868
  37.5 124.9 %all-to-all-start.1 = ((bf16[64,2,128,128]{3,2,1,0:T(8,128)(2,1)}), bf16[64,2,128,128]{3,2,1,0:T(8,128)(2,1)}, u32[]{:S(2)}, u32[]{:S(2)}) async-start(bf16[64,2,128,128]{3,2,1,0:T(8,128)(2,1)} %broadcast_select_fusion), calls=%async_computation.1 | async-start | bytes 8388608 | tf_op jit(solution)/shard_map/all_to_all | solution.py:44
  45.8 133.9 %copy-start.2 = (bf16[512,128]{1,0:T(8,128)(2,1)S(1)}, bf16[512,128]{1,0:T(8,128)(2,1)}, u32[]{:S(2)}) copy-start(bf16[512,128]{1,0:T(8,128)(2,1)} %param.13) | copy-start | bytes 393220
  45.8 133.9 %copy-start.3 = (bf16[128,512]{1,0:T(8,128)(2,1)S(1)}, bf16[128,512]{1,0:T(8,128)(2,1)}, u32[]{:S(2)}) copy-start(bf16[128,512]{1,0:T(8,128)(2,1)} %param.12) | copy-start | bytes 393220
  166.6 13.1 %all-to-all-start.2 = ((f32[8,128,128]{1,2,0:T(8,128)}), f32[8,128,128]{1,2,0:T(8,128)S(1)}, u32[]{:S(2)}, u32[]{:S(2)}) async-start(f32[8,128,128]{1,2,0:T(8,128)} %bitcast_reduce_fusion), calls=%async_computation.2 | async-start | bytes 1048576 | tf_op jit(solution)/shard_map/all_to_all | solution.py:61
  196.4 162.2 %all-to-all-start.4 = ((bf16[64,2,128,128]{3,2,1,0:T(8,128)(2,1)}), bf16[64,2,128,128]{3,2,1,0:T(8,128)(2,1)}, u32[]{:S(2)}, u32[]{:S(2)}) async-start(bf16[64,2,128,128]{3,2,1,0:T(8,128)(2,1)} %bitcast.43), calls=%async_computation.4 | async-start | bytes 8388608 | tf_op jit(solution)/shard_map/all_to_all | solution.py:76
  218.9 144.4 %copy-start.1 = (bf16[2048,128]{1,0:T(8,128)(2,1)S(1)}, bf16[2048,128]{1,0:T(8,128)(2,1)}, u32[]{:S(2)}) copy-start(bf16[2048,128]{1,0:T(8,128)(2,1)} %param.7) | copy-start | bytes 1572868

commit v2 on v1

--- a/solution.py
+++ b/solution.py
@@ -32,15 +32,12 @@
     wanted = lax.all_to_all(
         wanted_out.reshape(owners, capacity), "wide", split_axis=0, concat_axis=0, tiled=True
     ).reshape(slot_count)
-    filled = wanted >= 0
     block_ids = jnp.arange(node_block_count, dtype=jnp.int32)
     selector = (wanted[None, :] == block_ids[:, None]).astype(jnp.bfloat16)
     grouped = tile_values.reshape(edge_blocks, per_block, block_size, block_size)
     current = node_rows
     node_blocks = current.reshape(node_block_count, block_size, channels)
-    picked = jnp.where(
-        filled[:, None, None], node_blocks[jnp.maximum(wanted, 0)], jnp.zeros((), jnp.bfloat16)
-    )
+    picked = node_blocks[jnp.maximum(wanted, 0)]
     arrived = lax.all_to_all(
         picked.reshape(owners, capacity, block_size, channels),
         "wide",
@@ -71,8 +68,8 @@
     tile_terms = jnp.einsum(
         "ekji,ejc->ekic", grouped, blocks_out, preferred_element_type=jnp.float32
     ).astype(jnp.bfloat16)
-    outgoing = jnp.zeros((slot_count, block_size, channels), jnp.bfloat16)
-    outgoing = outgoing.at[slot_of].set(tile_terms.reshape(tile_count, block_size, channels))
+    tile_of_slot = jnp.sum(jnp.where(matches, positions[:, None], 0), axis=0)
+    outgoing = tile_terms.reshape(tile_count, block_size, channels)[tile_of_slot]
     returned = lax.all_to_all(
         outgoing.reshape(owners, capacity, block_size, channels),
         "wide",

time: 365 us -> 362 us (level)
  the two profiles are of different devices: /device:TPU:86 before, /device:TPU:80 now
where the time goes in v2:
time: 362 us; the launch traced here: 361 us
  waiting for transfers between devices  268 us (74%)
  starting transfers between devices  38.4 us (11%)
  blocking collectives  24.7 us (7%)
  local copies, waits for them, and re-layouts  18.3 us (5%)
  matrix products  6.48 us (2%)
  other arithmetic  4.91 us (1%)
    all_to_all x1, waiting for transfers between devices, body(): lax.all_to_all(outgoing.reshape(owners, capacity, block_size, channels),...  134 us
    all_to_all x1, waiting for transfers between devices, body(): lax.all_to_all(picked.reshape(owners, capacity, block_size, channels), 'w...  117 us
    all_to_all x1, blocking collectives, body(): lax.all_to_all(wanted_out.reshape(owners, capacity), 'wide', split_axis=0...  24.7 us
    all_to_all x1, starting transfers between devices, body(): lax.all_to_all(outgoing.reshape(owners, capacity, block_size, channels),...  22.4 us
    all_to_all x1, waiting for transfers between devices, body(): lax.all_to_all(partial_value.reshape(groups, own_rows, channels), 'narrow...  9.59 us
    gather x2, local copies, waits for them, and re-layouts, body(): tile_terms.reshape(tile_count, block_size, channels)[tile_of_slot]  9.44 us
    all_to_all x1, starting transfers between devices, body(): lax.all_to_all(picked.reshape(owners, capacity, block_size, channels), 'w...  8.24 us
    all_to_all x1, waiting for transfers between devices, body(): lax.all_to_all(jnp.broadcast_to(own_out[None], (groups, own_rows, channel...  7.43 us
  transfers between devices with their start and end apart: 4, of which 4 were waited for; matrix products, arithmetic and copies ran while one was open for 0% of the time, Pallas kernels for 0%

profile of v2, /device:TPU:80, one launch (start us, length us, event | category | flops | bytes accessed | tf_op | source)
XLA Modules:
  0.0 361.1 jit_solution(4674313666547759712)
XLA Ops:
  0.0 0.0 copy-start
  0.0 0.7 broadcast_add_fusion.1
  0.7 0.9 convert_reduce_fusion
  1.6 0.7 fusion.9
  2.3 0.1 select_reduce_fusion
  2.4 0.1 sub.7
  2.5 24.7 %all_to_all.26 = s32[64,1,2]{2,1,0:T(1,128)S(1)} all-to-all(s32[64,1,2]{2,1,0:T(1,128)S(1)} %bitcast.48), channel_id=1, replica_groups=mesh['wide'=64,'narrow'=8] {'wide'}, dimensions={0} | all-to-all | bytes 1024 | tf_op jit(solution)/shard_map/all_to_all | solution.py:32
  27.2 0.5 broadcast.105
  27.7 0.8 fusion.13
  28.5 0.1 reshape.90
  28.7 4.1 %gather_fusion = bf16[128,128,128]{2,1,0:T(8,128)(2,1)} fusion(bf16[16,128,128]{2,1,0:T(8,128)(2,1)} %bitcast.45, s32[1024]{0:T(1024)S(1)} %pad_clamp_fusion.2), kind=kCustom, calls=%fused_computation | custom fusion | bytes 8389120 | tf_op jit(solution)/shard_map/gather | solution.py:40
  32.8 8.2 %all-to-all-start.1 = ((bf16[64,2,128,128]{3,2,1,0:T(8,128)(2,1)}), bf16[64,2,128,128]{3,2,1,0:T(8,128)(2,1)}, u32[]{:S(2)}, u32[]{:S(2)}) async-start(bf16[64,2,128,128]{3,2,1,0:T(8,128)(2,1)} %bitcast.46), calls=%async_computation.1 | async-start | bytes 8388608 | tf_op jit(solution)/shard_map/all_to_all | solution.py:41
  41.0 0.0 copy-start.2
  41.0 0.0 copy-start.3
  41.1 116.6 %all-to-all-done.1 = bf16[64,2,128,128]{3,2,1,0:T(8,128)(2,1)} async-done(((bf16[64,2,128,128]{3,2,1,0:T(8,128)(2,1)}), bf16[64,2,128,128]{3,2,1,0:T(8,128)(2,1)}, u32[]{:S(2)}, u32[]{:S(2)}) %all-to-all-start.1) | async-done | bytes 4194336 | tf_op jit(solution)/shard_map/all_to_all | solution.py:41
  157.7 2.8 gather_fusion.1
  160.5 0.0 copy-done
  160.6 1.3 bitcast_reduce_fusion
  161.9 4.3 %all-to-all-start.2 = ((f32[8,128,128]{1,2,0:T(8,128)}), f32[8,128,128]{1,2,0:T(8,128)S(1)}, u32[]{:S(2)}, u32[]{:S(2)}) async-start(f32[8,128,128]{1,2,0:T(8,128)} %bitcast_reduce_fusion), calls=%async_computation.2 | async-start | bytes 1048576 | tf_op jit(solution)/shard_map/all_to_all | solution.py:58
  166.2 0.8 dynamic-slice_convert_fusion
  166.9 9.6 %all-to-all-done.2 = f32[8,128,128]{1,2,0:T(8,128)S(1)} async-done(((f32[8,128,128]{1,2,0:T(8,128)}), f32[8,128,128]{1,2,0:T(8,128)S(1)}, u32[]{:S(2)}, u32[]{:S(2)}) %all-to-all-start.2) | async-done | bytes 524320 | tf_op jit(solution)/shard_map/all_to_all | solution.py:58
  176.6 0.0 copy-done.2
  176.6 0.0 copy-done.3
  176.6 0.4 convolution_convert_fusion.1
  177.0 0.1 copy.20
  177.1 0.7 broadcast_in_dim.20
  177.8 3.4 all-to-all-start.3
  181.3 7.4 %all-to-all-done.3 = bf16[8,128,128]{1,2,0:T(8,128)(2,1)S(1)} async-done(((bf16[8,128,128]{1,2,0:T(8,128)(2,1)}), bf16[8,128,128]{1,2,0:T(8,128)(2,1)S(1)}, u32[]{:S(2)}, u32[]{:S(2)}) %all-to-all-start.3) | async-done | bytes 262176 | tf_op jit(solution)/shard_map/all_to_all | solution.py:64
  188.7 0.3 convolution_convert_fusion
  189.0 3.1 gather_fusion.2
  192.1 6.4 %copy.21 = bf16[128,128,128]{2,1,0:T(8,128)(2,1)} copy(bf16[128,128,128]{1,2,0:T(8,128)(2,1)} %gather_fusion.2) | data formatting | bytes 8388608 | tf_op jit(solution)/shard_map/gather | solution.py:72
  198.4 22.4 %all-to-all-start.4 = ((bf16[64,2,128,128]{3,2,1,0:T(8,128)(2,1)}), bf16[64,2,128,128]{3,2,1,0:T(8,128)(2,1)}, u32[]{:S(2)}, u32[]{:S(2)}) async-start(bf16[64,2,128,128]{3,2,1,0:T(8,128)(2,1)} %bitcast.47), calls=%async_computation.4 | async-start | bytes 8388608 | tf_op jit(solution)/shard_map/all_to_all | solution.py:73
  220.9 0.0 copy-start.1
  220.9 0.1 eq.55
  221.1 134.5 %all-to-all-done.4 = bf16[64,2,128,128]{3,2,1,0:T(8,128)(2,1)} async-done(((bf16[64,2,128,128]{3,2,1,0:T(8,128)(2,1)}), bf16[64,2,128,128]{3,2,1,0:T(8,128)(2,1)}, u32[]{:S(2)}, u32[]{:S(2)}) %all-to-all-start.4) | async-done | bytes 4194336 | tf_op jit(solution)/shard_map/all_to_all | solution.py:73
  355.5 4.5 %fusion = f32[16,16384]{1,0:T(8,128)S(1)} fusion(bf16[16,8,128,128]{3,2,1,0:T(8,128)(2,1)} %bitcast.22, s32[128]{0:T(128)S(1)} %eq.55), kind=kOutput, calls=%fused_computation.3 | convolution fusion | flops 67110912 | bytes 5243392 | tf_op jit(solution)/shard_map/dot_general | solution.py:80
  360.0 0.2 reshape.87
  360.2 0.0 copy-done.1
  360.2 0.9 add_convert_fusion
  (6 shorter events, 0.1 us)
Async XLA Ops:
  0.0 160.5 %copy-start = (bf16[16,128,128]{2,1,0:T(8,128)(2,1)S(1)}, bf16[16,128,128]{2,1,0:T(8,128)(2,1)}, u32[]{:S(2)}) copy-start(bf16[16,128,128]{2,1,0:T(8,128)(2,1)} %param.8) | copy-start | bytes 1572868
  32.8 124.9 %all-to-all-start.1 = ((bf16[64,2,128,128]{3,2,1,0:T(8,128)(2,1)}), bf16[64,2,128,128]{3,2,1,0:T(8,128)(2,1)}, u32[]{:S(2)}, u32[]{:S(2)}) async-start(bf16[64,2,128,128]{3,2,1,0:T(8,128)(2,1)} %bitcast.46), calls=%async_computation.1 | async-start | bytes 8388608 | tf_op jit(solution)/shard_map/all_to_all | solution.py:41
  41.0 135.5 %copy-start.2 = (bf16[512,128]{1,0:T(8,128)(2,1)S(1)}, bf16[512,128]{1,0:T(8,128)(2,1)}, u32[]{:S(2)}) copy-start(bf16[512,128]{1,0:T(8,128)(2,1)} %param.13) | copy-start | bytes 393220
  41.0 135.5 %copy-start.3 = (bf16[128,512]{1,0:T(8,128)(2,1)S(1)}, bf16[128,512]{1,0:T(8,128)(2,1)}, u32[]{:S(2)}) copy-start(bf16[128,512]{1,0:T(8,128)(2,1)} %param.12) | copy-start | bytes 393220
  161.9 14.7 %all-to-all-start.2 = ((f32[8,128,128]{1,2,0:T(8,128)}), f32[8,128,128]{1,2,0:T(8,128)S(1)}, u32[]{:S(2)}, u32[]{:S(2)}) async-start(f32[8,128,128]{1,2,0:T(8,128)} %bitcast_reduce_fusion), calls=%async_computation.2 | async-start | bytes 1048576 | tf_op jit(solution)/shard_map/all_to_all | solution.py:58
  177.8 10.9 %all-to-all-start.3 = ((bf16[8,128,128]{1,2,0:T(8,128)(2,1)}), bf16[8,128,128]{1,2,0:T(8,128)(2,1)S(1)}, u32[]{:S(2)}, u32[]{:S(2)}) async-start(bf16[8,128,128]{1,2,0:T(8,128)(2,1)} %broadcast_in_dim.20), calls=%async_computation.3 | async-start | bytes 524288 | tf_op jit(solution)/shard_map/all_to_all | solution.py:64
  198.4 157.1 %all-to-all-start.4 = ((bf16[64,2,128,128]{3,2,1,0:T(8,128)(2,1)}), bf16[64,2,128,128]{3,2,1,0:T(8,128)(2,1)}, u32[]{:S(2)}, u32[]{:S(2)}) async-start(bf16[64,2,128,128]{3,2,1,0:T(8,128)(2,1)} %bitcast.47), calls=%async_computation.4 | async-start | bytes 8388608 | tf_op jit(solution)/shard_map/all_to_all | solution.py:73
  220.9 139.3 %copy-start.1 = (bf16[2048,128]{1,0:T(8,128)(2,1)S(1)}, bf16[2048,128]{1,0:T(8,128)(2,1)}, u32[]{:S(2)}) copy-start(bf16[2048,128]{1,0:T(8,128)(2,1)} %param.7) | copy-start | bytes 1572868

commit v3 on v2

--- a/solution.py
+++ b/solution.py
@@ -1,7 +1,78 @@
+import functools
+
 import jax
 import jax.numpy as jnp
 from jax import lax
+from jax.experimental import pallas as pl
+from jax.experimental.pallas import tpu as pltpu
 from jax.sharding import PartitionSpec as P
+MESH = pl.DeviceIdType.MESH
+
+
+def _edge_kernel(groups, parts_ref, degree_ref, w_in_ref, w_out_ref, out_ref,
+                 inbox, stage, send_a, recv_a, send_b, recv_b):
+    me = lax.axis_index("narrow")
+    col = lax.axis_index("wide")
+    barrier = pltpu.get_barrier_semaphore()
+    for k in range(1, groups):
+        pl.semaphore_signal(barrier, inc=1, device_id=(col, lax.rem(me + k, groups)), device_id_type=MESH)
+    pl.semaphore_wait(barrier, groups - 1)
+
+    def first(d):
+        return pltpu.make_async_remote_copy(
+            src_ref=parts_ref.at[d], dst_ref=inbox.at[me], send_sem=send_a.at[d],
+            recv_sem=recv_a.at[me], device_id=(col, d), device_id_type=MESH)
+
+    for k in range(1, groups):
+        first(lax.rem(me + k, groups)).start()
+    total = parts_ref[me]
+    for k in range(1, groups):
+        d = lax.rem(me + k, groups)
+        s = lax.rem(me + groups - k, groups)
+        first(d).wait_send()
+        pltpu.make_async_remote_copy(
+            src_ref=parts_ref.at[s], dst_ref=inbox.at[s], send_sem=send_a.at[s],
+            recv_sem=recv_a.at[s], device_id=(col, s), device_id_type=MESH).wait_recv()
+        total = total + inbox[s]
+    edge_in = (total / degree_ref[...]).astype(jnp.bfloat16)
+    pre = jnp.dot(edge_in, w_in_ref[...], preferred_element_type=jnp.float32)
+    hidden = (pre * jax.nn.sigmoid(pre)).astype(jnp.bfloat16)
+    own = jnp.dot(hidden, w_out_ref[...], preferred_element_type=jnp.float32).astype(jnp.bfloat16)
+    stage[...] = own
+    out_ref[me] = own
+
+    def second(d):
+        return pltpu.make_async_remote_copy(
+            src_ref=stage, dst_ref=out_ref.at[me], send_sem=send_b.at[d],
+            recv_sem=recv_b.at[me], device_id=(col, d), device_id_type=MESH)
+
+    for k in range(1, groups):
+        second(lax.rem(me + k, groups)).start()
+    for k in range(1, groups):
+        d = lax.rem(me + k, groups)
+        s = lax.rem(me + groups - k, groups)
+        second(d).wait_send()
+        pltpu.make_async_remote_copy(
+            src_ref=stage, dst_ref=out_ref.at[s], send_sem=send_b.at[s],
+            recv_sem=recv_b.at[s], device_id=(col, s), device_id_type=MESH).wait_recv()
+
+
+def edge_exchange(parts, degree, w_in, w_out, collective_id):
+    groups, rows, channels = parts.shape
+    vmem = pl.BlockSpec(memory_space=pltpu.VMEM)
+    return pl.pallas_call(
+        functools.partial(_edge_kernel, groups),
+        out_shape=jax.ShapeDtypeStruct((groups, rows, channels), jnp.bfloat16),
+        in_specs=[vmem] * 4,
+        out_specs=vmem,
+        scratch_shapes=[
+            pltpu.VMEM((groups, rows, channels), jnp.float32),
+            pltpu.VMEM((rows, channels), jnp.bfloat16),
+            pltpu.SemaphoreType.DMA((groups,)), pltpu.SemaphoreType.DMA((groups,)),
+            pltpu.SemaphoreType.DMA((groups,)), pltpu.SemaphoreType.DMA((groups,)),
+        ],
+        compiler_params=pltpu.CompilerParams(collective_id=collective_id, has_side_effects=True),
+    )(parts, degree, w_in, w_out)
 
 
 def edge_network(summed, degrees, w_in, w_out):
@@ -55,14 +126,13 @@
     groups = lax.axis_size("narrow")
     me = lax.axis_index("narrow")
     own_rows = edge_row_count // groups
-    pieces = lax.all_to_all(
-        partial_value.reshape(groups, own_rows, channels), "narrow", 0, 0, tiled=True
-    )
-    summed = jnp.sum(pieces, axis=0)
     own_degree = lax.dynamic_slice_in_dim(edge_degree, me * own_rows, own_rows)
-    own_out = edge_network(summed, own_degree, w_in, w_out)
-    edge_out = lax.all_to_all(
-        jnp.broadcast_to(own_out[None], (groups, own_rows, channels)), "narrow", 0, 0, tiled=True
+    edge_out = edge_exchange(
+        partial_value.reshape(groups, own_rows, channels),
+        own_degree.astype(jnp.float32)[:, None],
+        w_in,
+        w_out,
+        0,
     )
     blocks_out = edge_out.reshape(edge_blocks, block_size, channels)
     tile_terms = jnp.einsum(

time: 362 us -> 360 us (level)
  the two profiles are of different devices: /device:TPU:80 before, /device:TPU:212 now
where the time goes in v3:
time: 360 us; the launch traced here: 359 us
  waiting for transfers between devices  256 us (71%)
  starting transfers between devices  34.6 us (10%)
  blocking collectives  21.1 us (6%)
  local copies, waits for them, and re-layouts  19.2 us (5%)
  Pallas kernels  17.3 us (5%)
  matrix products  6.32 us (2%)
  other arithmetic  4.83 us (1%)
    all_to_all x1, waiting for transfers between devices, body(): lax.all_to_all(outgoing.reshape(owners, capacity, block_size, channels),...  143 us
    all_to_all x1, waiting for transfers between devices, body(): lax.all_to_all(picked.reshape(owners, capacity, block_size, channels), 'w...  113 us
    all_to_all x1, starting transfers between devices, body(): lax.all_to_all(outgoing.reshape(owners, capacity, block_size, channels),...  24.7 us
    all_to_all x1, blocking collectives, body(): lax.all_to_all(wanted_out.reshape(owners, capacity), 'wide', split_axis=0...  21.1 us
    pallas_call x1, Pallas kernels, edge_exchange(): pl.pallas_call(functools.partial(_edge_kernel, groups), out_shape=jax.Sha...  17.3 us
    all_to_all x1, starting transfers between devices, body(): lax.all_to_all(picked.reshape(owners, capacity, block_size, channels), 'w...  9.97 us
    gather x2, local copies, waits for them, and re-layouts, body(): tile_terms.reshape(tile_count, block_size, channels)[tile_of_slot]  9.44 us
  transfers between devices with their start and end apart: 2, of which 2 were waited for; matrix products, arithmetic and copies ran while one was open for 0% of the time, Pallas kernels for 0%

profile of v3, /device:TPU:212, one launch (start us, length us, event | category | flops | bytes accessed | tf_op | source)
XLA Modules:
  0.0 359.3 jit_solution(16838281290372795251)
XLA Ops:
  0.0 0.0 copy-start
  0.0 0.9 convert_reduce_fusion
  0.9 0.7 fusion.6
  1.6 0.7 broadcast_add_fusion.1
  2.2 0.1 select_reduce_fusion
  2.3 0.1 sub.7
  2.5 21.1 %all_to_all.16 = s32[64,1,2]{2,1,0:T(1,128)S(1)} all-to-all(s32[64,1,2]{2,1,0:T(1,128)S(1)} %bitcast.48), channel_id=1, replica_groups=mesh['wide'=64,'narrow'=8] {'wide'}, dimensions={0} | all-to-all | bytes 1024 | tf_op jit(solution)/shard_map/all_to_all | solution.py:103
  23.6 0.5 broadcast.101
  24.1 0.8 fusion.9
  24.9 0.1 reshape.88
  25.1 4.1 %gather_fusion = bf16[128,128,128]{2,1,0:T(8,128)(2,1)} fusion(bf16[16,128,128]{2,1,0:T(8,128)(2,1)} %bitcast.45, s32[1024]{0:T(1024)S(1)} %pad_clamp_fusion.2), kind=kCustom, calls=%fused_computation | custom fusion | bytes 8389120 | tf_op jit(solution)/shard_map/gather | solution.py:111
  29.2 10.0 %all-to-all-start.1 = ((bf16[64,2,128,128]{3,2,1,0:T(8,128)(2,1)}), bf16[64,2,128,128]{3,2,1,0:T(8,128)(2,1)}, u32[]{:S(2)}, u32[]{:S(2)}) async-start(bf16[64,2,128,128]{3,2,1,0:T(8,128)(2,1)} %bitcast.46), calls=%async_computation.1 | async-start | bytes 8388608 | tf_op jit(solution)/shard_map/all_to_all | solution.py:112
  39.2 0.8 convert_bitcast_fusion
  39.9 0.7 copy.23.degree_ref
  40.7 112.9 %all-to-all-done.1 = bf16[64,2,128,128]{3,2,1,0:T(8,128)(2,1)} async-done(((bf16[64,2,128,128]{3,2,1,0:T(8,128)(2,1)}), bf16[64,2,128,128]{3,2,1,0:T(8,128)(2,1)}, u32[]{:S(2)}, u32[]{:S(2)}) %all-to-all-start.1) | async-done | bytes 4194336 | tf_op jit(solution)/shard_map/all_to_all | solution.py:112
  153.6 2.8 gather_fusion.1
  156.5 0.0 copy-done
  156.5 0.5 bitcast_reduce_fusion
  157.0 1.0 copy.22.parts_ref
  158.0 17.3 %shard_map.73 = bf16[8,128,128]{2,1,0:T(8,128)(2,1)} custom-call(f32[8,128,128]{2,1,0:T(8,128)} %copy.22.parts_ref, f32[128,1]{1,0:T(8,128)} %copy.23.degree_ref, bf16[128,512]{1,0:T(8,128)(2,1)} %w_in_ref.1, bf16[512,128]{1,0:T(8,128)(2,1)} %w_out_ref.1), custom_call_target="tpu_custom_call" | custom-call | tf_op jit(solution)/shard_map/pallas_call | solution.py:63
  175.3 1.3 convolution_convert_fusion
  176.6 3.1 gather_fusion.2
  179.7 6.4 %copy.25 = bf16[128,128,128]{2,1,0:T(8,128)(2,1)} copy(bf16[128,128,128]{1,2,0:T(8,128)(2,1)} %gather_fusion.2) | data formatting | bytes 8388608 | tf_op jit(solution)/shard_map/gather | solution.py:142
  186.1 24.7 %all-to-all-start.2 = ((bf16[64,2,128,128]{3,2,1,0:T(8,128)(2,1)}), bf16[64,2,128,128]{3,2,1,0:T(8,128)(2,1)}, u32[]{:S(2)}, u32[]{:S(2)}) async-start(bf16[64,2,128,128]{3,2,1,0:T(8,128)(2,1)} %bitcast.47), calls=%async_computation.2 | async-start | bytes 8388608 | tf_op jit(solution)/shard_map/all_to_all | solution.py:143
  210.7 0.0 copy-start.1
  210.7 0.1 eq.55
  210.9 142.8 %all-to-all-done.2 = bf16[64,2,128,128]{3,2,1,0:T(8,128)(2,1)} async-done(((bf16[64,2,128,128]{3,2,1,0:T(8,128)(2,1)}), bf16[64,2,128,128]{3,2,1,0:T(8,128)(2,1)}, u32[]{:S(2)}, u32[]{:S(2)}) %all-to-all-start.2) | async-done | bytes 4194336 | tf_op jit(solution)/shard_map/all_to_all | solution.py:143
  353.7 4.5 %fusion = f32[16,16384]{1,0:T(8,128)S(1)} fusion(bf16[16,8,128,128]{3,2,1,0:T(8,128)(2,1)} %bitcast.23, s32[128]{0:T(128)S(1)} %eq.55), kind=kOutput, calls=%fused_computation.3 | convolution fusion | flops 67110912 | bytes 5243392 | tf_op jit(solution)/shard_map/dot_general | solution.py:150
  358.2 0.2 reshape.85
  358.4 0.0 copy-done.1
  358.4 0.9 add_convert_fusion
  (5 shorter events, 0.0 us)
Async XLA Ops:
  0.0 156.5 %copy-start = (bf16[16,128,128]{2,1,0:T(8,128)(2,1)S(1)}, bf16[16,128,128]{2,1,0:T(8,128)(2,1)}, u32[]{:S(2)}) copy-start(bf16[16,128,128]{2,1,0:T(8,128)(2,1)} %param.8) | copy-start | bytes 1572868
  29.2 124.4 %all-to-all-start.1 = ((bf16[64,2,128,128]{3,2,1,0:T(8,128)(2,1)}), bf16[64,2,128,128]{3,2,1,0:T(8,128)(2,1)}, u32[]{:S(2)}, u32[]{:S(2)}) async-start(bf16[64,2,128,128]{3,2,1,0:T(8,128)(2,1)} %bitcast.46), calls=%async_computation.1 | async-start | bytes 8388608 | tf_op jit(solution)/shard_map/all_to_all | solution.py:112
  186.1 167.6 %all-to-all-start.2 = ((bf16[64,2,128,128]{3,2,1,0:T(8,128)(2,1)}), bf16[64,2,128,128]{3,2,1,0:T(8,128)(2,1)}, u32[]{:S(2)}, u32[]{:S(2)}) async-start(bf16[64,2,128,128]{3,2,1,0:T(8,128)(2,1)} %bitcast.47), calls=%async_computation.2 | async-start | bytes 8388608 | tf_op jit(solution)/shard_map/all_to_all | solution.py:143
  210.7 147.6 %copy-start.1 = (bf16[2048,128]{1,0:T(8,128)(2,1)S(1)}, bf16[2048,128]{1,0:T(8,128)(2,1)}, u32[]{:S(2)}) copy-start(bf16[2048,128]{1,0:T(8,128)(2,1)} %param.7) | copy-start | bytes 1572868

commit v4 on v3

--- a/solution.py
+++ b/solution.py
@@ -9,29 +9,41 @@
 MESH = pl.DeviceIdType.MESH
 
 
-def _edge_kernel(groups, parts_ref, degree_ref, w_in_ref, w_out_ref, out_ref,
-                 inbox, stage, send_a, recv_a, send_b, recv_b):
+def _round_kernel(groups, per_block, slot_of_ref, slot_tile_ref, arrived_ref, tiles_ref,
+                  degree_ref, w_in_ref, w_out_ref, out_ref,
+                  parts, inbox, stage, edge_out, terms, send_a, recv_a, send_b, recv_b):
     me = lax.axis_index("narrow")
     col = lax.axis_index("wide")
+    tile_count = tiles_ref.shape[0]
     barrier = pltpu.get_barrier_semaphore()
     for k in range(1, groups):
         pl.semaphore_signal(barrier, inc=1, device_id=(col, lax.rem(me + k, groups)), device_id_type=MESH)
+
+    for e in range(tile_count // per_block):
+        acc = None
+        for k in range(per_block):
+            t = e * per_block + k
+            rows = arrived_ref[slot_of_ref[t]]
+            p = jnp.dot(tiles_ref[t], rows, preferred_element_type=jnp.float32)
+            acc = p if acc is None else acc + p
+        parts[e] = acc
+
     pl.semaphore_wait(barrier, groups - 1)
 
     def first(d):
         return pltpu.make_async_remote_copy(
-            src_ref=parts_ref.at[d], dst_ref=inbox.at[me], send_sem=send_a.at[d],
+            src_ref=parts.at[d], dst_ref=inbox.at[me], send_sem=send_a.at[d],
             recv_sem=recv_a.at[me], device_id=(col, d), device_id_type=MESH)
 
     for k in range(1, groups):
         first(lax.rem(me + k, groups)).start()
-    total = parts_ref[me]
+    total = parts[me]
     for k in range(1, groups):
         d = lax.rem(me + k, groups)
         s = lax.rem(me + groups - k, groups)
         first(d).wait_send()
         pltpu.make_async_remote_copy(
-            src_ref=parts_ref.at[s], dst_ref=inbox.at[s], send_sem=send_a.at[s],
+            src_ref=parts.at[s], dst_ref=inbox.at[s], send_sem=send_a.at[s],
             recv_sem=recv_a.at[s], device_id=(col, s), device_id_type=MESH).wait_recv()
         total = total + inbox[s]
     edge_in = (total / degree_ref[...]).astype(jnp.bfloat16)
@@ -39,11 +51,11 @@
     hidden = (pre * jax.nn.sigmoid(pre)).astype(jnp.bfloat16)
     own = jnp.dot(hidden, w_out_ref[...], preferred_element_type=jnp.float32).astype(jnp.bfloat16)
     stage[...] = own
-    out_ref[me] = own
+    edge_out[me] = own
 
     def second(d):
         return pltpu.make_async_remote_copy(
-            src_ref=stage, dst_ref=out_ref.at[me], send_sem=send_b.at[d],
+            src_ref=stage, dst_ref=edge_out.at[me], send_sem=send_b.at[d],
             recv_sem=recv_b.at[me], device_id=(col, d), device_id_type=MESH)
 
     for k in range(1, groups):
@@ -53,26 +65,43 @@
         s = lax.rem(me + groups - k, groups)
         second(d).wait_send()
         pltpu.make_async_remote_copy(
-            src_ref=stage, dst_ref=out_ref.at[s], send_sem=send_b.at[s],
+            src_ref=stage, dst_ref=edge_out.at[s], send_sem=send_b.at[s],
             recv_sem=recv_b.at[s], device_id=(col, s), device_id_type=MESH).wait_recv()
 
+    for t in range(tile_count):
+        term = lax.dot_general(
+            tiles_ref[t], edge_out[t // per_block], (((0,), (0,)), ((), ())),
+            preferred_element_type=jnp.float32)
+        terms[t] = term.astype(jnp.bfloat16)
 
-def edge_exchange(parts, degree, w_in, w_out, collective_id):
-    groups, rows, channels = parts.shape
+    def place(slot, carry):
+        out_ref[slot] = terms[slot_tile_ref[slot]]
+        return carry
+
+    lax.fori_loop(0, out_ref.shape[0], place, 0)
+
+
+def round_kernel(slot_of, slot_tile, arrived, tiles, degree, w_in, w_out, groups, per_block):
+    slots, rows, channels = arrived.shape
     vmem = pl.BlockSpec(memory_space=pltpu.VMEM)
+    smem = pl.BlockSpec(memory_space=pltpu.SMEM)
     return pl.pallas_call(
-        functools.partial(_edge_kernel, groups),
-        out_shape=jax.ShapeDtypeStruct((groups, rows, channels), jnp.bfloat16),
-        in_specs=[vmem] * 4,
+        functools.partial(_round_kernel, groups, per_block),
+        out_shape=jax.ShapeDtypeStruct((slots, rows, channels), jnp.bfloat16),
+        in_specs=[smem, smem] + [vmem] * 5,
         out_specs=vmem,
         scratch_shapes=[
             pltpu.VMEM((groups, rows, channels), jnp.float32),
+            pltpu.VMEM((groups, rows, channels), jnp.float32),
             pltpu.VMEM((rows, channels), jnp.bfloat16),
+            pltpu.VMEM((groups, rows, channels), jnp.bfloat16),
+            pltpu.VMEM(tiles.shape, jnp.bfloat16),
             pltpu.SemaphoreType.DMA((groups,)), pltpu.SemaphoreType.DMA((groups,)),
             pltpu.SemaphoreType.DMA((groups,)), pltpu.SemaphoreType.DMA((groups,)),
         ],
-        compiler_params=pltpu.CompilerParams(collective_id=collective_id, has_side_effects=True),
-    )(parts, degree, w_in, w_out)
+        compiler_params=pltpu.CompilerParams(
+            collective_id=0, has_side_effects=True, vmem_limit_bytes=48 * 1024 * 1024),
+    )(slot_of, slot_tile, arrived, tiles, degree, w_in, w_out)
 
 
 def edge_network(summed, degrees, w_in, w_out):
@@ -105,7 +134,6 @@
     ).reshape(slot_count)
     block_ids = jnp.arange(node_block_count, dtype=jnp.int32)
     selector = (wanted[None, :] == block_ids[:, None]).astype(jnp.bfloat16)
-    grouped = tile_values.reshape(edge_blocks, per_block, block_size, block_size)
     current = node_rows
     node_blocks = current.reshape(node_block_count, block_size, channels)
     picked = node_blocks[jnp.maximum(wanted, 0)]
@@ -116,30 +144,22 @@
         concat_axis=0,
         tiled=True,
     )
-    tile_rows = arrived.reshape(slot_count, block_size, channels)[slot_of]
-    partial_value = jnp.einsum(
-        "tij,tjc->tic", tile_values, tile_rows, preferred_element_type=jnp.float32
-    )
-    partial_value = jnp.sum(
-        partial_value.reshape(edge_blocks, per_block, block_size, channels), axis=1
-    )
     groups = lax.axis_size("narrow")
     me = lax.axis_index("narrow")
     own_rows = edge_row_count // groups
     own_degree = lax.dynamic_slice_in_dim(edge_degree, me * own_rows, own_rows)
-    edge_out = edge_exchange(
-        partial_value.reshape(groups, own_rows, channels),
+    tile_of_slot = jnp.sum(jnp.where(matches, positions[:, None], 0), axis=0)
+    outgoing = round_kernel(
+        slot_of,
+        tile_of_slot,
+        arrived.reshape(slot_count, block_size, channels),
+        tile_values,
         own_degree.astype(jnp.float32)[:, None],
         w_in,
         w_out,
-        0,
+        groups,
+        per_block,
     )
-    blocks_out = edge_out.reshape(edge_blocks, block_size, channels)
-    tile_terms = jnp.einsum(
-        "ekji,ejc->ekic", grouped, blocks_out, preferred_element_type=jnp.float32
-    ).astype(jnp.bfloat16)
-    tile_of_slot = jnp.sum(jnp.where(matches, positions[:, None], 0), axis=0)
-    outgoing = tile_terms.reshape(tile_count, block_size, channels)[tile_of_slot]
     returned = lax.all_to_all(
         outgoing.reshape(owners, capacity, block_size, channels),
         "wide",

time: 360 us -> 348 us (0.967)
  local copies, waits for them, and re-layouts: 19.2 us -> 7.27 us
    gather x3 -> x0, local copies, waits for them, and re-layouts: 12.3 us -> none  [the longest x2 9.44 us: body(): tile_terms.reshape(tile_count, block_size, channels)[tile_of_slot]]
where the time goes in v4:
time: 348 us
  waiting for transfers between devices  256 us (74%)
  starting transfers between devices  34.8 us (10%)
  blocking collectives  21.1 us (6%)
  Pallas kernels  19 us (5%)
  local copies, waits for them, and re-layouts  7.27 us (2%)
  other arithmetic  4.82 us (1%)
  matrix products  4.51 us (1%)
    all_to_all x1, waiting for transfers between devices, body(): lax.all_to_all(outgoing.reshape(owners, capacity, block_size, channels),...  143 us
    all_to_all x1, waiting for transfers between devices, body(): lax.all_to_all(picked.reshape(owners, capacity, block_size, channels), 'w...  114 us
    all_to_all x1, starting transfers between devices, body(): lax.all_to_all(outgoing.reshape(owners, capacity, block_size, channels),...  24.7 us
    all_to_all x1, blocking collectives, body(): lax.all_to_all(wanted_out.reshape(owners, capacity), 'wide', split_axis=0...  21.1 us
    pallas_call x1, Pallas kernels, round_kernel(): pl.pallas_call(functools.partial(_round_kernel, groups, per_block), out_s...  19 us
    all_to_all x1, starting transfers between devices, body(): lax.all_to_all(picked.reshape(owners, capacity, block_size, channels), 'w...  10.1 us
  transfers between devices with their start and end apart: 2, of which 2 were waited for; matrix products, arithmetic and copies ran while one was open for 0% of the time, Pallas kernels for 0%

profile of v4, /device:TPU:212, one launch (start us, length us, event | category | flops | bytes accessed | tf_op | source)
XLA Modules:
  0.0 347.9 jit_solution(16274338356403432764)
XLA Ops:
  0.0 0.9 convert_reduce_fusion
  0.9 0.7 fusion.5
  1.6 0.7 broadcast_add_fusion.1
  2.2 0.1 select_reduce_fusion.1
  2.3 0.1 sub.7
  2.5 21.1 %all_to_all.16 = s32[64,1,2]{2,1,0:T(1,128)S(1)} all-to-all(s32[64,1,2]{2,1,0:T(1,128)S(1)} %bitcast.23), channel_id=1, replica_groups=mesh['wide'=64,'narrow'=8] {'wide'}, dimensions={0} | all-to-all | bytes 1024 | tf_op jit(solution)/shard_map/all_to_all | solution.py:132
  23.6 0.5 broadcast.57
  24.1 0.8 fusion.6
  24.9 0.1 reshape.62
  25.1 4.1 %gather_fusion = bf16[128,128,128]{2,1,0:T(8,128)(2,1)} fusion(bf16[16,128,128]{2,1,0:T(8,128)(2,1)} %bitcast.21, s32[1024]{0:T(1024)S(1)} %pad_clamp_fusion), kind=kCustom, calls=%fused_computation | custom fusion | bytes 8389120 | tf_op jit(solution)/shard_map/gather | solution.py:139
  29.2 0.0 copy-start.5
  29.2 0.0 copy-start.1
  29.2 0.0 copy-start.2
  29.2 0.0 copy-start.3
  29.2 10.1 %all-to-all-start.1 = ((bf16[64,2,128,128]{3,2,1,0:T(8,128)(2,1)}), bf16[64,2,128,128]{3,2,1,0:T(8,128)(2,1)}, u32[]{:S(2)}, u32[]{:S(2)}) async-start(bf16[64,2,128,128]{3,2,1,0:T(8,128)(2,1)} %bitcast.22), calls=%async_computation.1 | async-start | bytes 8388608 | tf_op jit(solution)/shard_map/all_to_all | solution.py:140
  39.3 0.8 convert_bitcast_fusion
  40.1 0.1 copy.13.degree_ref
  40.2 0.0 copy-done.5
  40.2 113.6 %all-to-all-done.1 = bf16[64,2,128,128]{3,2,1,0:T(8,128)(2,1)} async-done(((bf16[64,2,128,128]{3,2,1,0:T(8,128)(2,1)}), bf16[64,2,128,128]{3,2,1,0:T(8,128)(2,1)}, u32[]{:S(2)}, u32[]{:S(2)}) %all-to-all-start.1) | async-done | bytes 4194336 | tf_op jit(solution)/shard_map/all_to_all | solution.py:140
  153.8 0.0 copy-done.1
  153.8 0.0 copy-done.2
  153.8 0.0 copy-done.3
  153.8 19.0 %shard_map.73 = bf16[128,128,128]{2,1,0:T(8,128)(2,1)S(1)} custom-call(s32[16]{0:T(128)S(1)} %multiply_add_fusion.slot_of_ref, s32[128]{0:T(128)S(1)} %get-tuple-element.8.slot_tile_ref, bf16[128,128,128]{2,1,0:T(8,128)(2,1)} %bitcast.6.arrived_ref, bf16[16,128,128]{2,1,0:T(8,128)(2,1)S(1)} %copy-done.1, f32[128,1]{1,0:T(8,128)S(1)} %copy.13.degree_ref, ...), custom_call_target="tpu_custom_call" | custom-call | tf_op jit(solution)/shard_map/pallas_call | solution.py:88
  172.8 0.0 copy-start
  172.8 2.0 copy-done
  174.7 24.7 %all-to-all-start.2 = ((bf16[64,2,128,128]{3,2,1,0:T(8,128)(2,1)}), bf16[64,2,128,128]{3,2,1,0:T(8,128)(2,1)}, u32[]{:S(2)}, u32[]{:S(2)}) async-start(bf16[64,2,128,128]{3,2,1,0:T(8,128)(2,1)} %bitcast.20), calls=%async_computation.2 | async-start | bytes 8388608 | tf_op jit(solution)/shard_map/all_to_all | solution.py:163
  199.4 0.0 copy-start.4
  199.4 0.1 eq.55
  199.6 142.8 %all-to-all-done.2 = bf16[64,2,128,128]{3,2,1,0:T(8,128)(2,1)} async-done(((bf16[64,2,128,128]{3,2,1,0:T(8,128)(2,1)}), bf16[64,2,128,128]{3,2,1,0:T(8,128)(2,1)}, u32[]{:S(2)}, u32[]{:S(2)}) %all-to-all-start.2) | async-done | bytes 4194336 | tf_op jit(solution)/shard_map/all_to_all | solution.py:163
  342.4 4.5 %fusion = f32[16,16384]{1,0:T(8,128)S(1)} fusion(bf16[16,8,128,128]{3,2,1,0:T(8,128)(2,1)} %bitcast.10, s32[128]{0:T(128)S(1)} %eq.55), kind=kOutput, calls=%fused_computation.1 | convolution fusion | flops 67110912 | bytes 5243392 | tf_op jit(solution)/shard_map/dot_general | solution.py:170
  346.9 0.2 reshape.59
  347.0 0.0 copy-done.4
  347.0 0.9 add_convert_fusion
  (3 shorter events, 0.0 us)
Async XLA Ops:
  29.2 11.0 %copy-start.5 = (s32[16,1]{0,1:T(1,128)S(1)}, s32[16,1]{0,1:T(1,128)}, u32[]{:S(2)}) copy-start(s32[16,1]{0,1:T(1,128)} %param.9) | copy-start | bytes 196
  29.2 124.6 %copy-start.1 = (bf16[16,128,128]{2,1,0:T(8,128)(2,1)S(1)}, bf16[16,128,128]{2,1,0:T(8,128)(2,1)}, u32[]{:S(2)}) copy-start(bf16[16,128,128]{2,1,0:T(8,128)(2,1)} %tiles_ref.1) | copy-start | bytes 1572868
  29.2 124.6 %copy-start.2 = (bf16[128,512]{1,0:T(8,128)(2,1)S(1)}, bf16[128,512]{1,0:T(8,128)(2,1)}, u32[]{:S(2)}) copy-start(bf16[128,512]{1,0:T(8,128)(2,1)} %w_in_ref.1) | copy-start | bytes 393220
  29.2 124.6 %copy-start.3 = (bf16[512,128]{1,0:T(8,128)(2,1)S(1)}, bf16[512,128]{1,0:T(8,128)(2,1)}, u32[]{:S(2)}) copy-start(bf16[512,128]{1,0:T(8,128)(2,1)} %w_out_ref.1) | copy-start | bytes 393220
  29.2 124.6 %all-to-all-start.1 = ((bf16[64,2,128,128]{3,2,1,0:T(8,128)(2,1)}), bf16[64,2,128,128]{3,2,1,0:T(8,128)(2,1)}, u32[]{:S(2)}, u32[]{:S(2)}) async-start(bf16[64,2,128,128]{3,2,1,0:T(8,128)(2,1)} %bitcast.22), calls=%async_computation.1 | async-start | bytes 8388608 | tf_op jit(solution)/shard_map/all_to_all | solution.py:140
  172.8 2.0 copy-start
  174.7 167.6 %all-to-all-start.2 = ((bf16[64,2,128,128]{3,2,1,0:T(8,128)(2,1)}), bf16[64,2,128,128]{3,2,1,0:T(8,128)(2,1)}, u32[]{:S(2)}, u32[]{:S(2)}) async-start(bf16[64,2,128,128]{3,2,1,0:T(8,128)(2,1)} %bitcast.20), calls=%async_computation.2 | async-start | bytes 8388608 | tf_op jit(solution)/shard_map/all_to_all | solution.py:163
  199.4 147.6 %copy-start.4 = (bf16[2048,128]{1,0:T(8,128)(2,1)S(1)}, bf16[2048,128]{1,0:T(8,128)(2,1)}, u32[]{:S(2)}) copy-start(bf16[2048,128]{1,0:T(8,128)(2,1)} %param.7) | copy-start | bytes 1572868

commit v5 on v4

--- a/solution.py
+++ b/solution.py
@@ -104,6 +104,91 @@
     )(slot_of, slot_tile, arrived, tiles, degree, w_in, w_out)
 
 
+def _pick_kernel(wanted_ref, rows_ref, out_ref, sems):
+    last = rows_ref.shape[0] - 1
+
+    def copy(slot):
+        block = jnp.minimum(wanted_ref[slot], last)
+        return pltpu.make_async_copy(rows_ref.at[block], out_ref.at[slot], sems.at[slot])
+
+    def start(slot, carry):
+        @pl.when(wanted_ref[slot] >= 0)
+        def _():
+            copy(slot).start()
+
+        return carry
+
+    def finish(slot, carry):
+        @pl.when(wanted_ref[slot] >= 0)
+        def _():
+            copy(slot).wait()
+
+        return carry
+
+    lax.fori_loop(0, out_ref.shape[0], start, 0)
+    lax.fori_loop(0, out_ref.shape[0], finish, 0)
+
+
+def pick_rows(wanted, blocks):
+    slots = wanted.shape[0]
+    _, rows, channels = blocks.shape
+    return pl.pallas_call(
+        _pick_kernel,
+        out_shape=jax.ShapeDtypeStruct((slots, rows, channels), blocks.dtype),
+        in_specs=[pl.BlockSpec(memory_space=pltpu.SMEM), pl.BlockSpec(memory_space=pltpu.VMEM)],
+        out_specs=pl.BlockSpec(memory_space=pl.ANY),
+        scratch_shapes=[pltpu.SemaphoreType.DMA((slots,))],
+    )(wanted, blocks)
+
+
+def _land_kernel(wanted_ref, returned_ref, rows_ref, out_ref, buf, acc, sems):
+    last = rows_ref.shape[0] - 1
+
+    def copy(slot):
+        return pltpu.make_async_copy(returned_ref.at[slot], buf.at[slot], sems.at[slot])
+
+    def start(slot, carry):
+        @pl.when(wanted_ref[slot] >= 0)
+        def _():
+            copy(slot).start()
+
+        return carry
+
+    lax.fori_loop(0, buf.shape[0], start, 0)
+    acc[...] = rows_ref[...].astype(jnp.float32)
+
+    def add(slot, carry):
+        @pl.when(wanted_ref[slot] >= 0)
+        def _():
+            copy(slot).wait()
+            block = jnp.minimum(wanted_ref[slot], last)
+            acc[block] = acc[block] + buf[slot].astype(jnp.float32)
+
+        return carry
+
+    lax.fori_loop(0, buf.shape[0], add, 0)
+    out_ref[...] = acc[...].astype(out_ref.dtype)
+
+
+def land_terms(wanted, returned, blocks):
+    slots, rows, channels = returned.shape
+    return pl.pallas_call(
+        _land_kernel,
+        out_shape=jax.ShapeDtypeStruct(blocks.shape, blocks.dtype),
+        in_specs=[
+            pl.BlockSpec(memory_space=pltpu.SMEM),
+            pl.BlockSpec(memory_space=pl.ANY),
+            pl.BlockSpec(memory_space=pltpu.VMEM),
+        ],
+        out_specs=pl.BlockSpec(memory_space=pltpu.VMEM),
+        scratch_shapes=[
+            pltpu.VMEM((slots, rows, channels), returned.dtype),
+            pltpu.VMEM(blocks.shape, jnp.float32),
+            pltpu.SemaphoreType.DMA((slots,)),
+        ],
+    )(wanted, returned, blocks)
+
+
 def edge_network(summed, degrees, w_in, w_out):
     edge_in = (summed / degrees.astype(jnp.float32)[:, None]).astype(jnp.bfloat16)
     pre_act = jnp.dot(edge_in, w_in, preferred_element_type=jnp.float32)
@@ -132,11 +217,9 @@
     wanted = lax.all_to_all(
         wanted_out.reshape(owners, capacity), "wide", split_axis=0, concat_axis=0, tiled=True
     ).reshape(slot_count)
-    block_ids = jnp.arange(node_block_count, dtype=jnp.int32)
-    selector = (wanted[None, :] == block_ids[:, None]).astype(jnp.bfloat16)
     current = node_rows
     node_blocks = current.reshape(node_block_count, block_size, channels)
-    picked = node_blocks[jnp.maximum(wanted, 0)]
+    picked = pick_rows(wanted, node_blocks)
     arrived = lax.all_to_all(
         picked.reshape(owners, capacity, block_size, channels),
         "wide",
@@ -167,14 +250,9 @@
         concat_axis=0,
         tiled=True,
     )
-    gathered = jnp.dot(
-        selector,
-        returned.reshape(slot_count, block_size * channels),
-        preferred_element_type=jnp.float32,
-    )
-    current = (
-        current.astype(jnp.float32) + gathered.reshape(node_block_count * block_size, channels)
-    ).astype(jnp.bfloat16)
+    current = land_terms(
+        wanted, returned.reshape(slot_count, block_size, channels), node_blocks
+    ).reshape(node_block_count * block_size, channels)
     return current
 
 

time: 348 us -> 325 us (0.934)
  the two profiles are of different devices: /device:TPU:212 before, /device:TPU:88 now
where the time goes in v5:
time: 325 us; the launch traced here: 324 us
  blocking collectives  157 us (48%)
  waiting for transfers between devices  121 us (37%)
  Pallas kernels  31.8 us (10%)
  starting transfers between devices  9.28 us (3%)
  other arithmetic  3.82 us (1%)
    all_to_all x1, blocking collectives, body(): lax.all_to_all(outgoing.reshape(owners, capacity, block_size, channels),...  134 us
    all_to_all x1, waiting for transfers between devices, body(): lax.all_to_all(picked.reshape(owners, capacity, block_size, channels), 'w...  121 us
    all_to_all x1, blocking collectives, body(): lax.all_to_all(wanted_out.reshape(owners, capacity), 'wide', split_axis=0...  23.7 us
    pallas_call x1, Pallas kernels, round_kernel(): pl.pallas_call(functools.partial(_round_kernel, groups, per_block), out_s...  20.8 us
    all_to_all x1, starting transfers between devices, body(): lax.all_to_all(picked.reshape(owners, capacity, block_size, channels), 'w...  9.28 us
  transfers between devices with their start and end apart: 1, of which 1 were waited for; matrix products, arithmetic and copies ran while one was open for 0% of the time, Pallas kernels for 0%

profile of v5, /device:TPU:88, one launch (start us, length us, event | category | flops | bytes accessed | tf_op | source)
XLA Modules:
  0.0 324.2 jit_solution(7177001911325074680)
XLA Ops:
  0.0 0.9 convert_reduce_fusion
  0.9 0.7 fusion.1
  1.6 0.7 broadcast_add_fusion.1
  2.2 0.1 select_reduce_fusion
  2.3 0.1 sub.7
  2.5 23.7 %all_to_all.16 = s32[64,1,2]{2,1,0:T(1,128)S(1)} all-to-all(s32[64,1,2]{2,1,0:T(1,128)S(1)} %bitcast.22), channel_id=1, replica_groups=mesh['wide'=64,'narrow'=8] {'wide'}, dimensions={0} | all-to-all | bytes 1024 | tf_op jit(solution)/shard_map/all_to_all | solution.py:217
  26.2 0.5 broadcast.35
  26.7 0.7 reduce.3
  27.4 0.6 reshape.42.wanted_ref
  28.0 5.0 %shard_map.73 = bf16[128,128,128]{2,1,0:T(8,128)(2,1)} custom-call(s32[128]{0:T(128)} %reshape.42.wanted_ref, bf16[16,128,128]{2,1,0:T(8,128)(2,1)} %bitcast.20), custom_call_target="tpu_custom_call" | custom-call | tf_op jit(solution)/shard_map/pallas_call | solution.py:135
  33.1 0.0 copy-start.3
  33.1 0.0 copy-start
  33.1 0.0 copy-start.1
  33.1 0.0 copy-start.2
  33.1 9.3 %all-to-all-start.1 = ((bf16[64,2,128,128]{3,2,1,0:T(8,128)(2,1)}), bf16[64,2,128,128]{3,2,1,0:T(8,128)(2,1)}, u32[]{:S(2)}, u32[]{:S(2)}) async-start(bf16[64,2,128,128]{3,2,1,0:T(8,128)(2,1)} %bitcast.18), calls=%async_computation.1 | async-start | bytes 8388608 | tf_op jit(solution)/shard_map/all_to_all | solution.py:223
  42.4 0.8 convert_bitcast_fusion
  43.2 0.1 copy.13.degree_ref
  43.3 0.0 copy-done.3
  43.3 120.6 %all-to-all-done.1 = bf16[64,2,128,128]{3,2,1,0:T(8,128)(2,1)} async-done(((bf16[64,2,128,128]{3,2,1,0:T(8,128)(2,1)}), bf16[64,2,128,128]{3,2,1,0:T(8,128)(2,1)}, u32[]{:S(2)}, u32[]{:S(2)}) %all-to-all-start.1) | async-done | bytes 4194336 | tf_op jit(solution)/shard_map/all_to_all | solution.py:223
  163.9 0.0 copy-done
  163.9 0.0 copy-done.1
  163.9 0.0 copy-done.2
  163.9 20.8 %shard_map.74 = bf16[128,128,128]{2,1,0:T(8,128)(2,1)S(1)} custom-call(s32[16]{0:T(128)S(1)} %multiply_add_fusion.slot_of_ref, s32[128]{0:T(128)S(1)} %get-tuple-element.5.slot_tile_ref, bf16[128,128,128]{2,1,0:T(8,128)(2,1)} %bitcast.6.arrived_ref, bf16[16,128,128]{2,1,0:T(8,128)(2,1)S(1)} %copy-done, f32[128,1]{1,0:T(8,128)S(1)} %copy.13.degree_ref, ...), custom_call_target="tpu_custom_call" | custom-call | tf_op jit(solution)/shard_map/pallas_call | solution.py:88
  184.7 133.5 %all_to_all.17 = bf16[64,2,128,128]{3,2,1,0:T(8,128)(2,1)} all-to-all(bf16[64,2,128,128]{3,2,1,0:T(8,128)(2,1)S(1)} %bitcast.17), channel_id=1, replica_groups=mesh['wide'=64,'narrow'=8] {'wide'}, dimensions={0} | all-to-all | bytes 8388608 | tf_op jit(solution)/shard_map/all_to_all | solution.py:246
  318.2 6.0 %shard_map.75 = bf16[16,128,128]{2,1,0:T(8,128)(2,1)} custom-call(s32[128]{0:T(128)} %reshape.42.wanted_ref, bf16[128,128,128]{2,1,0:T(8,128)(2,1)} %bitcast.19, bf16[16,128,128]{2,1,0:T(8,128)(2,1)} %bitcast.21), custom_call_target="tpu_custom_call" | custom-call | tf_op jit(solution)/shard_map/pallas_call | solution.py:175
  (2 shorter events, 0.0 us)
Async XLA Ops:
  33.1 10.2 %copy-start.3 = (s32[16,1]{0,1:T(1,128)S(1)}, s32[16,1]{0,1:T(1,128)}, u32[]{:S(2)}) copy-start(s32[16,1]{0,1:T(1,128)} %param.9) | copy-start | bytes 196
  33.1 130.8 %copy-start = (bf16[16,128,128]{2,1,0:T(8,128)(2,1)S(1)}, bf16[16,128,128]{2,1,0:T(8,128)(2,1)}, u32[]{:S(2)}) copy-start(bf16[16,128,128]{2,1,0:T(8,128)(2,1)} %tiles_ref.1) | copy-start | bytes 1572868
  33.1 130.8 %copy-start.1 = (bf16[128,512]{1,0:T(8,128)(2,1)S(1)}, bf16[128,512]{1,0:T(8,128)(2,1)}, u32[]{:S(2)}) copy-start(bf16[128,512]{1,0:T(8,128)(2,1)} %w_in_ref.1) | copy-start | bytes 393220
  33.1 130.8 %copy-start.2 = (bf16[512,128]{1,0:T(8,128)(2,1)S(1)}, bf16[512,128]{1,0:T(8,128)(2,1)}, u32[]{:S(2)}) copy-start(bf16[512,128]{1,0:T(8,128)(2,1)} %w_out_ref.1) | copy-start | bytes 393220
  33.1 130.8 %all-to-all-start.1 = ((bf16[64,2,128,128]{3,2,1,0:T(8,128)(2,1)}), bf16[64,2,128,128]{3,2,1,0:T(8,128)(2,1)}, u32[]{:S(2)}, u32[]{:S(2)}) async-start(bf16[64,2,128,128]{3,2,1,0:T(8,128)(2,1)} %bitcast.18), calls=%async_computation.1 | async-start | bytes 8388608 | tf_op jit(solution)/shard_map/all_to_all | solution.py:223

commit v6 on v5

--- a/solution.py
+++ b/solution.py
@@ -214,11 +214,20 @@
     slot_ids = jnp.arange(slot_count, dtype=jnp.int32)
     matches = slot_of[:, None] == slot_ids[None, :]
     wanted_out = jnp.sum(jnp.where(matches, tile_block[:, None] + 1, 0), axis=0) - 1
+    groups = lax.axis_size("narrow")
+    me = lax.axis_index("narrow")
+    own_rows = edge_row_count // groups
+    own_degree = lax.dynamic_slice_in_dim(edge_degree, me * own_rows, own_rows)
+    tile_of_slot = jnp.sum(jnp.where(matches, positions[:, None], 0), axis=0)
     wanted = lax.all_to_all(
         wanted_out.reshape(owners, capacity), "wide", split_axis=0, concat_axis=0, tiled=True
     ).reshape(slot_count)
     current = node_rows
     node_blocks = current.reshape(node_block_count, block_size, channels)
+    degree_column = jnp.broadcast_to(own_degree.astype(jnp.float32)[:, None], (own_rows, channels))
+    wanted, slot_of, tile_of_slot, degree_column = lax.optimization_barrier(
+        (wanted, slot_of, tile_of_slot, degree_column)
+    )
     picked = pick_rows(wanted, node_blocks)
     arrived = lax.all_to_all(
         picked.reshape(owners, capacity, block_size, channels),
@@ -227,17 +236,12 @@
         concat_axis=0,
         tiled=True,
     )
-    groups = lax.axis_size("narrow")
-    me = lax.axis_index("narrow")
-    own_rows = edge_row_count // groups
-    own_degree = lax.dynamic_slice_in_dim(edge_degree, me * own_rows, own_rows)
-    tile_of_slot = jnp.sum(jnp.where(matches, positions[:, None], 0), axis=0)
     outgoing = round_kernel(
         slot_of,
         tile_of_slot,
         arrived.reshape(slot_count, block_size, channels),
         tile_values,
-        own_degree.astype(jnp.float32)[:, None],
+        degree_column,
         w_in,
         w_out,
         groups,

time: 325 us -> 296 us (0.911)
  the two profiles are of different devices: /device:TPU:88 before, /device:TPU:90 now
where the time goes in v6:
time: 296 us; the launch traced here: 295 us
  blocking collectives  236 us (80%)
  Pallas kernels  30.2 us (10%)
  starting transfers between devices  15.5 us (5%)
  waiting for transfers between devices  6.92 us (2%)
  other arithmetic  4.47 us (2%)
    all_to_all x1, blocking collectives, body(): lax.all_to_all(outgoing.reshape(owners, capacity, block_size, channels),...  125 us
    all_to_all x1, blocking collectives, body(): lax.all_to_all(picked.reshape(owners, capacity, block_size, channels), 'w...  111 us
    pallas_call x1, Pallas kernels, round_kernel(): pl.pallas_call(functools.partial(_round_kernel, groups, per_block), out_s...  19.2 us
    all_to_all x1, starting transfers between devices, body(): lax.all_to_all(wanted_out.reshape(owners, capacity), 'wide', split_axis=0...  15.5 us
    all_to_all x1, waiting for transfers between devices, body(): lax.all_to_all(wanted_out.reshape(owners, capacity), 'wide', split_axis=0...  6.92 us
    pallas_call x1, Pallas kernels, land_terms(): pl.pallas_call(_land_kernel, out_shape=jax.ShapeDtypeStruct(blocks.shape,...  5.94 us
  transfers between devices with their start and end apart: 1, of which 1 were waited for; matrix products, arithmetic and copies ran while one was open for 0% of the time, Pallas kernels for 0%

profile of v6, /device:TPU:90, one launch (start us, length us, event | category | flops | bytes accessed | tf_op | source)
XLA Modules:
  0.0 295.3 jit_solution(13944372859246368591)
XLA Ops:
  0.0 0.9 convert_reduce_fusion
  0.9 0.7 fusion.1
  1.6 0.7 broadcast_add_fusion.1
  2.2 0.1 select_reduce_fusion
  2.3 0.8 sub.7
  3.1 15.5 %all-to-all-start = ((s32[64,1,2]{2,1,0:T(1,128)}), s32[64,1,2]{2,1,0:T(1,128)S(1)}, u32[]{:S(2)}, u32[]{:S(2)}) async-start(s32[64,1,2]{2,1,0:T(1,128)} %bitcast.3), calls=%async_computation | async-start | bytes 65536 | tf_op jit(solution)/shard_map/all_to_all | solution.py:222
  18.6 0.7 multiply_add_fusion.slot_of_ref
  19.3 0.8 dynamic-slice_convert_fusion
  20.0 6.9 %all-to-all-done = s32[64,1,2]{2,1,0:T(1,128)S(1)} async-done(((s32[64,1,2]{2,1,0:T(1,128)}), s32[64,1,2]{2,1,0:T(1,128)S(1)}, u32[]{:S(2)}, u32[]{:S(2)}) %all-to-all-start) | async-done | bytes 544 | tf_op jit(solution)/shard_map/all_to_all | solution.py:222
  26.9 0.5 broadcast.36
  27.4 0.7 reduce.3
  28.2 0.6 reshape.43.wanted_ref
  28.8 0.1 broadcast_in_dim.33.degree_ref
  28.9 5.0 %shard_map.73 = bf16[128,128,128]{2,1,0:T(8,128)(2,1)} custom-call(s32[128]{0:T(128)} %reshape.43.wanted_ref, bf16[16,128,128]{2,1,0:T(8,128)(2,1)} %bitcast.19), custom_call_target="tpu_custom_call" | custom-call | tf_op jit(solution)/shard_map/pallas_call | solution.py:135
  33.9 0.0 copy-start
  33.9 0.0 copy-start.1
  33.9 0.0 copy-start.2
  34.0 110.9 %all_to_all.16 = bf16[64,2,128,128]{3,2,1,0:T(8,128)(2,1)} all-to-all(bf16[64,2,128,128]{3,2,1,0:T(8,128)(2,1)} %bitcast.18), channel_id=1, replica_groups=mesh['wide'=64,'narrow'=8] {'wide'}, dimensions={0} | all-to-all | bytes 8388608 | tf_op jit(solution)/shard_map/all_to_all | solution.py:232
  144.9 0.0 copy-done
  144.9 0.0 copy-done.1
  144.9 0.0 copy-done.2
  144.9 19.2 %shard_map.74 = bf16[128,128,128]{2,1,0:T(8,128)(2,1)S(1)} custom-call(s32[16]{0:T(128)S(1)} %multiply_add_fusion.slot_of_ref, s32[128]{0:T(128)S(1)} %get-tuple-element.11.slot_tile_ref, bf16[128,128,128]{2,1,0:T(8,128)(2,1)} %bitcast.16, bf16[16,128,128]{2,1,0:T(8,128)(2,1)S(1)} %copy-done, f32[128,128]{1,0:T(8,128)S(1)} %broadcast_in_dim.33.degree_ref, ...), custom_call_target="tpu_custom_call" | custom-call | tf_op jit(solution)/shard_map/pallas_call | solution.py:88
  164.1 125.3 %all_to_all.17 = bf16[64,2,128,128]{3,2,1,0:T(8,128)(2,1)} all-to-all(bf16[64,2,128,128]{3,2,1,0:T(8,128)(2,1)S(1)} %bitcast.15), channel_id=1, replica_groups=mesh['wide'=64,'narrow'=8] {'wide'}, dimensions={0} | all-to-all | bytes 8388608 | tf_op jit(solution)/shard_map/all_to_all | solution.py:250
  289.4 5.9 %shard_map.75 = bf16[16,128,128]{2,1,0:T(8,128)(2,1)} custom-call(s32[128]{0:T(128)} %reshape.43.wanted_ref, bf16[128,128,128]{2,1,0:T(8,128)(2,1)} %bitcast.17, bf16[16,128,128]{2,1,0:T(8,128)(2,1)} %bitcast.20), custom_call_target="tpu_custom_call" | custom-call | tf_op jit(solution)/shard_map/pallas_call | solution.py:175
  (1 shorter events, 0.0 us)
Async XLA Ops:
  3.1 23.8 %all-to-all-start = ((s32[64,1,2]{2,1,0:T(1,128)}), s32[64,1,2]{2,1,0:T(1,128)S(1)}, u32[]{:S(2)}, u32[]{:S(2)}) async-start(s32[64,1,2]{2,1,0:T(1,128)} %bitcast.3), calls=%async_computation | async-start | bytes 65536 | tf_op jit(solution)/shard_map/all_to_all | solution.py:222
  33.9 110.9 %copy-start = (bf16[16,128,128]{2,1,0:T(8,128)(2,1)S(1)}, bf16[16,128,128]{2,1,0:T(8,128)(2,1)}, u32[]{:S(2)}) copy-start(bf16[16,128,128]{2,1,0:T(8,128)(2,1)} %tiles_ref.1) | copy-start | bytes 1572868
  33.9 110.9 %copy-start.1 = (bf16[128,512]{1,0:T(8,128)(2,1)S(1)}, bf16[128,512]{1,0:T(8,128)(2,1)}, u32[]{:S(2)}) copy-start(bf16[128,512]{1,0:T(8,128)(2,1)} %w_in_ref.1) | copy-start | bytes 393220
  33.9 110.9 %copy-start.2 = (bf16[512,128]{1,0:T(8,128)(2,1)S(1)}, bf16[512,128]{1,0:T(8,128)(2,1)}, u32[]{:S(2)}) copy-start(bf16[512,128]{1,0:T(8,128)(2,1)} %w_out_ref.1) | copy-start | bytes 393220

commit v7 on v6

--- a/solution.py
+++ b/solution.py
@@ -11,7 +11,8 @@
 
 def _round_kernel(groups, per_block, slot_of_ref, slot_tile_ref, arrived_ref, tiles_ref,
                   degree_ref, w_in_ref, w_out_ref, out_ref,
-                  parts, inbox, stage, edge_out, terms, send_a, recv_a, send_b, recv_b):
+                  parts, inbox, stage, edge_out, terms, send_a, recv_a, send_b, recv_b,
+                  placed, flush_sem):
     me = lax.axis_index("narrow")
     col = lax.axis_index("wide")
     tile_count = tiles_ref.shape[0]
@@ -75,10 +76,13 @@
         terms[t] = term.astype(jnp.bfloat16)
 
     def place(slot, carry):
-        out_ref[slot] = terms[slot_tile_ref[slot]]
+        placed[slot] = terms[slot_tile_ref[slot]]
         return carry
 
     lax.fori_loop(0, out_ref.shape[0], place, 0)
+    flush = pltpu.make_async_copy(placed, out_ref, flush_sem)
+    flush.start()
+    flush.wait()
 
 
 def round_kernel(slot_of, slot_tile, arrived, tiles, degree, w_in, w_out, groups, per_block):
@@ -89,7 +93,7 @@
         functools.partial(_round_kernel, groups, per_block),
         out_shape=jax.ShapeDtypeStruct((slots, rows, channels), jnp.bfloat16),
         in_specs=[smem, smem] + [vmem] * 5,
-        out_specs=vmem,
+        out_specs=pl.BlockSpec(memory_space=pltpu.HBM),
         scratch_shapes=[
             pltpu.VMEM((groups, rows, channels), jnp.float32),
             pltpu.VMEM((groups, rows, channels), jnp.float32),
@@ -98,9 +102,11 @@
             pltpu.VMEM(tiles.shape, jnp.bfloat16),
             pltpu.SemaphoreType.DMA((groups,)), pltpu.SemaphoreType.DMA((groups,)),
             pltpu.SemaphoreType.DMA((groups,)), pltpu.SemaphoreType.DMA((groups,)),
+            pltpu.VMEM((slots, rows, channels), jnp.bfloat16),
+            pltpu.SemaphoreType.DMA,
         ],
         compiler_params=pltpu.CompilerParams(
-            collective_id=0, has_side_effects=True, vmem_limit_bytes=48 * 1024 * 1024),
+            collective_id=0, has_side_effects=True, vmem_limit_bytes=67043328),
     )(slot_of, slot_tile, arrived, tiles, degree, w_in, w_out)
 
 

time: 296 us -> 301 us (1.017)
  the two profiles are of different devices: /device:TPU:90 before, /device:TPU:88 now
where the time goes in v7:
time: 301 us
  blocking collectives  237 us (79%)
  Pallas kernels  33.9 us (11%)
  starting transfers between devices  15.5 us (5%)
  waiting for transfers between devices  6.4 us (2%)
  other arithmetic  5.5 us (2%)
    all_to_all x1, blocking collectives, body(): lax.all_to_all(outgoing.reshape(owners, capacity, block_size, channels),...  126 us
    all_to_all x1, blocking collectives, body(): lax.all_to_all(picked.reshape(owners, capacity, block_size, channels), 'w...  111 us
    pallas_call x1, Pallas kernels, round_kernel(): pl.pallas_call(functools.partial(_round_kernel, groups, per_block), out_s...  22.9 us
    all_to_all x1, starting transfers between devices, body(): lax.all_to_all(wanted_out.reshape(owners, capacity), 'wide', split_axis=0...  15.5 us
    all_to_all x1, waiting for transfers between devices, body(): lax.all_to_all(wanted_out.reshape(owners, capacity), 'wide', split_axis=0...  6.4 us
  transfers between devices with their start and end apart: 1, of which 1 were waited for; matrix products, arithmetic and copies ran while one was open for 1% of the time, Pallas kernels for 0%

profile of v7, /device:TPU:88, one launch (start us, length us, event | category | flops | bytes accessed | tf_op | source)
XLA Modules:
  0.0 300.5 jit_solution(11012962304187727565)
XLA Ops:
  0.0 0.9 convert_reduce_fusion
  0.9 0.7 fusion.1
  1.6 0.7 broadcast_add_fusion.1
  2.2 0.6 select_reduce_fusion
  2.8 0.8 sub.7
  3.6 15.5 %all-to-all-start = ((s32[64,1,2]{2,1,0:T(1,128)}), s32[64,1,2]{2,1,0:T(1,128)S(1)}, u32[]{:S(2)}, u32[]{:S(2)}) async-start(s32[64,1,2]{2,1,0:T(1,128)} %bitcast.3), calls=%async_computation | async-start | bytes 65536 | tf_op jit(solution)/shard_map/all_to_all | solution.py:228
  19.1 1.2 multiply_add_fusion.slot_of_ref
  20.3 0.8 dynamic-slice_convert_fusion
  21.0 6.4 %all-to-all-done = s32[64,1,2]{2,1,0:T(1,128)S(1)} async-done(((s32[64,1,2]{2,1,0:T(1,128)}), s32[64,1,2]{2,1,0:T(1,128)S(1)}, u32[]{:S(2)}, u32[]{:S(2)}) %all-to-all-start) | async-done | bytes 544 | tf_op jit(solution)/shard_map/all_to_all | solution.py:228
  27.5 0.5 broadcast.36
  28.0 0.7 reduce.3
  28.7 0.6 reshape.43.wanted_ref
  29.3 0.7 broadcast_in_dim.33.degree_ref
  30.0 5.0 %shard_map.73 = bf16[128,128,128]{2,1,0:T(8,128)(2,1)} custom-call(s32[128]{0:T(128)} %reshape.43.wanted_ref, bf16[16,128,128]{2,1,0:T(8,128)(2,1)} %bitcast.19), custom_call_target="tpu_custom_call" | custom-call | tf_op jit(solution)/shard_map/pallas_call | solution.py:141
  35.1 110.8 %all_to_all.16 = bf16[64,2,128,128]{3,2,1,0:T(8,128)(2,1)} all-to-all(bf16[64,2,128,128]{3,2,1,0:T(8,128)(2,1)} %bitcast.18), channel_id=1, replica_groups=mesh['wide'=64,'narrow'=8] {'wide'}, dimensions={0} | all-to-all | bytes 8388608 | tf_op jit(solution)/shard_map/all_to_all | solution.py:238
  145.8 22.9 %shard_map.74 = bf16[128,128,128]{2,1,0:T(8,128)(2,1)} custom-call(s32[16]{0:T(128)} %multiply_add_fusion.slot_of_ref, s32[128]{0:T(128)} %get-tuple-element.11.slot_tile_ref, bf16[128,128,128]{2,1,0:T(8,128)(2,1)} %bitcast.15, bf16[16,128,128]{2,1,0:T(8,128)(2,1)} %tiles_ref.1, f32[128,128]{1,0:T(8,128)} %broadcast_in_dim.33.degree_ref, ...), custom_call_target="tpu_custom_call" | custom-call | tf_op jit(solution)/shard_map/pallas_call | solution.py:92
  168.7 125.8 %all_to_all.17 = bf16[64,2,128,128]{3,2,1,0:T(8,128)(2,1)} all-to-all(bf16[64,2,128,128]{3,2,1,0:T(8,128)(2,1)} %bitcast.16), channel_id=1, replica_groups=mesh['wide'=64,'narrow'=8] {'wide'}, dimensions={0} | all-to-all | bytes 8388608 | tf_op jit(solution)/shard_map/all_to_all | solution.py:256
  294.6 6.0 %shard_map.75 = bf16[16,128,128]{2,1,0:T(8,128)(2,1)} custom-call(s32[128]{0:T(128)} %reshape.43.wanted_ref, bf16[128,128,128]{2,1,0:T(8,128)(2,1)} %bitcast.17, bf16[16,128,128]{2,1,0:T(8,128)(2,1)} %bitcast.20), custom_call_target="tpu_custom_call" | custom-call | tf_op jit(solution)/shard_map/pallas_call | solution.py:181
  (1 shorter events, 0.0 us)
Async XLA Ops:
  3.6 23.8 %all-to-all-start = ((s32[64,1,2]{2,1,0:T(1,128)}), s32[64,1,2]{2,1,0:T(1,128)S(1)}, u32[]{:S(2)}, u32[]{:S(2)}) async-start(s32[64,1,2]{2,1,0:T(1,128)} %bitcast.3), calls=%async_computation | async-start | bytes 65536 | tf_op jit(solution)/shard_map/all_to_all | solution.py:228

commit v8 on v6

--- a/solution.py
+++ b/solution.py
@@ -104,89 +104,76 @@
     )(slot_of, slot_tile, arrived, tiles, degree, w_in, w_out)
 
 
-def _pick_kernel(wanted_ref, rows_ref, out_ref, sems):
+def _pick_kernel(count_ref, order_ref, wanted_ref, rows_ref, out_ref, sems):
     last = rows_ref.shape[0] - 1
 
-    def copy(slot):
-        block = jnp.minimum(wanted_ref[slot], last)
-        return pltpu.make_async_copy(rows_ref.at[block], out_ref.at[slot], sems.at[slot])
-
-    def start(slot, carry):
-        @pl.when(wanted_ref[slot] >= 0)
-        def _():
-            copy(slot).start()
-
-        return carry
-
-    def finish(slot, carry):
-        @pl.when(wanted_ref[slot] >= 0)
-        def _():
-            copy(slot).wait()
-
-        return carry
-
-    lax.fori_loop(0, out_ref.shape[0], start, 0)
-    lax.fori_loop(0, out_ref.shape[0], finish, 0)
-
-
-def pick_rows(wanted, blocks):
+    def copy(i):
+        slot = order_ref[i]
+        block = jnp.clip(wanted_ref[slot], 0, last)
+        return pltpu.make_async_copy(rows_ref.at[block], out_ref.at[slot], sems.at[i])
+
+    def start(i, carry):
+        copy(i).start()
+        return carry
+
+    def finish(i, carry):
+        copy(i).wait()
+        return carry
+
+    lax.fori_loop(0, count_ref[0], start, 0)
+    lax.fori_loop(0, count_ref[0], finish, 0)
+
+
+def pick_rows(count, order, wanted, blocks):
     slots = wanted.shape[0]
     _, rows, channels = blocks.shape
+    smem = pl.BlockSpec(memory_space=pltpu.SMEM)
     return pl.pallas_call(
         _pick_kernel,
         out_shape=jax.ShapeDtypeStruct((slots, rows, channels), blocks.dtype),
-        in_specs=[pl.BlockSpec(memory_space=pltpu.SMEM), pl.BlockSpec(memory_space=pltpu.VMEM)],
+        in_specs=[smem, smem, smem, pl.BlockSpec(memory_space=pltpu.VMEM)],
         out_specs=pl.BlockSpec(memory_space=pl.ANY),
         scratch_shapes=[pltpu.SemaphoreType.DMA((slots,))],
-    )(wanted, blocks)
-
-
-def _land_kernel(wanted_ref, returned_ref, rows_ref, out_ref, buf, acc, sems):
+    )(count, order, wanted, blocks)
+
+
+def _land_kernel(count_ref, order_ref, wanted_ref, returned_ref, rows_ref, out_ref, buf, acc, sems):
     last = rows_ref.shape[0] - 1
 
-    def copy(slot):
-        return pltpu.make_async_copy(returned_ref.at[slot], buf.at[slot], sems.at[slot])
-
-    def start(slot, carry):
-        @pl.when(wanted_ref[slot] >= 0)
-        def _():
-            copy(slot).start()
-
-        return carry
-
-    lax.fori_loop(0, buf.shape[0], start, 0)
+    def copy(i):
+        return pltpu.make_async_copy(returned_ref.at[order_ref[i]], buf.at[i], sems.at[i])
+
+    def start(i, carry):
+        copy(i).start()
+        return carry
+
+    lax.fori_loop(0, count_ref[0], start, 0)
     acc[...] = rows_ref[...].astype(jnp.float32)
 
-    def add(slot, carry):
-        @pl.when(wanted_ref[slot] >= 0)
-        def _():
-            copy(slot).wait()
-            block = jnp.minimum(wanted_ref[slot], last)
-            acc[block] = acc[block] + buf[slot].astype(jnp.float32)
-
-        return carry
-
-    lax.fori_loop(0, buf.shape[0], add, 0)
+    def add(i, carry):
+        copy(i).wait()
+        block = jnp.clip(wanted_ref[order_ref[i]], 0, last)
+        acc[block] = acc[block] + buf[i].astype(jnp.float32)
+        return carry
+
+    lax.fori_loop(0, count_ref[0], add, 0)
     out_ref[...] = acc[...].astype(out_ref.dtype)
 
 
-def land_terms(wanted, returned, blocks):
+def land_terms(count, order, wanted, returned, blocks):
     slots, rows, channels = returned.shape
+    smem = pl.BlockSpec(memory_space=pltpu.SMEM)
     return pl.pallas_call(
         _land_kernel,
         out_shape=jax.ShapeDtypeStruct(blocks.shape, blocks.dtype),
-        in_specs=[
-            pl.BlockSpec(memory_space=pltpu.SMEM),
-            pl.BlockSpec(memory_space=pl.ANY),
-            pl.BlockSpec(memory_space=pltpu.VMEM),
-        ],
+        in_specs=[smem, smem, smem, pl.BlockSpec(memory_space=pl.ANY), pl.BlockSpec(memory_space=pltpu.VMEM)],
         out_specs=pl.BlockSpec(memory_space=pltpu.VMEM),
         scratch_shapes=[
             pltpu.VMEM((slots, rows, channels), returned.dtype),
             pltpu.VMEM(blocks.shape, jnp.float32),
             pltpu.SemaphoreType.DMA((slots,)),
         ],
-    )(wanted, returned, blocks)
+    )(count, order, wanted, returned, blocks)
 
 
 def edge_network(summed, degrees, w_in, w_out):
@@ -228,7 +215,14 @@
     wanted, slot_of, tile_of_slot, degree_column = lax.optimization_barrier(
         (wanted, slot_of, tile_of_slot, degree_column)
     )
-    picked = pick_rows(wanted, node_blocks)
+    filled = wanted >= 0
+    rank = jnp.cumsum(filled.astype(jnp.int32)) - 1
+    count = jnp.sum(filled.astype(jnp.int32)).reshape(1)
+    order = jnp.sum(
+        jnp.where(filled[None, :] & (rank[None, :] == slot_ids[:, None]), slot_ids[None, :], 0),
+        axis=1,
+    )
+    picked = pick_rows(count, order, wanted, node_blocks)
     arrived = lax.all_to_all(
         picked.reshape(owners, capacity, block_size, channels),
         "wide",
@@ -255,7 +249,7 @@
         tiled=True,
     )
     current = land_terms(
-        wanted, returned.reshape(slot_count, block_size, channels), node_blocks
+        count, order, wanted, returned.reshape(slot_count, block_size, channels), node_blocks
     ).reshape(node_block_count * block_size, channels)
     return current
 

time: 296 us -> 296 us (level)
  the two profiles are of different devices: /device:TPU:90 before, /device:TPU:88 now
where the time goes in v8:
time: 296 us; the launch traced here: 295 us
  blocking collectives  235 us (79%)
  Pallas kernels  30.1 us (10%)
  starting transfers between devices  15.5 us (5%)
  waiting for transfers between devices  6.92 us (2%)
  other arithmetic  6.02 us (2%)
    all_to_all x1, blocking collectives, body(): lax.all_to_all(outgoing.reshape(owners, capacity, block_size, channels),...  125 us
    all_to_all x1, blocking collectives, body(): lax.all_to_all(picked.reshape(owners, capacity, block_size, channels), 'w...  110 us
    pallas_call x1, Pallas kernels, round_kernel(): pl.pallas_call(functools.partial(_round_kernel, groups, per_block), out_s...  22 us
    all_to_all x1, starting transfers between devices, body(): lax.all_to_all(wanted_out.reshape(owners, capacity), 'wide', split_axis=0...  15.5 us
    all_to_all x1, waiting for transfers between devices, body(): lax.all_to_all(wanted_out.reshape(owners, capacity), 'wide', split_axis=0...  6.92 us
  transfers between devices with their start and end apart: 1, of which 1 were waited for; matrix products, arithmetic and copies ran while one was open for 0% of the time, Pallas kernels for 0%

profile of v8, /device:TPU:88, one launch (start us, length us, event | category | flops | bytes accessed | tf_op | source)
XLA Modules:
  0.0 295.3 jit_solution(15009416088146583050)
XLA Ops:
  0.0 0.9 convert_reduce_fusion
  0.9 0.7 fusion.2
  1.6 0.7 broadcast_add_fusion.1
  2.2 0.1 select_reduce_fusion.1
  2.3 0.8 sub.11
  3.1 15.5 %all-to-all-start = ((s32[64,1,2]{2,1,0:T(1,128)}), s32[64,1,2]{2,1,0:T(1,128)S(1)}, u32[]{:S(2)}, u32[]{:S(2)}) async-start(s32[64,1,2]{2,1,0:T(1,128)} %bitcast.3), calls=%async_computation | async-start | bytes 65536 | tf_op jit(solution)/shard_map/all_to_all | solution.py:209
  18.6 0.7 multiply_add_fusion.slot_of_ref
  19.3 0.8 dynamic-slice_convert_fusion
  20.0 6.9 %all-to-all-done = s32[64,1,2]{2,1,0:T(1,128)S(1)} async-done(((s32[64,1,2]{2,1,0:T(1,128)}), s32[64,1,2]{2,1,0:T(1,128)S(1)}, u32[]{:S(2)}, u32[]{:S(2)}) %all-to-all-start) | async-done | bytes 544 | tf_op jit(solution)/shard_map/all_to_all | solution.py:209
  26.9 0.5 broadcast.50
  27.4 0.7 reduce.5
  28.2 0.1 reshape.74.wanted_ref
  28.3 0.0 copy-start.3
  28.3 0.1 broadcast_in_dim.49.degree_ref
  28.4 0.6 convert_reduce_fusion.1
  29.0 0.1 copy.13
  29.1 0.2 reduce-window.8
  29.3 0.1 add_reduce_fusion
  29.4 0.7 select_reduce_fusion.order_ref
  30.1 0.0 copy-done.3
  30.1 3.5 %shard_map.73 = bf16[128,128,128]{2,1,0:T(8,128)(2,1)} custom-call(s32[1]{0:T(128)} %bitcast.4.count_ref, s32[128]{0:T(128)} %select_reduce_fusion.order_ref, s32[128]{0:T(128)} %copy-done.3, bf16[16,128,128]{2,1,0:T(8,128)(2,1)} %bitcast.22), custom_call_target="tpu_custom_call" | custom-call | tf_op jit(solution)/shard_map/pallas_call | solution.py:131
  33.6 0.0 copy-start
  33.6 0.0 copy-start.1
  33.6 0.0 copy-start.2
  33.6 109.6 %all_to_all.16 = bf16[64,2,128,128]{3,2,1,0:T(8,128)(2,1)} all-to-all(bf16[64,2,128,128]{3,2,1,0:T(8,128)(2,1)} %bitcast.21), channel_id=1, replica_groups=mesh['wide'=64,'narrow'=8] {'wide'}, dimensions={0} | all-to-all | bytes 8388608 | tf_op jit(solution)/shard_map/all_to_all | solution.py:226
  143.2 0.0 copy-done
  143.2 0.0 copy-done.1
  143.2 0.0 copy-done.2
  143.3 22.0 %shard_map.74 = bf16[128,128,128]{2,1,0:T(8,128)(2,1)S(1)} custom-call(s32[16]{0:T(128)S(1)} %multiply_add_fusion.slot_of_ref, s32[128]{0:T(128)S(1)} %get-tuple-element.11.slot_tile_ref, bf16[128,128,128]{2,1,0:T(8,128)(2,1)} %bitcast.19, bf16[16,128,128]{2,1,0:T(8,128)(2,1)S(1)} %copy-done, f32[128,128]{1,0:T(8,128)S(1)} %broadcast_in_dim.49.degree_ref, ...), custom_call_target="tpu_custom_call" | custom-call | tf_op jit(solution)/shard_map/pallas_call | solution.py:88
  165.3 125.4 %all_to_all.17 = bf16[64,2,128,128]{3,2,1,0:T(8,128)(2,1)} all-to-all(bf16[64,2,128,128]{3,2,1,0:T(8,128)(2,1)S(1)} %bitcast.18), channel_id=1, replica_groups=mesh['wide'=64,'narrow'=8] {'wide'}, dimensions={0} | all-to-all | bytes 8388608 | tf_op jit(solution)/shard_map/all_to_all | solution.py:244
  290.7 4.6 %shard_map.75 = bf16[16,128,128]{2,1,0:T(8,128)(2,1)} custom-call(s32[1]{0:T(128)} %bitcast.4.count_ref, s32[128]{0:T(128)} %select_reduce_fusion.order_ref, s32[128]{0:T(128)} %copy-done.3, bf16[128,128,128]{2,1,0:T(8,128)(2,1)} %bitcast.20, bf16[16,128,128]{2,1,0:T(8,128)(2,1)} %bitcast.23), custom_call_target="tpu_custom_call" | custom-call | tf_op jit(solution)/shard_map/pallas_call | solution.py:166
  (2 shorter events, 0.0 us)
Async XLA Ops:
  3.1 23.8 %all-to-all-start = ((s32[64,1,2]{2,1,0:T(1,128)}), s32[64,1,2]{2,1,0:T(1,128)S(1)}, u32[]{:S(2)}, u32[]{:S(2)}) async-start(s32[64,1,2]{2,1,0:T(1,128)} %bitcast.3), calls=%async_computation | async-start | bytes 65536 | tf_op jit(solution)/shard_map/all_to_all | solution.py:209
  28.3 1.8 copy-start.3
  33.6 109.6 %copy-start = (bf16[16,128,128]{2,1,0:T(8,128)(2,1)S(1)}, bf16[16,128,128]{2,1,0:T(8,128)(2,1)}, u32[]{:S(2)}) copy-start(bf16[16,128,128]{2,1,0:T(8,128)(2,1)} %tiles_ref.1) | copy-start | bytes 1572868
  33.6 109.6 %copy-start.1 = (bf16[128,512]{1,0:T(8,128)(2,1)S(1)}, bf16[128,512]{1,0:T(8,128)(2,1)}, u32[]{:S(2)}) copy-start(bf16[128,512]{1,0:T(8,128)(2,1)} %w_in_ref.1) | copy-start | bytes 393220
  33.6 109.6 %copy-start.2 = (bf16[512,128]{1,0:T(8,128)(2,1)S(1)}, bf16[512,128]{1,0:T(8,128)(2,1)}, u32[]{:S(2)}) copy-start(bf16[512,128]{1,0:T(8,128)(2,1)} %w_out_ref.1) | copy-start | bytes 393220

commit v9 on v8

--- a/solution.py
+++ b/solution.py
@@ -104,13 +104,25 @@
     )(slot_of, slot_tile, arrived, tiles, degree, w_in, w_out)
 
 
-def _pick_kernel(count_ref, order_ref, wanted_ref, rows_ref, out_ref, sems):
+def _pick_kernel(asked_ref, rows_ref, out_ref, order_ref, block_ref, count_ref, sems):
     last = rows_ref.shape[0] - 1
+    capacity = asked_ref.shape[2]
+
+    def scan(slot, filled):
+        block = asked_ref[slot // capacity, 0, slot % capacity]
+
+        @pl.when(block >= 0)
+        def _():
+            order_ref[filled] = slot
+            block_ref[filled] = jnp.minimum(block, last)
+
+        return filled + jnp.where(block >= 0, 1, 0)
+
+    count = lax.fori_loop(0, out_ref.shape[0], scan, 0)
+    count_ref[0] = count
 
     def copy(i):
-        slot = order_ref[i]
-        block = jnp.clip(wanted_ref[slot], 0, last)
-        return pltpu.make_async_copy(rows_ref.at[block], out_ref.at[slot], sems.at[i])
+        return pltpu.make_async_copy(rows_ref.at[block_ref[i]], out_ref.at[order_ref[i]], sems.at[i])
 
     def start(i, carry):
         copy(i).start()
@@ -120,24 +132,30 @@
         copy(i).wait()
         return carry
 
-    lax.fori_loop(0, count_ref[0], start, 0)
-    lax.fori_loop(0, count_ref[0], finish, 0)
-
-
-def pick_rows(count, order, wanted, blocks):
-    slots = wanted.shape[0]
+    lax.fori_loop(0, count, start, 0)
+    lax.fori_loop(0, count, finish, 0)
+
+
+def pick_rows(asked, blocks):
+    owners, _, capacity = asked.shape
+    slots = owners * capacity
     _, rows, channels = blocks.shape
     smem = pl.BlockSpec(memory_space=pltpu.SMEM)
     return pl.pallas_call(
         _pick_kernel,
-        out_shape=jax.ShapeDtypeStruct((slots, rows, channels), blocks.dtype),
-        in_specs=[smem, smem, smem, pl.BlockSpec(memory_space=pltpu.VMEM)],
-        out_specs=pl.BlockSpec(memory_space=pl.ANY),
+        out_shape=(
+            jax.ShapeDtypeStruct((slots, rows, channels), blocks.dtype),
+            jax.ShapeDtypeStruct((slots,), jnp.int32),
+            jax.ShapeDtypeStruct((slots,), jnp.int32),
+            jax.ShapeDtypeStruct((1,), jnp.int32),
+        ),
+        in_specs=[smem, pl.BlockSpec(memory_space=pltpu.VMEM)],
+        out_specs=(pl.BlockSpec(memory_space=pl.ANY), smem, smem, smem),
         scratch_shapes=[pltpu.SemaphoreType.DMA((slots,))],
-    )(count, order, wanted, blocks)
-
-
-def _land_kernel(count_ref, order_ref, wanted_ref, returned_ref, rows_ref, out_ref, buf, acc, sems):
+    )(asked, blocks)
+
+
+def _land_kernel(count_ref, order_ref, block_ref, returned_ref, rows_ref, out_ref, buf, acc, sems):
     last = rows_ref.shape[0] - 1
 
     def copy(i):
@@ -152,7 +170,7 @@
 
     def add(i, carry):
         copy(i).wait()
-        block = jnp.clip(wanted_ref[order_ref[i]], 0, last)
+        block = block_ref[i]
         acc[block] = acc[block] + buf[i].astype(jnp.float32)
         return carry
 
@@ -160,7 +178,7 @@
     out_ref[...] = acc[...].astype(out_ref.dtype)
 
 
-def land_terms(count, order, wanted, returned, blocks):
+def land_terms(count, order, block_list, returned, blocks):
     slots, rows, channels = returned.shape
     smem = pl.BlockSpec(memory_space=pltpu.SMEM)
     return pl.pallas_call(
@@ -173,7 +191,7 @@
             pltpu.VMEM(blocks.shape, jnp.float32),
             pltpu.SemaphoreType.DMA((slots,)),
         ],
-    )(count, order, wanted, returned, blocks)
+    )(count, order, block_list, returned, blocks)
 
 
 def edge_network(summed, degrees, w_in, w_out):
@@ -206,23 +224,16 @@
     own_rows = edge_row_count // groups
     own_degree = lax.dynamic_slice_in_dim(edge_degree, me * own_rows, own_rows)
     tile_of_slot = jnp.sum(jnp.where(matches, positions[:, None], 0), axis=0)
-    wanted = lax.all_to_all(
-        wanted_out.reshape(owners, capacity), "wide", split_axis=0, concat_axis=0, tiled=True
-    ).reshape(slot_count)
+    asked = lax.all_to_all(
+        wanted_out.reshape(owners, 1, capacity), "wide", split_axis=0, concat_axis=0, tiled=True
+    )
     current = node_rows
     node_blocks = current.reshape(node_block_count, block_size, channels)
     degree_column = jnp.broadcast_to(own_degree.astype(jnp.float32)[:, None], (own_rows, channels))
-    wanted, slot_of, tile_of_slot, degree_column = lax.optimization_barrier(
-        (wanted, slot_of, tile_of_slot, degree_column)
-    )
-    filled = wanted >= 0
-    rank = jnp.cumsum(filled.astype(jnp.int32)) - 1
-    count = jnp.sum(filled.astype(jnp.int32)).reshape(1)
-    order = jnp.sum(
-        jnp.where(filled[None, :] & (rank[None, :] == slot_ids[:, None]), slot_ids[None, :], 0),
-        axis=1,
-    )
-    picked = pick_rows(count, order, wanted, node_blocks)
+    asked, slot_of, tile_of_slot, degree_column = lax.optimization_barrier(
+        (asked, slot_of, tile_of_slot, degree_column)
+    )
+    picked, order, block_list, count = pick_rows(asked, node_blocks)
     arrived = lax.all_to_all(
         picked.reshape(owners, capacity, block_size, channels),
         "wide",
@@ -249,7 +260,7 @@
         tiled=True,
     )
     current = land_terms(
-        count, order, wanted, returned.reshape(slot_count, block_size, channels), node_blocks
+        count, order, block_list, returned.reshape(slot_count, block_size, channels), node_blocks
     ).reshape(node_block_count * block_size, channels)
     return current
 

time: 296 us -> 294 us (level)
  Pallas kernels: 30.1 us -> 33.3 us
where the time goes in v9:
time: 294 us
  blocking collectives  233 us (79%)
  Pallas kernels  33.3 us (11%)
  starting transfers between devices  15.5 us (5%)
  waiting for transfers between devices  6.92 us (2%)
  other arithmetic  3.75 us (1%)
    all_to_all x1, blocking collectives, body(): lax.all_to_all(outgoing.reshape(owners, capacity, block_size, channels),...  124 us
    all_to_all x1, blocking collectives, body(): lax.all_to_all(picked.reshape(owners, capacity, block_size, channels), 'w...  108 us
    pallas_call x1, Pallas kernels, round_kernel(): pl.pallas_call(functools.partial(_round_kernel, groups, per_block), out_s...  22.7 us
    all_to_all x1, starting transfers between devices, body(): lax.all_to_all(wanted_out.reshape(owners, 1, capacity), 'wide', split_axi...  15.5 us
    all_to_all x1, waiting for transfers between devices, body(): lax.all_to_all(wanted_out.reshape(owners, 1, capacity), 'wide', split_axi...  6.92 us
    pallas_call x1, Pallas kernels, pick_rows(): pl.pallas_call(_pick_kernel, out_shape=(jax.ShapeDtypeStruct((slots, rows...  5.98 us
  transfers between devices with their start and end apart: 1, of which 1 were waited for; matrix products, arithmetic and copies ran while one was open for 0% of the time, Pallas kernels for 0%

profile of v9, /device:TPU:88, one launch (start us, length us, event | category | flops | bytes accessed | tf_op | source)
XLA Modules:
  0.0 293.6 jit_solution(14439698822817708391)
XLA Ops:
  0.0 0.9 convert_reduce_fusion
  0.9 0.7 fusion.1
  1.6 0.7 broadcast_add_fusion.1
  2.2 0.1 select_reduce_fusion
  2.3 0.8 sub.7
  3.1 15.5 %all-to-all-start = ((s32[64,1,2]{2,1,0:T(1,128)}), s32[64,1,2]{2,1,0:T(1,128)S(1)}, u32[]{:S(2)}, u32[]{:S(2)}) async-start(s32[64,1,2]{2,1,0:T(1,128)} %bitcast.3), calls=%async_computation | async-start | bytes 65536 | tf_op jit(solution)/shard_map/all_to_all | solution.py:227
  18.6 0.7 multiply_add_fusion.slot_of_ref
  19.3 0.8 dynamic-slice_convert_fusion
  20.0 6.9 %all-to-all-done.asked_ref = s32[64,1,2]{2,1,0:T(1,128)S(1)} async-done(((s32[64,1,2]{2,1,0:T(1,128)}), s32[64,1,2]{2,1,0:T(1,128)S(1)}, u32[]{:S(2)}, u32[]{:S(2)}) %all-to-all-start) | async-done | bytes 544 | tf_op jit(solution)/shard_map/all_to_all | solution.py:227
  26.9 0.0 copy-start.3
  26.9 0.1 broadcast_in_dim.33.degree_ref
  27.0 0.5 copy-done.3
  27.5 6.0 %shard_map.73 = (bf16[128,128,128]{2,1,0:T(8,128)(2,1)}, s32[128]{0:T(128)}, s32[128]{0:T(128)}, s32[1]{0:T(128)}) custom-call(s32[64,1,2]{2,1,0:T(1,128)} %copy-done.3, bf16[16,128,128]{2,1,0:T(8,128)(2,1)} %bitcast.19), custom_call_target="tpu_custom_call" | custom-call | tf_op jit(solution)/shard_map/pallas_call | solution.py:144
  33.5 0.0 copy-start
  33.5 0.0 copy-start.1
  33.6 0.0 copy-start.2
  33.6 108.4 %all_to_all.15 = bf16[64,2,128,128]{3,2,1,0:T(8,128)(2,1)} all-to-all(bf16[64,2,128,128]{3,2,1,0:T(8,128)(2,1)} %bitcast.18), channel_id=1, replica_groups=mesh['wide'=64,'narrow'=8] {'wide'}, dimensions={0} | all-to-all | bytes 8388608 | tf_op jit(solution)/shard_map/all_to_all | solution.py:237
  142.0 0.0 copy-done
  142.0 0.0 copy-done.1
  142.0 0.0 copy-done.2
  142.0 22.7 %shard_map.74 = bf16[128,128,128]{2,1,0:T(8,128)(2,1)S(1)} custom-call(s32[16]{0:T(128)S(1)} %multiply_add_fusion.slot_of_ref, s32[128]{0:T(128)S(1)} %get-tuple-element.18.slot_tile_ref, bf16[128,128,128]{2,1,0:T(8,128)(2,1)} %bitcast.16, bf16[16,128,128]{2,1,0:T(8,128)(2,1)S(1)} %copy-done, f32[128,128]{1,0:T(8,128)S(1)} %broadcast_in_dim.33.degree_ref, ...), custom_call_target="tpu_custom_call" | custom-call | tf_op jit(solution)/shard_map/pallas_call | solution.py:88
  164.7 124.2 %all_to_all.16 = bf16[64,2,128,128]{3,2,1,0:T(8,128)(2,1)} all-to-all(bf16[64,2,128,128]{3,2,1,0:T(8,128)(2,1)S(1)} %bitcast.15), channel_id=1, replica_groups=mesh['wide'=64,'narrow'=8] {'wide'}, dimensions={0} | all-to-all | bytes 8388608 | tf_op jit(solution)/shard_map/all_to_all | solution.py:255
  289.0 4.6 %shard_map.75 = bf16[16,128,128]{2,1,0:T(8,128)(2,1)} custom-call(s32[1]{0:T(128)} %get-tuple-element.14.count_ref, s32[128]{0:T(128)} %get-tuple-element.15.order_ref, s32[128]{0:T(128)} %get-tuple-element.16.block_ref, bf16[128,128,128]{2,1,0:T(8,128)(2,1)} %bitcast.17, bf16[16,128,128]{2,1,0:T(8,128)(2,1)} %bitcast.20), custom_call_target="tpu_custom_call" | custom-call | tf_op jit(solution)/shard_map/pallas_call | solution.py:184
  (1 shorter events, 0.0 us)
Async XLA Ops:
  3.1 23.8 %all-to-all-start = ((s32[64,1,2]{2,1,0:T(1,128)}), s32[64,1,2]{2,1,0:T(1,128)S(1)}, u32[]{:S(2)}, u32[]{:S(2)}) async-start(s32[64,1,2]{2,1,0:T(1,128)} %bitcast.3), calls=%async_computation | async-start | bytes 65536 | tf_op jit(solution)/shard_map/all_to_all | solution.py:227
  26.9 0.6 copy-start.3
  33.5 108.5 %copy-start = (bf16[16,128,128]{2,1,0:T(8,128)(2,1)S(1)}, bf16[16,128,128]{2,1,0:T(8,128)(2,1)}, u32[]{:S(2)}) copy-start(bf16[16,128,128]{2,1,0:T(8,128)(2,1)} %tiles_ref.1) | copy-start | bytes 1572868
  33.5 108.5 %copy-start.1 = (bf16[128,512]{1,0:T(8,128)(2,1)S(1)}, bf16[128,512]{1,0:T(8,128)(2,1)}, u32[]{:S(2)}) copy-start(bf16[128,512]{1,0:T(8,128)(2,1)} %w_in_ref.1) | copy-start | bytes 393220
  33.6 108.4 %copy-start.2 = (bf16[512,128]{1,0:T(8,128)(2,1)S(1)}, bf16[512,128]{1,0:T(8,128)(2,1)}, u32[]{:S(2)}) copy-start(bf16[512,128]{1,0:T(8,128)(2,1)} %w_out_ref.1) | copy-start | bytes 393220

commit v10 on v8

--- a/solution.py
+++ b/solution.py
@@ -60,6 +60,16 @@
 
     for k in range(1, groups):
         second(lax.rem(me + k, groups)).start()
+
+    def block_terms(e, block):
+        for k in range(per_block):
+            t = e * per_block + k
+            term = lax.dot_general(
+                tiles_ref[t], block, (((0,), (0,)), ((), ())),
+                preferred_element_type=jnp.float32)
+            terms[t] = term.astype(jnp.bfloat16)
+
+    block_terms(me, own)
     for k in range(1, groups):
         d = lax.rem(me + k, groups)
         s = lax.rem(me + groups - k, groups)
@@ -67,12 +77,7 @@
         pltpu.make_async_remote_copy(
             src_ref=stage, dst_ref=edge_out.at[s], send_sem=send_b.at[s],
             recv_sem=recv_b.at[s], device_id=(col, s), device_id_type=MESH).wait_recv()
-
-    for t in range(tile_count):
-        term = lax.dot_general(
-            tiles_ref[t], edge_out[t // per_block], (((0,), (0,)), ((), ())),
-            preferred_element_type=jnp.float32)
-        terms[t] = term.astype(jnp.bfloat16)
+        block_terms(s, edge_out[s])
 
     def place(slot, carry):
         out_ref[slot] = terms[slot_tile_ref[slot]]

time: 296 us -> 298 us (level)
  the two profiles are of different devices: /device:TPU:88 before, /device:TPU:42 now
where the time goes in v10:
time: 298 us; the launch traced here: 297 us
  blocking collectives  239 us (80%)
  Pallas kernels  27.5 us (9%)
  starting transfers between devices  16.3 us (5%)
  waiting for transfers between devices  6.35 us (2%)
  other arithmetic  6.02 us (2%)
    all_to_all x1, blocking collectives, body(): lax.all_to_all(outgoing.reshape(owners, capacity, block_size, channels),...  128 us
    all_to_all x1, blocking collectives, body(): lax.all_to_all(picked.reshape(owners, capacity, block_size, channels), 'w...  112 us
    pallas_call x1, Pallas kernels, round_kernel(): pl.pallas_call(functools.partial(_round_kernel, groups, per_block), out_s...  19.5 us
    all_to_all x1, starting transfers between devices, body(): lax.all_to_all(wanted_out.reshape(owners, capacity), 'wide', split_axis=0...  16.3 us
    all_to_all x1, waiting for transfers between devices, body(): lax.all_to_all(wanted_out.reshape(owners, capacity), 'wide', split_axis=0...  6.35 us
  transfers between devices with their start and end apart: 1, of which 1 were waited for; matrix products, arithmetic and copies ran while one was open for 0% of the time, Pallas kernels for 0%

profile of v10, /device:TPU:42, one launch (start us, length us, event | category | flops | bytes accessed | tf_op | source)
XLA Modules:
  0.0 297.2 jit_solution(2366617522630745452)
XLA Ops:
  0.0 0.9 convert_reduce_fusion
  0.9 0.7 fusion.2
  1.6 0.7 broadcast_add_fusion.1
  2.2 0.1 select_reduce_fusion.1
  2.3 0.8 sub.11
  3.1 16.3 %all-to-all-start = ((s32[64,1,2]{2,1,0:T(1,128)}), s32[64,1,2]{2,1,0:T(1,128)S(1)}, u32[]{:S(2)}, u32[]{:S(2)}) async-start(s32[64,1,2]{2,1,0:T(1,128)} %bitcast.3), calls=%async_computation | async-start | bytes 65536 | tf_op jit(solution)/shard_map/all_to_all | solution.py:214
  19.4 0.7 multiply_add_fusion.slot_of_ref
  20.0 0.8 dynamic-slice_convert_fusion
  20.8 6.4 %all-to-all-done = s32[64,1,2]{2,1,0:T(1,128)S(1)} async-done(((s32[64,1,2]{2,1,0:T(1,128)}), s32[64,1,2]{2,1,0:T(1,128)S(1)}, u32[]{:S(2)}, u32[]{:S(2)}) %all-to-all-start) | async-done | bytes 544 | tf_op jit(solution)/shard_map/all_to_all | solution.py:214
  27.2 0.5 broadcast.50
  27.7 0.7 reduce.5
  28.4 0.1 reshape.74.wanted_ref
  28.5 0.0 copy-start.3
  28.5 0.1 broadcast_in_dim.49.degree_ref
  28.6 0.6 convert_reduce_fusion.1
  29.2 0.1 copy.13
  29.4 0.2 reduce-window.8
  29.5 0.1 add_reduce_fusion
  29.6 0.7 select_reduce_fusion.order_ref
  30.3 0.0 copy-done.3
  30.3 3.5 %shard_map.73 = bf16[128,128,128]{2,1,0:T(8,128)(2,1)} custom-call(s32[1]{0:T(128)} %bitcast.4.count_ref, s32[128]{0:T(128)} %select_reduce_fusion.order_ref, s32[128]{0:T(128)} %copy-done.3, bf16[16,128,128]{2,1,0:T(8,128)(2,1)} %bitcast.22), custom_call_target="tpu_custom_call" | custom-call | tf_op jit(solution)/shard_map/pallas_call | solution.py:136
  33.8 0.0 copy-start
  33.8 0.0 copy-start.1
  33.8 0.0 copy-start.2
  33.8 111.5 %all_to_all.16 = bf16[64,2,128,128]{3,2,1,0:T(8,128)(2,1)} all-to-all(bf16[64,2,128,128]{3,2,1,0:T(8,128)(2,1)} %bitcast.21), channel_id=1, replica_groups=mesh['wide'=64,'narrow'=8] {'wide'}, dimensions={0} | all-to-all | bytes 8388608 | tf_op jit(solution)/shard_map/all_to_all | solution.py:231
  145.3 0.0 copy-done
  145.4 0.0 copy-done.1
  145.4 0.0 copy-done.2
  145.4 19.5 %shard_map.74 = bf16[128,128,128]{2,1,0:T(8,128)(2,1)S(1)} custom-call(s32[16]{0:T(128)S(1)} %multiply_add_fusion.slot_of_ref, s32[128]{0:T(128)S(1)} %get-tuple-element.11.slot_tile_ref, bf16[128,128,128]{2,1,0:T(8,128)(2,1)} %bitcast.19, bf16[16,128,128]{2,1,0:T(8,128)(2,1)S(1)} %copy-done, f32[128,128]{1,0:T(8,128)S(1)} %broadcast_in_dim.49.degree_ref, ...), custom_call_target="tpu_custom_call" | custom-call | tf_op jit(solution)/shard_map/pallas_call | solution.py:93
  164.9 127.8 %all_to_all.17 = bf16[64,2,128,128]{3,2,1,0:T(8,128)(2,1)} all-to-all(bf16[64,2,128,128]{3,2,1,0:T(8,128)(2,1)S(1)} %bitcast.18), channel_id=1, replica_groups=mesh['wide'=64,'narrow'=8] {'wide'}, dimensions={0} | all-to-all | bytes 8388608 | tf_op jit(solution)/shard_map/all_to_all | solution.py:249
  292.6 4.5 %shard_map.75 = bf16[16,128,128]{2,1,0:T(8,128)(2,1)} custom-call(s32[1]{0:T(128)} %bitcast.4.count_ref, s32[128]{0:T(128)} %select_reduce_fusion.order_ref, s32[128]{0:T(128)} %copy-done.3, bf16[128,128,128]{2,1,0:T(8,128)(2,1)} %bitcast.20, bf16[16,128,128]{2,1,0:T(8,128)(2,1)} %bitcast.23), custom_call_target="tpu_custom_call" | custom-call | tf_op jit(solution)/shard_map/pallas_call | solution.py:171
  (2 shorter events, 0.0 us)
Async XLA Ops:
  3.1 24.1 %all-to-all-start = ((s32[64,1,2]{2,1,0:T(1,128)}), s32[64,1,2]{2,1,0:T(1,128)S(1)}, u32[]{:S(2)}, u32[]{:S(2)}) async-start(s32[64,1,2]{2,1,0:T(1,128)} %bitcast.3), calls=%async_computation | async-start | bytes 65536 | tf_op jit(solution)/shard_map/all_to_all | solution.py:214
  28.5 1.8 copy-start.3
  33.8 111.6 %copy-start = (bf16[16,128,128]{2,1,0:T(8,128)(2,1)S(1)}, bf16[16,128,128]{2,1,0:T(8,128)(2,1)}, u32[]{:S(2)}) copy-start(bf16[16,128,128]{2,1,0:T(8,128)(2,1)} %tiles_ref.1) | copy-start | bytes 1572868
  33.8 111.5 %copy-start.1 = (bf16[128,512]{1,0:T(8,128)(2,1)S(1)}, bf16[128,512]{1,0:T(8,128)(2,1)}, u32[]{:S(2)}) copy-start(bf16[128,512]{1,0:T(8,128)(2,1)} %w_in_ref.1) | copy-start | bytes 393220
  33.8 111.5 %copy-start.2 = (bf16[512,128]{1,0:T(8,128)(2,1)S(1)}, bf16[512,128]{1,0:T(8,128)(2,1)}, u32[]{:S(2)}) copy-start(bf16[512,128]{1,0:T(8,128)(2,1)} %w_out_ref.1) | copy-start | bytes 393220

commit v11 on v10

--- a/solution.py
+++ b/solution.py
@@ -11,7 +11,7 @@
 
 def _round_kernel(groups, per_block, slot_of_ref, slot_tile_ref, arrived_ref, tiles_ref,
                   degree_ref, w_in_ref, w_out_ref, out_ref,
-                  parts, inbox, stage, edge_out, terms, send_a, recv_a, send_b, recv_b):
+                  parts, inbox, stage, edge_out, terms, send_a, recv_a, send_b, recv_b, exact):
     me = lax.axis_index("narrow")
     col = lax.axis_index("wide")
     tile_count = tiles_ref.shape[0]
@@ -26,7 +26,8 @@
             rows = arrived_ref[slot_of_ref[t]]
             p = jnp.dot(tiles_ref[t], rows, preferred_element_type=jnp.float32)
             acc = p if acc is None else acc + p
-        parts[e] = acc
+        parts[e] = acc.astype(parts.dtype)
+        exact[e] = acc
 
     pl.semaphore_wait(barrier, groups - 1)
 
@@ -37,7 +38,7 @@
 
     for k in range(1, groups):
         first(lax.rem(me + k, groups)).start()
-    total = parts[me]
+    total = exact[me]
     for k in range(1, groups):
         d = lax.rem(me + k, groups)
         s = lax.rem(me + groups - k, groups)
@@ -45,7 +46,7 @@
         pltpu.make_async_remote_copy(
             src_ref=parts.at[s], dst_ref=inbox.at[s], send_sem=send_a.at[s],
             recv_sem=recv_a.at[s], device_id=(col, s), device_id_type=MESH).wait_recv()
-        total = total + inbox[s]
+        total = total + inbox[s].astype(jnp.float32)
     edge_in = (total / degree_ref[...]).astype(jnp.bfloat16)
     pre = jnp.dot(edge_in, w_in_ref[...], preferred_element_type=jnp.float32)
     hidden = (pre * jax.nn.sigmoid(pre)).astype(jnp.bfloat16)
@@ -96,13 +97,14 @@
         in_specs=[smem, smem] + [vmem] * 5,
         out_specs=vmem,
         scratch_shapes=[
-            pltpu.VMEM((groups, rows, channels), jnp.float32),
-            pltpu.VMEM((groups, rows, channels), jnp.float32),
+            pltpu.VMEM((groups, rows, channels), jnp.bfloat16),
+            pltpu.VMEM((groups, rows, channels), jnp.bfloat16),
             pltpu.VMEM((rows, channels), jnp.bfloat16),
             pltpu.VMEM((groups, rows, channels), jnp.bfloat16),
             pltpu.VMEM(tiles.shape, jnp.bfloat16),
             pltpu.SemaphoreType.DMA((groups,)), pltpu.SemaphoreType.DMA((groups,)),
             pltpu.SemaphoreType.DMA((groups,)), pltpu.SemaphoreType.DMA((groups,)),
+            pltpu.VMEM((groups, rows, channels), jnp.float32),
         ],
         compiler_params=pltpu.CompilerParams(
             collective_id=0, has_side_effects=True, vmem_limit_bytes=48 * 1024 * 1024),

time: 298 us -> 292 us (0.980)
  the two profiles are of different devices: /device:TPU:42 before, /device:TPU:46 now
where the time goes in v11:
time: 292 us
  blocking collectives  238 us (82%)
  Pallas kernels  23.8 us (8%)
  starting transfers between devices  16.3 us (6%)
  waiting for transfers between devices  6.35 us (2%)
  other arithmetic  6.02 us (2%)
    all_to_all x1, blocking collectives, body(): lax.all_to_all(outgoing.reshape(owners, capacity, block_size, channels),...  125 us
    all_to_all x1, blocking collectives, body(): lax.all_to_all(picked.reshape(owners, capacity, block_size, channels), 'w...  113 us
    all_to_all x1, starting transfers between devices, body(): lax.all_to_all(wanted_out.reshape(owners, capacity), 'wide', split_axis=0...  16.3 us
    pallas_call x1, Pallas kernels, round_kernel(): pl.pallas_call(functools.partial(_round_kernel, groups, per_block), out_s...  15.7 us
    all_to_all x1, waiting for transfers between devices, body(): lax.all_to_all(wanted_out.reshape(owners, capacity), 'wide', split_axis=0...  6.35 us
  transfers between devices with their start and end apart: 1, of which 1 were waited for; matrix products, arithmetic and copies ran while one was open for 0% of the time, Pallas kernels for 0%

profile of v11, /device:TPU:46, one launch (start us, length us, event | category | flops | bytes accessed | tf_op | source)
XLA Modules:
  0.0 291.9 jit_solution(13255150322064862945)
XLA Ops:
  0.0 0.9 convert_reduce_fusion
  0.9 0.7 fusion.2
  1.6 0.7 broadcast_add_fusion.1
  2.2 0.1 select_reduce_fusion.1
  2.3 0.8 sub.11
  3.1 16.3 %all-to-all-start = ((s32[64,1,2]{2,1,0:T(1,128)}), s32[64,1,2]{2,1,0:T(1,128)S(1)}, u32[]{:S(2)}, u32[]{:S(2)}) async-start(s32[64,1,2]{2,1,0:T(1,128)} %bitcast.3), calls=%async_computation | async-start | bytes 65536 | tf_op jit(solution)/shard_map/all_to_all | solution.py:216
  19.4 0.7 multiply_add_fusion.slot_of_ref
  20.0 0.8 dynamic-slice_convert_fusion
  20.8 6.4 %all-to-all-done = s32[64,1,2]{2,1,0:T(1,128)S(1)} async-done(((s32[64,1,2]{2,1,0:T(1,128)}), s32[64,1,2]{2,1,0:T(1,128)S(1)}, u32[]{:S(2)}, u32[]{:S(2)}) %all-to-all-start) | async-done | bytes 544 | tf_op jit(solution)/shard_map/all_to_all | solution.py:216
  27.2 0.5 broadcast.50
  27.7 0.7 reduce.5
  28.4 0.1 reshape.74.wanted_ref
  28.5 0.0 copy-start.3
  28.5 0.1 broadcast_in_dim.49.degree_ref
  28.6 0.6 convert_reduce_fusion.1
  29.2 0.1 copy.13
  29.4 0.2 reduce-window.8
  29.5 0.1 add_reduce_fusion
  29.6 0.7 select_reduce_fusion.order_ref
  30.3 0.0 copy-done.3
  30.3 3.5 %shard_map.73 = bf16[128,128,128]{2,1,0:T(8,128)(2,1)} custom-call(s32[1]{0:T(128)} %bitcast.4.count_ref, s32[128]{0:T(128)} %select_reduce_fusion.order_ref, s32[128]{0:T(128)} %copy-done.3, bf16[16,128,128]{2,1,0:T(8,128)(2,1)} %bitcast.22), custom_call_target="tpu_custom_call" | custom-call | tf_op jit(solution)/shard_map/pallas_call | solution.py:138
  33.8 0.0 copy-start
  33.8 0.0 copy-start.1
  33.9 0.0 copy-start.2
  33.9 113.0 %all_to_all.16 = bf16[64,2,128,128]{3,2,1,0:T(8,128)(2,1)} all-to-all(bf16[64,2,128,128]{3,2,1,0:T(8,128)(2,1)} %bitcast.21), channel_id=1, replica_groups=mesh['wide'=64,'narrow'=8] {'wide'}, dimensions={0} | all-to-all | bytes 8388608 | tf_op jit(solution)/shard_map/all_to_all | solution.py:233
  146.9 0.0 copy-done
  146.9 0.0 copy-done.1
  146.9 0.0 copy-done.2
  146.9 15.7 %shard_map.74 = bf16[128,128,128]{2,1,0:T(8,128)(2,1)S(1)} custom-call(s32[16]{0:T(128)S(1)} %multiply_add_fusion.slot_of_ref, s32[128]{0:T(128)S(1)} %get-tuple-element.11.slot_tile_ref, bf16[128,128,128]{2,1,0:T(8,128)(2,1)} %bitcast.19, bf16[16,128,128]{2,1,0:T(8,128)(2,1)S(1)} %copy-done, f32[128,128]{1,0:T(8,128)S(1)} %broadcast_in_dim.49.degree_ref, ...), custom_call_target="tpu_custom_call" | custom-call | tf_op jit(solution)/shard_map/pallas_call | solution.py:94
  162.6 124.8 %all_to_all.17 = bf16[64,2,128,128]{3,2,1,0:T(8,128)(2,1)} all-to-all(bf16[64,2,128,128]{3,2,1,0:T(8,128)(2,1)S(1)} %bitcast.18), channel_id=1, replica_groups=mesh['wide'=64,'narrow'=8] {'wide'}, dimensions={0} | all-to-all | bytes 8388608 | tf_op jit(solution)/shard_map/all_to_all | solution.py:251
  287.3 4.6 %shard_map.75 = bf16[16,128,128]{2,1,0:T(8,128)(2,1)} custom-call(s32[1]{0:T(128)} %bitcast.4.count_ref, s32[128]{0:T(128)} %select_reduce_fusion.order_ref, s32[128]{0:T(128)} %copy-done.3, bf16[128,128,128]{2,1,0:T(8,128)(2,1)} %bitcast.20, bf16[16,128,128]{2,1,0:T(8,128)(2,1)} %bitcast.23), custom_call_target="tpu_custom_call" | custom-call | tf_op jit(solution)/shard_map/pallas_call | solution.py:173
  (2 shorter events, 0.0 us)
Async XLA Ops:
  3.1 24.1 %all-to-all-start = ((s32[64,1,2]{2,1,0:T(1,128)}), s32[64,1,2]{2,1,0:T(1,128)S(1)}, u32[]{:S(2)}, u32[]{:S(2)}) async-start(s32[64,1,2]{2,1,0:T(1,128)} %bitcast.3), calls=%async_computation | async-start | bytes 65536 | tf_op jit(solution)/shard_map/all_to_all | solution.py:216
  28.5 1.8 copy-start.3
  33.8 113.1 %copy-start = (bf16[16,128,128]{2,1,0:T(8,128)(2,1)S(1)}, bf16[16,128,128]{2,1,0:T(8,128)(2,1)}, u32[]{:S(2)}) copy-start(bf16[16,128,128]{2,1,0:T(8,128)(2,1)} %tiles_ref.1) | copy-start | bytes 1572868
  33.8 113.1 %copy-start.1 = (bf16[128,512]{1,0:T(8,128)(2,1)S(1)}, bf16[128,512]{1,0:T(8,128)(2,1)}, u32[]{:S(2)}) copy-start(bf16[128,512]{1,0:T(8,128)(2,1)} %w_in_ref.1) | copy-start | bytes 393220
  33.9 113.1 %copy-start.2 = (bf16[512,128]{1,0:T(8,128)(2,1)S(1)}, bf16[512,128]{1,0:T(8,128)(2,1)}, u32[]{:S(2)}) copy-start(bf16[512,128]{1,0:T(8,128)(2,1)} %w_out_ref.1) | copy-start | bytes 393220

commit v12 on v10

--- a/solution.py
+++ b/solution.py
@@ -83,7 +83,7 @@
         out_ref[slot] = terms[slot_tile_ref[slot]]
         return carry
 
-    lax.fori_loop(0, out_ref.shape[0], place, 0)
+    lax.fori_loop(0, out_ref.shape[0], place, 0, unroll=8)
 
 
 def round_kernel(slot_of, slot_tile, arrived, tiles, degree, w_in, w_out, groups, per_block):

time: 298 us -> 293 us (0.983)
  the two profiles are of different devices: /device:TPU:42 before, /device:TPU:24 now
where the time goes in v12:
time: 293 us; the launch traced here: 292 us
  blocking collectives  231 us (79%)
  Pallas kernels  29.8 us (10%)
  starting transfers between devices  16.4 us (6%)
  waiting for transfers between devices  7.81 us (3%)
  other arithmetic  6.02 us (2%)
    all_to_all x1, blocking collectives, body(): lax.all_to_all(outgoing.reshape(owners, capacity, block_size, channels),...  121 us
    all_to_all x1, blocking collectives, body(): lax.all_to_all(picked.reshape(owners, capacity, block_size, channels), 'w...  109 us
    pallas_call x1, Pallas kernels, round_kernel(): pl.pallas_call(functools.partial(_round_kernel, groups, per_block), out_s...  20.2 us
    all_to_all x1, starting transfers between devices, body(): lax.all_to_all(wanted_out.reshape(owners, capacity), 'wide', split_axis=0...  16.4 us
    all_to_all x1, waiting for transfers between devices, body(): lax.all_to_all(wanted_out.reshape(owners, capacity), 'wide', split_axis=0...  7.81 us
  transfers between devices with their start and end apart: 1, of which 1 were waited for; matrix products, arithmetic and copies ran while one was open for 0% of the time, Pallas kernels for 0%

profile of v12, /device:TPU:24, one launch (start us, length us, event | category | flops | bytes accessed | tf_op | source)
XLA Modules:
  0.0 292.3 jit_solution(2106786104434171078)
XLA Ops:
  0.0 0.9 convert_reduce_fusion
  0.9 0.7 fusion.2
  1.6 0.7 broadcast_add_fusion.1
  2.2 0.1 select_reduce_fusion.1
  2.3 0.8 sub.11
  3.1 16.4 %all-to-all-start = ((s32[64,1,2]{2,1,0:T(1,128)}), s32[64,1,2]{2,1,0:T(1,128)S(1)}, u32[]{:S(2)}, u32[]{:S(2)}) async-start(s32[64,1,2]{2,1,0:T(1,128)} %bitcast.3), calls=%async_computation | async-start | bytes 65536 | tf_op jit(solution)/shard_map/all_to_all | solution.py:214
  19.5 0.7 multiply_add_fusion.slot_of_ref
  20.2 0.8 dynamic-slice_convert_fusion
  20.9 7.8 %all-to-all-done = s32[64,1,2]{2,1,0:T(1,128)S(1)} async-done(((s32[64,1,2]{2,1,0:T(1,128)}), s32[64,1,2]{2,1,0:T(1,128)S(1)}, u32[]{:S(2)}, u32[]{:S(2)}) %all-to-all-start) | async-done | bytes 544 | tf_op jit(solution)/shard_map/all_to_all | solution.py:214
  28.7 0.5 broadcast.50
  29.2 0.7 reduce.5
  30.0 0.1 reshape.74.wanted_ref
  30.1 0.0 copy-start.3
  30.1 0.1 broadcast_in_dim.49.degree_ref
  30.2 0.6 convert_reduce_fusion.1
  30.8 0.1 copy.13
  30.9 0.2 reduce-window.8
  31.1 0.1 add_reduce_fusion
  31.2 0.7 select_reduce_fusion.order_ref
  31.9 0.0 copy-done.3
  31.9 4.1 %shard_map.73 = bf16[128,128,128]{2,1,0:T(8,128)(2,1)} custom-call(s32[1]{0:T(128)} %bitcast.4.count_ref, s32[128]{0:T(128)} %select_reduce_fusion.order_ref, s32[128]{0:T(128)} %copy-done.3, bf16[16,128,128]{2,1,0:T(8,128)(2,1)} %bitcast.22), custom_call_target="tpu_custom_call" | custom-call | tf_op jit(solution)/shard_map/pallas_call | solution.py:136
  36.0 0.0 copy-start
  36.0 0.0 copy-start.1
  36.0 0.0 copy-start.2
  36.1 109.3 %all_to_all.16 = bf16[64,2,128,128]{3,2,1,0:T(8,128)(2,1)} all-to-all(bf16[64,2,128,128]{3,2,1,0:T(8,128)(2,1)} %bitcast.21), channel_id=1, replica_groups=mesh['wide'=64,'narrow'=8] {'wide'}, dimensions={0} | all-to-all | bytes 8388608 | tf_op jit(solution)/shard_map/all_to_all | solution.py:231
  145.3 0.0 copy-done
  145.3 0.0 copy-done.1
  145.3 0.0 copy-done.2
  145.4 20.2 %shard_map.74 = bf16[128,128,128]{2,1,0:T(8,128)(2,1)S(1)} custom-call(s32[16]{0:T(128)S(1)} %multiply_add_fusion.slot_of_ref, s32[128]{0:T(128)S(1)} %get-tuple-element.11.slot_tile_ref, bf16[128,128,128]{2,1,0:T(8,128)(2,1)} %bitcast.19, bf16[16,128,128]{2,1,0:T(8,128)(2,1)S(1)} %copy-done, f32[128,128]{1,0:T(8,128)S(1)} %broadcast_in_dim.49.degree_ref, ...), custom_call_target="tpu_custom_call" | custom-call | tf_op jit(solution)/shard_map/pallas_call | solution.py:93
  165.6 121.3 %all_to_all.17 = bf16[64,2,128,128]{3,2,1,0:T(8,128)(2,1)} all-to-all(bf16[64,2,128,128]{3,2,1,0:T(8,128)(2,1)S(1)} %bitcast.18), channel_id=1, replica_groups=mesh['wide'=64,'narrow'=8] {'wide'}, dimensions={0} | all-to-all | bytes 8388608 | tf_op jit(solution)/shard_map/all_to_all | solution.py:249
  286.9 5.4 %shard_map.75 = bf16[16,128,128]{2,1,0:T(8,128)(2,1)} custom-call(s32[1]{0:T(128)} %bitcast.4.count_ref, s32[128]{0:T(128)} %select_reduce_fusion.order_ref, s32[128]{0:T(128)} %copy-done.3, bf16[128,128,128]{2,1,0:T(8,128)(2,1)} %bitcast.20, bf16[16,128,128]{2,1,0:T(8,128)(2,1)} %bitcast.23), custom_call_target="tpu_custom_call" | custom-call | tf_op jit(solution)/shard_map/pallas_call | solution.py:171
  (2 shorter events, 0.0 us)
Async XLA Ops:
  3.1 25.6 %all-to-all-start = ((s32[64,1,2]{2,1,0:T(1,128)}), s32[64,1,2]{2,1,0:T(1,128)S(1)}, u32[]{:S(2)}, u32[]{:S(2)}) async-start(s32[64,1,2]{2,1,0:T(1,128)} %bitcast.3), calls=%async_computation | async-start | bytes 65536 | tf_op jit(solution)/shard_map/all_to_all | solution.py:214
  30.1 1.8 copy-start.3
  36.0 109.3 %copy-start = (bf16[16,128,128]{2,1,0:T(8,128)(2,1)S(1)}, bf16[16,128,128]{2,1,0:T(8,128)(2,1)}, u32[]{:S(2)}) copy-start(bf16[16,128,128]{2,1,0:T(8,128)(2,1)} %tiles_ref.1) | copy-start | bytes 1572868
  36.0 109.3 %copy-start.1 = (bf16[128,512]{1,0:T(8,128)(2,1)S(1)}, bf16[128,512]{1,0:T(8,128)(2,1)}, u32[]{:S(2)}) copy-start(bf16[128,512]{1,0:T(8,128)(2,1)} %w_in_ref.1) | copy-start | bytes 393220
  36.0 109.3 %copy-start.2 = (bf16[512,128]{1,0:T(8,128)(2,1)S(1)}, bf16[512,128]{1,0:T(8,128)(2,1)}, u32[]{:S(2)}) copy-start(bf16[512,128]{1,0:T(8,128)(2,1)} %w_out_ref.1) | copy-start | bytes 393220

commit v13 on v12

--- a/solution.py
+++ b/solution.py
@@ -9,24 +9,15 @@
 MESH = pl.DeviceIdType.MESH
 
 
-def _round_kernel(groups, per_block, slot_of_ref, slot_tile_ref, arrived_ref, tiles_ref,
+def _round_kernel(groups, per_block, slot_tile_ref, parts, tiles_ref,
                   degree_ref, w_in_ref, w_out_ref, out_ref,
-                  parts, inbox, stage, edge_out, terms, send_a, recv_a, send_b, recv_b):
+                  inbox, stage, edge_out, terms, send_a, recv_a, send_b, recv_b):
     me = lax.axis_index("narrow")
     col = lax.axis_index("wide")
     tile_count = tiles_ref.shape[0]
     barrier = pltpu.get_barrier_semaphore()
     for k in range(1, groups):
         pl.semaphore_signal(barrier, inc=1, device_id=(col, lax.rem(me + k, groups)), device_id_type=MESH)
-
-    for e in range(tile_count // per_block):
-        acc = None
-        for k in range(per_block):
-            t = e * per_block + k
-            rows = arrived_ref[slot_of_ref[t]]
-            p = jnp.dot(tiles_ref[t], rows, preferred_element_type=jnp.float32)
-            acc = p if acc is None else acc + p
-        parts[e] = acc
 
     pl.semaphore_wait(barrier, groups - 1)
 
@@ -86,17 +77,50 @@
     lax.fori_loop(0, out_ref.shape[0], place, 0, unroll=8)
 
 
-def round_kernel(slot_of, slot_tile, arrived, tiles, degree, w_in, w_out, groups, per_block):
-    slots, rows, channels = arrived.shape
+def _product_kernel(per_block, slot_of_ref, arrived_ref, tiles_ref, out_ref, rows, sems):
+    last = arrived_ref.shape[0] - 1
+    copies = [
+        pltpu.make_async_copy(
+            arrived_ref.at[jnp.minimum(slot_of_ref[t], last)], rows.at[t], sems.at[t])
+        for t in range(tiles_ref.shape[0])
+    ]
+    for copy in copies:
+        copy.start()
+    for e in range(out_ref.shape[0]):
+        acc = None
+        for k in range(per_block):
+            t = e * per_block + k
+            copies[t].wait()
+            p = jnp.dot(tiles_ref[t], rows[t], preferred_element_type=jnp.float32)
+            acc = p if acc is None else acc + p
+        out_ref[e] = acc
+
+
+def tile_products(slot_of, arrived, tiles, per_block):
+    count, rows, channels = tiles.shape
+    return pl.pallas_call(
+        functools.partial(_product_kernel, per_block),
+        out_shape=jax.ShapeDtypeStruct((count // per_block, rows, channels), jnp.float32),
+        in_specs=[
+            pl.BlockSpec(memory_space=pltpu.SMEM),
+            pl.BlockSpec(memory_space=pl.ANY),
+            pl.BlockSpec(memory_space=pltpu.VMEM),
+        ],
+        out_specs=pl.BlockSpec(memory_space=pltpu.VMEM),
+        scratch_shapes=[pltpu.VMEM(tiles.shape, tiles.dtype), pltpu.SemaphoreType.DMA((count,))],
+    )(slot_of, arrived, tiles)
+
+
+def round_kernel(slot_tile, parts, slots, tiles, degree, w_in, w_out, groups, per_block):
+    _, rows, channels = parts.shape
     vmem = pl.BlockSpec(memory_space=pltpu.VMEM)
     smem = pl.BlockSpec(memory_space=pltpu.SMEM)
     return pl.pallas_call(
         functools.partial(_round_kernel, groups, per_block),
         out_shape=jax.ShapeDtypeStruct((slots, rows, channels), jnp.bfloat16),
-        in_specs=[smem, smem] + [vmem] * 5,
+        in_specs=[smem] + [vmem] * 5,
         out_specs=vmem,
         scratch_shapes=[
-            pltpu.VMEM((groups, rows, channels), jnp.float32),
             pltpu.VMEM((groups, rows, channels), jnp.float32),
             pltpu.VMEM((rows, channels), jnp.bfloat16),
             pltpu.VMEM((groups, rows, channels), jnp.bfloat16),
@@ -106,7 +130,7 @@
         ],
         compiler_params=pltpu.CompilerParams(
             collective_id=0, has_side_effects=True, vmem_limit_bytes=48 * 1024 * 1024),
-    )(slot_of, slot_tile, arrived, tiles, degree, w_in, w_out)
+    )(slot_tile, parts, tiles, degree, w_in, w_out)
 
 
 def _pick_kernel(count_ref, order_ref, wanted_ref, rows_ref, out_ref, sems):
@@ -235,10 +259,13 @@
         concat_axis=0,
         tiled=True,
     )
+    parts = tile_products(
+        slot_of, arrived.reshape(slot_count, block_size, channels), tile_values, per_block
+    )
     outgoing = round_kernel(
-        slot_of,
         tile_of_slot,
-        arrived.reshape(slot_count, block_size, channels),
+        parts,
+        slot_count,
         tile_values,
         degree_column,
         w_in,

time: 293 us -> 297 us (1.014)
  the two profiles are of different devices: /device:TPU:24 before, /device:TPU:38 now
where the time goes in v13:
time: 297 us; the launch traced here: 296 us
  blocking collectives  236 us (79%)
  Pallas kernels  29.3 us (10%)
  starting transfers between devices  16.3 us (5%)
  other arithmetic  6.54 us (2%)
  waiting for transfers between devices  5.18 us (2%)
    all_to_all x1, blocking collectives, body(): lax.all_to_all(outgoing.reshape(owners, capacity, block_size, channels),...  126 us
    all_to_all x1, blocking collectives, body(): lax.all_to_all(picked.reshape(owners, capacity, block_size, channels), 'w...  110 us
    pallas_call x1, Pallas kernels, round_kernel(): pl.pallas_call(functools.partial(_round_kernel, groups, per_block), out_s...  17 us
    all_to_all x1, starting transfers between devices, body(): lax.all_to_all(wanted_out.reshape(owners, capacity), 'wide', split_axis=0...  16.3 us
  transfers between devices with their start and end apart: 1, of which 1 were waited for; matrix products, arithmetic and copies ran while one was open for 1% of the time, Pallas kernels for 0%

profile of v13, /device:TPU:38, one launch (start us, length us, event | category | flops | bytes accessed | tf_op | source)
XLA Modules:
  0.0 296.0 jit_solution(11736916136170510253)
XLA Ops:
  0.0 0.9 convert_reduce_fusion
  0.9 0.7 fusion.2
  1.6 0.7 broadcast_add_fusion.1
  2.2 0.1 select_reduce_fusion.1
  2.3 0.8 sub.11
  3.1 16.3 %all-to-all-start = ((s32[64,1,2]{2,1,0:T(1,128)}), s32[64,1,2]{2,1,0:T(1,128)S(1)}, u32[]{:S(2)}, u32[]{:S(2)}) async-start(s32[64,1,2]{2,1,0:T(1,128)} %bitcast.3), calls=%async_computation | async-start | bytes 65536 | tf_op jit(solution)/shard_map/all_to_all | solution.py:238
  19.4 1.2 multiply_add_fusion.slot_of_ref
  20.6 0.8 dynamic-slice_convert_fusion
  21.4 5.2 %all-to-all-done = s32[64,1,2]{2,1,0:T(1,128)S(1)} async-done(((s32[64,1,2]{2,1,0:T(1,128)}), s32[64,1,2]{2,1,0:T(1,128)S(1)}, u32[]{:S(2)}, u32[]{:S(2)}) %all-to-all-start) | async-done | bytes 544 | tf_op jit(solution)/shard_map/all_to_all | solution.py:238
  26.6 0.5 broadcast.50
  27.1 0.7 reduce.5
  27.8 0.1 reshape.74.wanted_ref
  27.9 0.0 copy-start.4
  28.0 0.1 broadcast_in_dim.49.degree_ref
  28.0 0.6 convert_reduce_fusion.1
  28.7 0.1 copy.13
  28.8 0.2 reduce-window.8
  28.9 0.1 add_reduce_fusion
  29.0 0.7 select_reduce_fusion.order_ref
  29.7 0.0 copy-done.4
  29.7 3.5 %shard_map.73 = bf16[128,128,128]{2,1,0:T(8,128)(2,1)} custom-call(s32[1]{0:T(128)} %bitcast.4.count_ref, s32[128]{0:T(128)} %select_reduce_fusion.order_ref, s32[128]{0:T(128)} %copy-done.4, bf16[16,128,128]{2,1,0:T(8,128)(2,1)} %bitcast.22), custom_call_target="tpu_custom_call" | custom-call | tf_op jit(solution)/shard_map/pallas_call | solution.py:160
  33.2 110.1 %all_to_all.16 = bf16[64,2,128,128]{3,2,1,0:T(8,128)(2,1)} all-to-all(bf16[64,2,128,128]{3,2,1,0:T(8,128)(2,1)} %bitcast.21), channel_id=1, replica_groups=mesh['wide'=64,'narrow'=8] {'wide'}, dimensions={0} | all-to-all | bytes 8388608 | tf_op jit(solution)/shard_map/all_to_all | solution.py:255
  143.3 0.0 copy-start
  143.3 0.0 copy-start.2
  143.3 0.0 copy-start.3
  143.3 4.2 %shard_map.74.parts = f32[8,128,128]{2,1,0:T(8,128)} custom-call(s32[16]{0:T(128)} %multiply_add_fusion.slot_of_ref, bf16[128,128,128]{2,1,0:T(8,128)(2,1)} %bitcast.20, bf16[16,128,128]{2,1,0:T(8,128)(2,1)} %tiles_ref.3), custom_call_target="tpu_custom_call" | custom-call | tf_op jit(solution)/shard_map/pallas_call | solution.py:101
  147.6 0.0 copy-done
  147.6 0.0 copy-done.2
  147.6 0.0 copy-done.3
  147.6 0.0 copy-start.1
  147.6 1.0 copy-done.1
  148.6 17.0 %shard_map.75 = bf16[128,128,128]{2,1,0:T(8,128)(2,1)S(1)} custom-call(s32[128]{0:T(128)S(1)} %get-tuple-element.10.slot_tile_ref, f32[8,128,128]{2,1,0:T(8,128)S(1)} %copy-done.1, bf16[16,128,128]{2,1,0:T(8,128)(2,1)S(1)} %copy-done, f32[128,128]{1,0:T(8,128)S(1)} %broadcast_in_dim.49.degree_ref, bf16[128,512]{1,0:T(8,128)(2,1)S(1)} %copy-done.2, ...), custom_call_target="tpu_custom_call" | custom-call | tf_op jit(solution)/shard_map/pallas_call | solution.py:118
  165.7 125.8 %all_to_all.17 = bf16[64,2,128,128]{3,2,1,0:T(8,128)(2,1)} all-to-all(bf16[64,2,128,128]{3,2,1,0:T(8,128)(2,1)S(1)} %bitcast.18), channel_id=1, replica_groups=mesh['wide'=64,'narrow'=8] {'wide'}, dimensions={0} | all-to-all | bytes 8388608 | tf_op jit(solution)/shard_map/all_to_all | solution.py:276
  291.5 4.6 %shard_map.76 = bf16[16,128,128]{2,1,0:T(8,128)(2,1)} custom-call(s32[1]{0:T(128)} %bitcast.4.count_ref, s32[128]{0:T(128)} %select_reduce_fusion.order_ref, s32[128]{0:T(128)} %copy-done.4, bf16[128,128,128]{2,1,0:T(8,128)(2,1)} %bitcast.19, bf16[16,128,128]{2,1,0:T(8,128)(2,1)} %bitcast.23), custom_call_target="tpu_custom_call" | custom-call | tf_op jit(solution)/shard_map/pallas_call | solution.py:195
  (2 shorter events, 0.0 us)
Async XLA Ops:
  3.1 23.5 %all-to-all-start = ((s32[64,1,2]{2,1,0:T(1,128)}), s32[64,1,2]{2,1,0:T(1,128)S(1)}, u32[]{:S(2)}, u32[]{:S(2)}) async-start(s32[64,1,2]{2,1,0:T(1,128)} %bitcast.3), calls=%async_computation | async-start | bytes 65536 | tf_op jit(solution)/shard_map/all_to_all | solution.py:238
  27.9 1.8 copy-start.4
  143.3 4.2 %copy-start = (bf16[16,128,128]{2,1,0:T(8,128)(2,1)S(1)}, bf16[16,128,128]{2,1,0:T(8,128)(2,1)}, u32[]{:S(2)}) copy-start(bf16[16,128,128]{2,1,0:T(8,128)(2,1)} %tiles_ref.3) | copy-start | bytes 1572868
  143.3 4.2 %copy-start.2 = (bf16[128,512]{1,0:T(8,128)(2,1)S(1)}, bf16[128,512]{1,0:T(8,128)(2,1)}, u32[]{:S(2)}) copy-start(bf16[128,512]{1,0:T(8,128)(2,1)} %w_in_ref.1) | copy-start | bytes 393220
  143.3 4.2 %copy-start.3 = (bf16[512,128]{1,0:T(8,128)(2,1)S(1)}, bf16[512,128]{1,0:T(8,128)(2,1)}, u32[]{:S(2)}) copy-start(bf16[512,128]{1,0:T(8,128)(2,1)} %w_out_ref.1) | copy-start | bytes 393220
  147.6 1.0 copy-start.1

commit v14 on v12

--- a/solution.py
+++ b/solution.py
@@ -221,7 +221,8 @@
         (wanted, slot_of, tile_of_slot, degree_column)
     )
     filled = wanted >= 0
-    rank = jnp.cumsum(filled.astype(jnp.int32)) - 1
+    before = filled[None, :] & (slot_ids[None, :] < slot_ids[:, None])
+    rank = jnp.sum(before.astype(jnp.int32), axis=1)
     count = jnp.sum(filled.astype(jnp.int32)).reshape(1)
     order = jnp.sum(
         jnp.where(filled[None, :] & (rank[None, :] == slot_ids[:, None]), slot_ids[None, :], 0),

time: 293 us -> 294 us (level)
  the two profiles are of different devices: /device:TPU:24 before, /device:TPU:32 now
where the time goes in v14:
time: 294 us
  blocking collectives  235 us (80%)
  Pallas kernels  29.9 us (10%)
  starting transfers between devices  16.3 us (6%)
  other arithmetic  5.85 us (2%)
  waiting for transfers between devices  5.7 us (2%)
    all_to_all x1, blocking collectives, body(): lax.all_to_all(outgoing.reshape(owners, capacity, block_size, channels),...  123 us
    all_to_all x1, blocking collectives, body(): lax.all_to_all(picked.reshape(owners, capacity, block_size, channels), 'w...  112 us
    pallas_call x1, Pallas kernels, round_kernel(): pl.pallas_call(functools.partial(_round_kernel, groups, per_block), out_s...  21.9 us
    all_to_all x1, starting transfers between devices, body(): lax.all_to_all(wanted_out.reshape(owners, capacity), 'wide', split_axis=0...  16.3 us
  transfers between devices with their start and end apart: 1, of which 1 were waited for; matrix products, arithmetic and copies ran while one was open for 0% of the time, Pallas kernels for 0%

profile of v14, /device:TPU:32, one launch (start us, length us, event | category | flops | bytes accessed | tf_op | source)
XLA Modules:
  0.0 293.9 jit_solution(5672558799226088589)
XLA Ops:
  0.0 0.9 convert_reduce_fusion.1
  0.9 0.7 fusion.3
  1.6 0.7 broadcast_add_fusion.1
  2.2 0.1 select_reduce_fusion.1
  2.3 0.8 sub.7
  3.1 16.3 %all-to-all-start = ((s32[64,1,2]{2,1,0:T(1,128)}), s32[64,1,2]{2,1,0:T(1,128)S(1)}, u32[]{:S(2)}, u32[]{:S(2)}) async-start(s32[64,1,2]{2,1,0:T(1,128)} %bitcast.3), calls=%async_computation | async-start | bytes 65536 | tf_op jit(solution)/shard_map/all_to_all | solution.py:214
  19.4 0.7 multiply_add_fusion.slot_of_ref
  20.1 0.8 dynamic-slice_convert_fusion
  20.9 5.7 %all-to-all-done = s32[64,1,2]{2,1,0:T(1,128)S(1)} async-done(((s32[64,1,2]{2,1,0:T(1,128)}), s32[64,1,2]{2,1,0:T(1,128)S(1)}, u32[]{:S(2)}, u32[]{:S(2)}) %all-to-all-start) | async-done | bytes 544 | tf_op jit(solution)/shard_map/all_to_all | solution.py:214
  26.6 0.5 broadcast.38
  27.1 0.7 reduce.3
  27.8 0.1 reshape.48.wanted_ref
  27.9 0.0 copy-start.3
  28.0 0.1 broadcast_in_dim.50.degree_ref
  28.0 0.6 convert_reduce_fusion.2
  28.7 0.1 convert_reduce_fusion
  28.8 0.7 select_reduce_fusion.order_ref
  29.4 0.0 copy-done.3
  29.4 3.5 %shard_map.73 = bf16[128,128,128]{2,1,0:T(8,128)(2,1)} custom-call(s32[1]{0:T(128)} %bitcast.4.count_ref, s32[128]{0:T(128)} %select_reduce_fusion.order_ref, s32[128]{0:T(128)} %copy-done.3, bf16[16,128,128]{2,1,0:T(8,128)(2,1)} %bitcast.20), custom_call_target="tpu_custom_call" | custom-call | tf_op jit(solution)/shard_map/pallas_call | solution.py:136
  32.9 0.0 copy-start
  32.9 0.0 copy-start.1
  32.9 0.0 copy-start.2
  33.0 111.9 %all_to_all.16 = bf16[64,2,128,128]{3,2,1,0:T(8,128)(2,1)} all-to-all(bf16[64,2,128,128]{3,2,1,0:T(8,128)(2,1)} %bitcast.19), channel_id=1, replica_groups=mesh['wide'=64,'narrow'=8] {'wide'}, dimensions={0} | all-to-all | bytes 8388608 | tf_op jit(solution)/shard_map/all_to_all | solution.py:232
  144.9 0.0 copy-done
  144.9 0.0 copy-done.1
  144.9 0.0 copy-done.2
  144.9 21.9 %shard_map.74 = bf16[128,128,128]{2,1,0:T(8,128)(2,1)S(1)} custom-call(s32[16]{0:T(128)S(1)} %multiply_add_fusion.slot_of_ref, s32[128]{0:T(128)S(1)} %get-tuple-element.11.slot_tile_ref, bf16[128,128,128]{2,1,0:T(8,128)(2,1)} %bitcast.17, bf16[16,128,128]{2,1,0:T(8,128)(2,1)S(1)} %copy-done, f32[128,128]{1,0:T(8,128)S(1)} %broadcast_in_dim.50.degree_ref, ...), custom_call_target="tpu_custom_call" | custom-call | tf_op jit(solution)/shard_map/pallas_call | solution.py:93
  166.8 122.6 %all_to_all.17 = bf16[64,2,128,128]{3,2,1,0:T(8,128)(2,1)} all-to-all(bf16[64,2,128,128]{3,2,1,0:T(8,128)(2,1)S(1)} %bitcast.16), channel_id=1, replica_groups=mesh['wide'=64,'narrow'=8] {'wide'}, dimensions={0} | all-to-all | bytes 8388608 | tf_op jit(solution)/shard_map/all_to_all | solution.py:250
  289.4 4.5 %shard_map.75 = bf16[16,128,128]{2,1,0:T(8,128)(2,1)} custom-call(s32[1]{0:T(128)} %bitcast.4.count_ref, s32[128]{0:T(128)} %select_reduce_fusion.order_ref, s32[128]{0:T(128)} %copy-done.3, bf16[128,128,128]{2,1,0:T(8,128)(2,1)} %bitcast.18, bf16[16,128,128]{2,1,0:T(8,128)(2,1)} %bitcast.21), custom_call_target="tpu_custom_call" | custom-call | tf_op jit(solution)/shard_map/pallas_call | solution.py:171
  (2 shorter events, 0.0 us)
Async XLA Ops:
  3.1 23.5 %all-to-all-start = ((s32[64,1,2]{2,1,0:T(1,128)}), s32[64,1,2]{2,1,0:T(1,128)S(1)}, u32[]{:S(2)}, u32[]{:S(2)}) async-start(s32[64,1,2]{2,1,0:T(1,128)} %bitcast.3), calls=%async_computation | async-start | bytes 65536 | tf_op jit(solution)/shard_map/all_to_all | solution.py:214
  27.9 1.5 copy-start.3
  32.9 111.9 %copy-start = (bf16[16,128,128]{2,1,0:T(8,128)(2,1)S(1)}, bf16[16,128,128]{2,1,0:T(8,128)(2,1)}, u32[]{:S(2)}) copy-start(bf16[16,128,128]{2,1,0:T(8,128)(2,1)} %tiles_ref.1) | copy-start | bytes 1572868
  32.9 111.9 %copy-start.1 = (bf16[128,512]{1,0:T(8,128)(2,1)S(1)}, bf16[128,512]{1,0:T(8,128)(2,1)}, u32[]{:S(2)}) copy-start(bf16[128,512]{1,0:T(8,128)(2,1)} %w_in_ref.1) | copy-start | bytes 393220
  32.9 111.9 %copy-start.2 = (bf16[512,128]{1,0:T(8,128)(2,1)S(1)}, bf16[512,128]{1,0:T(8,128)(2,1)}, u32[]{:S(2)}) copy-start(bf16[512,128]{1,0:T(8,128)(2,1)} %w_out_ref.1) | copy-start | bytes 393220

commit v15 on v14

--- a/solution.py
+++ b/solution.py
@@ -114,7 +114,8 @@
 
     def copy(i):
         slot = order_ref[i]
-        block = jnp.clip(wanted_ref[slot], 0, last)
+        cap = wanted_ref.shape[2]
+        block = jnp.clip(wanted_ref[slot // cap, 0, slot % cap], 0, last)
         return pltpu.make_async_copy(rows_ref.at[block], out_ref.at[slot], sems.at[i])
 
     def start(i, carry):
@@ -130,7 +131,7 @@
 
 
 def pick_rows(count, order, wanted, blocks):
-    slots = wanted.shape[0]
+    slots = wanted.shape[0] * wanted.shape[2]
     _, rows, channels = blocks.shape
     smem = pl.BlockSpec(memory_space=pltpu.SMEM)
     return pl.pallas_call(
@@ -157,7 +158,9 @@
 
     def add(i, carry):
         copy(i).wait()
-        block = jnp.clip(wanted_ref[order_ref[i]], 0, last)
+        slot = order_ref[i]
+        cap = wanted_ref.shape[2]
+        block = jnp.clip(wanted_ref[slot // cap, 0, slot % cap], 0, last)
         acc[block] = acc[block] + buf[i].astype(jnp.float32)
         return carry
 
@@ -211,16 +214,16 @@
     own_rows = edge_row_count // groups
     own_degree = lax.dynamic_slice_in_dim(edge_degree, me * own_rows, own_rows)
     tile_of_slot = jnp.sum(jnp.where(matches, positions[:, None], 0), axis=0)
-    wanted = lax.all_to_all(
-        wanted_out.reshape(owners, capacity), "wide", split_axis=0, concat_axis=0, tiled=True
-    ).reshape(slot_count)
+    asked = lax.all_to_all(
+        wanted_out.reshape(owners, 1, capacity), "wide", split_axis=0, concat_axis=0, tiled=True
+    )
     current = node_rows
     node_blocks = current.reshape(node_block_count, block_size, channels)
     degree_column = jnp.broadcast_to(own_degree.astype(jnp.float32)[:, None], (own_rows, channels))
-    wanted, slot_of, tile_of_slot, degree_column = lax.optimization_barrier(
-        (wanted, slot_of, tile_of_slot, degree_column)
-    )
-    filled = wanted >= 0
+    asked, slot_of, tile_of_slot, degree_column = lax.optimization_barrier(
+        (asked, slot_of, tile_of_slot, degree_column)
+    )
+    filled = asked.reshape(slot_count) >= 0
     before = filled[None, :] & (slot_ids[None, :] < slot_ids[:, None])
     rank = jnp.sum(before.astype(jnp.int32), axis=1)
     count = jnp.sum(filled.astype(jnp.int32)).reshape(1)
@@ -228,7 +231,7 @@
         jnp.where(filled[None, :] & (rank[None, :] == slot_ids[:, None]), slot_ids[None, :], 0),
         axis=1,
     )
-    picked = pick_rows(count, order, wanted, node_blocks)
+    picked = pick_rows(count, order, asked, node_blocks)
     arrived = lax.all_to_all(
         picked.reshape(owners, capacity, block_size, channels),
         "wide",
@@ -255,7 +258,7 @@
         tiled=True,
     )
     current = land_terms(
-        count, order, wanted, returned.reshape(slot_count, block_size, channels), node_blocks
+        count, order, asked, returned.reshape(slot_count, block_size, channels), node_blocks
     ).reshape(node_block_count * block_size, channels)
     return current
 

time: 294 us -> 293 us (level)
  the two profiles are of different devices: /device:TPU:32 before, /device:TPU:152 now
where the time goes in v15:
time: 293 us
  blocking collectives  234 us (80%)
  Pallas kernels  31.4 us (11%)
  starting transfers between devices  14.6 us (5%)
  waiting for transfers between devices  6.05 us (2%)
  other arithmetic  5.33 us (2%)
    all_to_all x1, blocking collectives, body(): lax.all_to_all(outgoing.reshape(owners, capacity, block_size, channels),...  124 us
    all_to_all x1, blocking collectives, body(): lax.all_to_all(picked.reshape(owners, capacity, block_size, channels), 'w...  111 us
    pallas_call x1, Pallas kernels, round_kernel(): pl.pallas_call(functools.partial(_round_kernel, groups, per_block), out_s...  23 us
    all_to_all x1, starting transfers between devices, body(): lax.all_to_all(wanted_out.reshape(owners, 1, capacity), 'wide', split_axi...  14.6 us
    all_to_all x1, waiting for transfers between devices, body(): lax.all_to_all(wanted_out.reshape(owners, 1, capacity), 'wide', split_axi...  6.05 us
  transfers between devices with their start and end apart: 1, of which 1 were waited for; matrix products, arithmetic and copies ran while one was open for 0% of the time, Pallas kernels for 0%

profile of v15, /device:TPU:152, one launch (start us, length us, event | category | flops | bytes accessed | tf_op | source)
XLA Modules:
  0.0 292.9 jit_solution(14717396544552493251)
XLA Ops:
  0.0 0.9 convert_reduce_fusion.1
  0.9 0.7 fusion.4
  1.6 0.7 broadcast_add_fusion.1
  2.2 0.1 select_reduce_fusion.1
  2.3 0.8 sub.7
  3.1 14.6 %all-to-all-start = ((s32[64,1,2]{2,1,0:T(1,128)}), s32[64,1,2]{2,1,0:T(1,128)S(1)}, u32[]{:S(2)}, u32[]{:S(2)}) async-start(s32[64,1,2]{2,1,0:T(1,128)} %bitcast.3), calls=%async_computation | async-start | bytes 65536 | tf_op jit(solution)/shard_map/all_to_all | solution.py:217
  17.7 0.7 multiply_add_fusion.slot_of_ref
  18.4 0.8 dynamic-slice_convert_fusion
  19.1 6.0 %all-to-all-done.wanted_ref = s32[64,1,2]{2,1,0:T(1,128)S(1)} async-done(((s32[64,1,2]{2,1,0:T(1,128)}), s32[64,1,2]{2,1,0:T(1,128)S(1)}, u32[]{:S(2)}, u32[]{:S(2)}) %all-to-all-start) | async-done | bytes 544 | tf_op jit(solution)/shard_map/all_to_all | solution.py:217
  25.2 0.0 copy-start.3
  25.2 0.1 broadcast_in_dim.50.degree_ref
  25.2 0.7 fusion.2
  26.0 0.1 compare_reduce_fusion
  26.1 0.1 ge.16
  26.2 0.1 convert_reduce_fusion
  26.3 0.7 select_reduce_fusion.order_ref
  27.0 0.0 copy-done.3
  27.0 3.7 %shard_map.73 = bf16[128,128,128]{2,1,0:T(8,128)(2,1)} custom-call(s32[1]{0:T(128)} %bitcast.4.count_ref, s32[128]{0:T(128)} %select_reduce_fusion.order_ref, s32[64,1,2]{2,1,0:T(1,128)} %copy-done.3, bf16[16,128,128]{2,1,0:T(8,128)(2,1)} %bitcast.20), custom_call_target="tpu_custom_call" | custom-call | tf_op jit(solution)/shard_map/pallas_call | solution.py:137
  30.7 0.0 copy-start
  30.7 0.0 copy-start.1
  30.7 0.0 copy-start.2
  30.7 110.7 %all_to_all.15 = bf16[64,2,128,128]{3,2,1,0:T(8,128)(2,1)} all-to-all(bf16[64,2,128,128]{3,2,1,0:T(8,128)(2,1)} %bitcast.19), channel_id=1, replica_groups=mesh['wide'=64,'narrow'=8] {'wide'}, dimensions={0} | all-to-all | bytes 8388608 | tf_op jit(solution)/shard_map/all_to_all | solution.py:235
  141.4 0.0 copy-done
  141.4 0.0 copy-done.1
  141.4 0.0 copy-done.2
  141.4 23.0 %shard_map.74 = bf16[128,128,128]{2,1,0:T(8,128)(2,1)S(1)} custom-call(s32[16]{0:T(128)S(1)} %multiply_add_fusion.slot_of_ref, s32[128]{0:T(128)S(1)} %get-tuple-element.11.slot_tile_ref, bf16[128,128,128]{2,1,0:T(8,128)(2,1)} %bitcast.17, bf16[16,128,128]{2,1,0:T(8,128)(2,1)S(1)} %copy-done, f32[128,128]{1,0:T(8,128)S(1)} %broadcast_in_dim.50.degree_ref, ...), custom_call_target="tpu_custom_call" | custom-call | tf_op jit(solution)/shard_map/pallas_call | solution.py:93
  164.4 123.8 %all_to_all.16 = bf16[64,2,128,128]{3,2,1,0:T(8,128)(2,1)} all-to-all(bf16[64,2,128,128]{3,2,1,0:T(8,128)(2,1)S(1)} %bitcast.16), channel_id=1, replica_groups=mesh['wide'=64,'narrow'=8] {'wide'}, dimensions={0} | all-to-all | bytes 8388608 | tf_op jit(solution)/shard_map/all_to_all | solution.py:253
  288.2 4.7 %shard_map.75 = bf16[16,128,128]{2,1,0:T(8,128)(2,1)} custom-call(s32[1]{0:T(128)} %bitcast.4.count_ref, s32[128]{0:T(128)} %select_reduce_fusion.order_ref, s32[64,1,2]{2,1,0:T(1,128)} %copy-done.3, bf16[128,128,128]{2,1,0:T(8,128)(2,1)} %bitcast.18, bf16[16,128,128]{2,1,0:T(8,128)(2,1)} %bitcast.21), custom_call_target="tpu_custom_call" | custom-call | tf_op jit(solution)/shard_map/pallas_call | solution.py:174
  (1 shorter events, 0.0 us)
Async XLA Ops:
  3.1 22.1 %all-to-all-start = ((s32[64,1,2]{2,1,0:T(1,128)}), s32[64,1,2]{2,1,0:T(1,128)S(1)}, u32[]{:S(2)}, u32[]{:S(2)}) async-start(s32[64,1,2]{2,1,0:T(1,128)} %bitcast.3), calls=%async_computation | async-start | bytes 65536 | tf_op jit(solution)/shard_map/all_to_all | solution.py:217
  25.2 1.8 copy-start.3
  30.7 110.8 %copy-start = (bf16[16,128,128]{2,1,0:T(8,128)(2,1)S(1)}, bf16[16,128,128]{2,1,0:T(8,128)(2,1)}, u32[]{:S(2)}) copy-start(bf16[16,128,128]{2,1,0:T(8,128)(2,1)} %tiles_ref.1) | copy-start | bytes 1572868
  30.7 110.8 %copy-start.1 = (bf16[128,512]{1,0:T(8,128)(2,1)S(1)}, bf16[128,512]{1,0:T(8,128)(2,1)}, u32[]{:S(2)}) copy-start(bf16[128,512]{1,0:T(8,128)(2,1)} %w_in_ref.1) | copy-start | bytes 393220
  30.7 110.8 %copy-start.2 = (bf16[512,128]{1,0:T(8,128)(2,1)S(1)}, bf16[512,128]{1,0:T(8,128)(2,1)}, u32[]{:S(2)}) copy-start(bf16[512,128]{1,0:T(8,128)(2,1)} %w_out_ref.1) | copy-start | bytes 393220

commit v16 on v15

--- a/solution.py
+++ b/solution.py
@@ -137,7 +137,7 @@
     return pl.pallas_call(
         _pick_kernel,
         out_shape=jax.ShapeDtypeStruct((slots, rows, channels), blocks.dtype),
-        in_specs=[smem, smem, smem, pl.BlockSpec(memory_space=pltpu.VMEM)],
+        in_specs=[smem, smem, smem, pl.BlockSpec(memory_space=pltpu.HBM)],
         out_specs=pl.BlockSpec(memory_space=pl.ANY),
         scratch_shapes=[pltpu.SemaphoreType.DMA((slots,))],
     )(count, order, wanted, blocks)

time: 293 us -> 417 us (1.42)
  the two profiles are of different devices: /device:TPU:152 before, /device:TPU:32 now
where the time goes in v16:
time: 417 us
  blocking collectives  343 us (82%)
  Pallas kernels  45.7 us (11%)
  starting transfers between devices  16.3 us (4%)
  waiting for transfers between devices  5.7 us (1%)
  other arithmetic  5.33 us (1%)
    all_to_all x1, blocking collectives, body(): lax.all_to_all(picked.reshape(owners, capacity, block_size, channels), 'w...  222 us
    all_to_all x1, blocking collectives, body(): lax.all_to_all(outgoing.reshape(owners, capacity, block_size, channels),...  121 us
    pallas_call x1, Pallas kernels, round_kernel(): pl.pallas_call(functools.partial(_round_kernel, groups, per_block), out_s...  20.9 us
    pallas_call x1, Pallas kernels, pick_rows(): pl.pallas_call(_pick_kernel, out_shape=jax.ShapeDtypeStruct((slots, rows,...  19.9 us
    all_to_all x1, starting transfers between devices, body(): lax.all_to_all(wanted_out.reshape(owners, 1, capacity), 'wide', split_axi...  16.3 us
  transfers between devices with their start and end apart: 1, of which 1 were waited for; matrix products, arithmetic and copies ran while one was open for 0% of the time, Pallas kernels for 0%

profile of v16, /device:TPU:32, one launch (start us, length us, event | category | flops | bytes accessed | tf_op | source)
XLA Modules:
  0.0 416.7 jit_solution(15143466602660066334)
XLA Ops:
  0.0 0.9 convert_reduce_fusion.1
  0.9 0.7 fusion.4
  1.6 0.7 broadcast_add_fusion.1
  2.2 0.1 select_reduce_fusion.1
  2.3 0.8 sub.7
  3.1 16.3 %all-to-all-start = ((s32[64,1,2]{2,1,0:T(1,128)}), s32[64,1,2]{2,1,0:T(1,128)S(1)}, u32[]{:S(2)}, u32[]{:S(2)}) async-start(s32[64,1,2]{2,1,0:T(1,128)} %bitcast.3), calls=%async_computation | async-start | bytes 65536 | tf_op jit(solution)/shard_map/all_to_all | solution.py:217
  19.4 0.7 multiply_add_fusion.slot_of_ref
  20.1 0.8 dynamic-slice_convert_fusion
  20.9 5.7 %all-to-all-done.wanted_ref = s32[64,1,2]{2,1,0:T(1,128)S(1)} async-done(((s32[64,1,2]{2,1,0:T(1,128)}), s32[64,1,2]{2,1,0:T(1,128)S(1)}, u32[]{:S(2)}, u32[]{:S(2)}) %all-to-all-start) | async-done | bytes 544 | tf_op jit(solution)/shard_map/all_to_all | solution.py:217
  26.6 0.0 copy-start.3
  26.6 0.1 broadcast_in_dim.50.degree_ref
  26.6 0.7 fusion.2
  27.4 0.1 compare_reduce_fusion
  27.5 0.1 ge.16
  27.6 0.1 convert_reduce_fusion
  27.7 0.7 select_reduce_fusion.order_ref
  28.4 0.0 copy-done.3
  28.4 19.9 %shard_map.73 = bf16[128,128,128]{2,1,0:T(8,128)(2,1)} custom-call(s32[1]{0:T(128)} %bitcast.4.count_ref, s32[128]{0:T(128)} %select_reduce_fusion.order_ref, s32[64,1,2]{2,1,0:T(1,128)} %copy-done.3, bf16[16,128,128]{2,1,0:T(8,128)(2,1)} %bitcast.20), custom_call_target="tpu_custom_call" | custom-call | tf_op jit(solution)/shard_map/pallas_call | solution.py:137
  48.3 0.0 copy-start
  48.3 0.0 copy-start.1
  48.3 0.0 copy-start.2
  48.4 222.0 %all_to_all.15 = bf16[64,2,128,128]{3,2,1,0:T(8,128)(2,1)} all-to-all(bf16[64,2,128,128]{3,2,1,0:T(8,128)(2,1)} %bitcast.19), channel_id=1, replica_groups=mesh['wide'=64,'narrow'=8] {'wide'}, dimensions={0} | all-to-all | bytes 8388608 | tf_op jit(solution)/shard_map/all_to_all | solution.py:235
  270.3 0.0 copy-done
  270.3 0.0 copy-done.1
  270.3 0.0 copy-done.2
  270.3 20.9 %shard_map.74 = bf16[128,128,128]{2,1,0:T(8,128)(2,1)S(1)} custom-call(s32[16]{0:T(128)S(1)} %multiply_add_fusion.slot_of_ref, s32[128]{0:T(128)S(1)} %get-tuple-element.11.slot_tile_ref, bf16[128,128,128]{2,1,0:T(8,128)(2,1)} %bitcast.17, bf16[16,128,128]{2,1,0:T(8,128)(2,1)S(1)} %copy-done, f32[128,128]{1,0:T(8,128)S(1)} %broadcast_in_dim.50.degree_ref, ...), custom_call_target="tpu_custom_call" | custom-call | tf_op jit(solution)/shard_map/pallas_call | solution.py:93
  291.2 120.6 %all_to_all.16 = bf16[64,2,128,128]{3,2,1,0:T(8,128)(2,1)} all-to-all(bf16[64,2,128,128]{3,2,1,0:T(8,128)(2,1)S(1)} %bitcast.16), channel_id=1, replica_groups=mesh['wide'=64,'narrow'=8] {'wide'}, dimensions={0} | all-to-all | bytes 8388608 | tf_op jit(solution)/shard_map/all_to_all | solution.py:253
  411.8 4.9 %shard_map.75 = bf16[16,128,128]{2,1,0:T(8,128)(2,1)} custom-call(s32[1]{0:T(128)} %bitcast.4.count_ref, s32[128]{0:T(128)} %select_reduce_fusion.order_ref, s32[64,1,2]{2,1,0:T(1,128)} %copy-done.3, bf16[128,128,128]{2,1,0:T(8,128)(2,1)} %bitcast.18, bf16[16,128,128]{2,1,0:T(8,128)(2,1)} %bitcast.21), custom_call_target="tpu_custom_call" | custom-call | tf_op jit(solution)/shard_map/pallas_call | solution.py:174
  (1 shorter events, 0.0 us)
Async XLA Ops:
  3.1 23.5 %all-to-all-start = ((s32[64,1,2]{2,1,0:T(1,128)}), s32[64,1,2]{2,1,0:T(1,128)S(1)}, u32[]{:S(2)}, u32[]{:S(2)}) async-start(s32[64,1,2]{2,1,0:T(1,128)} %bitcast.3), calls=%async_computation | async-start | bytes 65536 | tf_op jit(solution)/shard_map/all_to_all | solution.py:217
  26.6 1.8 copy-start.3
  48.3 222.0 %copy-start = (bf16[16,128,128]{2,1,0:T(8,128)(2,1)S(1)}, bf16[16,128,128]{2,1,0:T(8,128)(2,1)}, u32[]{:S(2)}) copy-start(bf16[16,128,128]{2,1,0:T(8,128)(2,1)} %tiles_ref.1) | copy-start | bytes 1572868
  48.3 222.0 %copy-start.1 = (bf16[128,512]{1,0:T(8,128)(2,1)S(1)}, bf16[128,512]{1,0:T(8,128)(2,1)}, u32[]{:S(2)}) copy-start(bf16[128,512]{1,0:T(8,128)(2,1)} %w_in_ref.1) | copy-start | bytes 393220
  48.3 222.0 %copy-start.2 = (bf16[512,128]{1,0:T(8,128)(2,1)S(1)}, bf16[512,128]{1,0:T(8,128)(2,1)}, u32[]{:S(2)}) copy-start(bf16[512,128]{1,0:T(8,128)(2,1)} %w_out_ref.1) | copy-start | bytes 393220

commit v17 on v15

--- a/solution.py
+++ b/solution.py
@@ -143,7 +143,8 @@
     )(count, order, wanted, blocks)
 
 
-def _land_kernel(count_ref, order_ref, wanted_ref, returned_ref, rows_ref, out_ref, buf, acc, sems):
+def _land_kernel(count_ref, order_ref, wanted_ref, returned_ref, rows_hbm, out_ref, buf, acc, sems,
+                 rows_ref, rows_sem):
     last = rows_ref.shape[0] - 1
 
     def copy(i):
@@ -153,7 +154,10 @@
         copy(i).start()
         return carry
 
+    rows_in = pltpu.make_async_copy(rows_hbm, rows_ref, rows_sem)
+    rows_in.start()
     lax.fori_loop(0, count_ref[0], start, 0)
+    rows_in.wait()
     acc[...] = rows_ref[...].astype(jnp.float32)
 
     def add(i, carry):
@@ -174,12 +178,14 @@
     return pl.pallas_call(
         _land_kernel,
         out_shape=jax.ShapeDtypeStruct(blocks.shape, blocks.dtype),
-        in_specs=[smem, smem, smem, pl.BlockSpec(memory_space=pl.ANY), pl.BlockSpec(memory_space=pltpu.VMEM)],
+        in_specs=[smem, smem, smem, pl.BlockSpec(memory_space=pl.ANY), pl.BlockSpec(memory_space=pl.ANY)],
         out_specs=pl.BlockSpec(memory_space=pltpu.VMEM),
         scratch_shapes=[
             pltpu.VMEM((slots, rows, channels), returned.dtype),
             pltpu.VMEM(blocks.shape, jnp.float32),
             pltpu.SemaphoreType.DMA((slots,)),
+            pltpu.VMEM(blocks.shape, blocks.dtype),
+            pltpu.SemaphoreType.DMA,
         ],
     )(count, order, wanted, returned, blocks)
 

time: 293 us -> 295 us (level)
  the two profiles are of different devices: /device:TPU:152 before, /device:TPU:88 now
where the time goes in v17:
time: 295 us; the launch traced here: 294 us
  blocking collectives  230 us (78%)
  Pallas kernels  35.5 us (12%)
  starting transfers between devices  15.5 us (5%)
  waiting for transfers between devices  6.92 us (2%)
  other arithmetic  5.33 us (2%)
    all_to_all x1, blocking collectives, body(): lax.all_to_all(outgoing.reshape(owners, capacity, block_size, channels),...  124 us
    all_to_all x1, blocking collectives, body(): lax.all_to_all(picked.reshape(owners, capacity, block_size, channels), 'w...  106 us
    pallas_call x1, Pallas kernels, round_kernel(): pl.pallas_call(functools.partial(_round_kernel, groups, per_block), out_s...  21.4 us
    all_to_all x1, starting transfers between devices, body(): lax.all_to_all(wanted_out.reshape(owners, 1, capacity), 'wide', split_axi...  15.5 us
    pallas_call x1, Pallas kernels, land_terms(): pl.pallas_call(_land_kernel, out_shape=jax.ShapeDtypeStruct(blocks.shape,...  8.05 us
    all_to_all x1, waiting for transfers between devices, body(): lax.all_to_all(wanted_out.reshape(owners, 1, capacity), 'wide', split_axi...  6.92 us
    pallas_call x1, Pallas kernels, pick_rows(): pl.pallas_call(_pick_kernel, out_shape=jax.ShapeDtypeStruct((slots, rows,...  6.1 us
  transfers between devices with their start and end apart: 1, of which 1 were waited for; matrix products, arithmetic and copies ran while one was open for 0% of the time, Pallas kernels for 0%

profile of v17, /device:TPU:88, one launch (start us, length us, event | category | flops | bytes accessed | tf_op | source)
XLA Modules:
  0.0 294.4 jit_solution(2142290995899559016)
XLA Ops:
  0.0 0.9 convert_reduce_fusion.1
  0.9 0.7 fusion.4
  1.6 0.7 broadcast_add_fusion.1
  2.2 0.1 select_reduce_fusion.1
  2.3 0.8 sub.7
  3.1 15.5 %all-to-all-start = ((s32[64,1,2]{2,1,0:T(1,128)}), s32[64,1,2]{2,1,0:T(1,128)S(1)}, u32[]{:S(2)}, u32[]{:S(2)}) async-start(s32[64,1,2]{2,1,0:T(1,128)} %bitcast.3), calls=%async_computation | async-start | bytes 65536 | tf_op jit(solution)/shard_map/all_to_all | solution.py:223
  18.6 0.7 multiply_add_fusion.slot_of_ref
  19.3 0.8 dynamic-slice_convert_fusion
  20.0 6.9 %all-to-all-done.wanted_ref = s32[64,1,2]{2,1,0:T(1,128)S(1)} async-done(((s32[64,1,2]{2,1,0:T(1,128)}), s32[64,1,2]{2,1,0:T(1,128)S(1)}, u32[]{:S(2)}, u32[]{:S(2)}) %all-to-all-start) | async-done | bytes 544 | tf_op jit(solution)/shard_map/all_to_all | solution.py:223
  26.9 0.0 copy-start.3
  26.9 0.1 broadcast_in_dim.50.degree_ref
  27.0 0.7 fusion.2
  27.7 0.1 compare_reduce_fusion
  27.8 0.1 ge.16
  28.0 0.1 convert_reduce_fusion
  28.1 0.7 select_reduce_fusion.order_ref
  28.7 0.0 copy-done.3
  28.7 6.1 %shard_map.73 = bf16[128,128,128]{2,1,0:T(8,128)(2,1)} custom-call(s32[1]{0:T(128)} %bitcast.4.count_ref, s32[128]{0:T(128)} %select_reduce_fusion.order_ref, s32[64,1,2]{2,1,0:T(1,128)} %copy-done.3, bf16[16,128,128]{2,1,0:T(8,128)(2,1)} %bitcast.20), custom_call_target="tpu_custom_call" | custom-call | tf_op jit(solution)/shard_map/pallas_call | solution.py:137
  34.9 0.0 copy-start
  34.9 0.0 copy-start.1
  34.9 0.0 copy-start.2
  34.9 106.2 %all_to_all.15 = bf16[64,2,128,128]{3,2,1,0:T(8,128)(2,1)} all-to-all(bf16[64,2,128,128]{3,2,1,0:T(8,128)(2,1)} %bitcast.19), channel_id=1, replica_groups=mesh['wide'=64,'narrow'=8] {'wide'}, dimensions={0} | all-to-all | bytes 8388608 | tf_op jit(solution)/shard_map/all_to_all | solution.py:241
  141.1 0.0 copy-done
  141.1 0.0 copy-done.1
  141.1 0.0 copy-done.2
  141.2 21.4 %shard_map.74 = bf16[128,128,128]{2,1,0:T(8,128)(2,1)S(1)} custom-call(s32[16]{0:T(128)S(1)} %multiply_add_fusion.slot_of_ref, s32[128]{0:T(128)S(1)} %get-tuple-element.11.slot_tile_ref, bf16[128,128,128]{2,1,0:T(8,128)(2,1)} %bitcast.17, bf16[16,128,128]{2,1,0:T(8,128)(2,1)S(1)} %copy-done, f32[128,128]{1,0:T(8,128)S(1)} %broadcast_in_dim.50.degree_ref, ...), custom_call_target="tpu_custom_call" | custom-call | tf_op jit(solution)/shard_map/pallas_call | solution.py:93
  162.5 123.9 %all_to_all.16 = bf16[64,2,128,128]{3,2,1,0:T(8,128)(2,1)} all-to-all(bf16[64,2,128,128]{3,2,1,0:T(8,128)(2,1)S(1)} %bitcast.16), channel_id=1, replica_groups=mesh['wide'=64,'narrow'=8] {'wide'}, dimensions={0} | all-to-all | bytes 8388608 | tf_op jit(solution)/shard_map/all_to_all | solution.py:259
  286.4 8.0 %shard_map.75 = bf16[16,128,128]{2,1,0:T(8,128)(2,1)} custom-call(s32[1]{0:T(128)} %bitcast.4.count_ref, s32[128]{0:T(128)} %select_reduce_fusion.order_ref, s32[64,1,2]{2,1,0:T(1,128)} %copy-done.3, bf16[128,128,128]{2,1,0:T(8,128)(2,1)} %bitcast.18, bf16[16,128,128]{2,1,0:T(8,128)(2,1)} %bitcast.21), custom_call_target="tpu_custom_call" | custom-call | tf_op jit(solution)/shard_map/pallas_call | solution.py:178
  (1 shorter events, 0.0 us)
Async XLA Ops:
  3.1 23.8 %all-to-all-start = ((s32[64,1,2]{2,1,0:T(1,128)}), s32[64,1,2]{2,1,0:T(1,128)S(1)}, u32[]{:S(2)}, u32[]{:S(2)}) async-start(s32[64,1,2]{2,1,0:T(1,128)} %bitcast.3), calls=%async_computation | async-start | bytes 65536 | tf_op jit(solution)/shard_map/all_to_all | solution.py:223
  26.9 1.8 copy-start.3
  34.9 106.3 %copy-start = (bf16[16,128,128]{2,1,0:T(8,128)(2,1)S(1)}, bf16[16,128,128]{2,1,0:T(8,128)(2,1)}, u32[]{:S(2)}) copy-start(bf16[16,128,128]{2,1,0:T(8,128)(2,1)} %tiles_ref.1) | copy-start | bytes 1572868
  34.9 106.3 %copy-start.1 = (bf16[128,512]{1,0:T(8,128)(2,1)S(1)}, bf16[128,512]{1,0:T(8,128)(2,1)}, u32[]{:S(2)}) copy-start(bf16[128,512]{1,0:T(8,128)(2,1)} %w_in_ref.1) | copy-start | bytes 393220
  34.9 106.3 %copy-start.2 = (bf16[512,128]{1,0:T(8,128)(2,1)S(1)}, bf16[512,128]{1,0:T(8,128)(2,1)}, u32[]{:S(2)}) copy-start(bf16[512,128]{1,0:T(8,128)(2,1)} %w_out_ref.1) | copy-start | bytes 393220

commit v18 on v15

--- a/solution.py
+++ b/solution.py
@@ -105,7 +105,7 @@
             pltpu.SemaphoreType.DMA((groups,)), pltpu.SemaphoreType.DMA((groups,)),
         ],
         compiler_params=pltpu.CompilerParams(
-            collective_id=0, has_side_effects=True, vmem_limit_bytes=48 * 1024 * 1024),
+            collective_id=0, has_side_effects=True, vmem_limit_bytes=24 * 1024 * 1024),
     )(slot_of, slot_tile, arrived, tiles, degree, w_in, w_out)
 
 

time: 293 us -> 289 us (0.986)
  the two profiles are of different devices: /device:TPU:152 before, /device:TPU:32 now
where the time goes in v18:
time: 289 us
  blocking collectives  232 us (80%)
  Pallas kernels  27.9 us (10%)
  starting transfers between devices  16.3 us (6%)
  waiting for transfers between devices  5.7 us (2%)
  other arithmetic  5.38 us (2%)
    all_to_all x1, blocking collectives, body(): lax.all_to_all(outgoing.reshape(owners, capacity, block_size, channels),...  122 us
    all_to_all x1, blocking collectives, body(): lax.all_to_all(picked.reshape(owners, capacity, block_size, channels), 'w...  111 us
    pallas_call x1, Pallas kernels, round_kernel(): pl.pallas_call(functools.partial(_round_kernel, groups, per_block), out_s...  19.2 us
    all_to_all x1, starting transfers between devices, body(): lax.all_to_all(wanted_out.reshape(owners, 1, capacity), 'wide', split_axi...  16.3 us
  transfers between devices with their start and end apart: 1, of which 1 were waited for; matrix products, arithmetic and copies ran while one was open for 0% of the time, Pallas kernels for 0%

profile of v18, /device:TPU:32, one launch (start us, length us, event | category | flops | bytes accessed | tf_op | source)
XLA Modules:
  0.0 288.8 jit_solution(3930785995318088859)
XLA Ops:
  0.0 0.9 convert_reduce_fusion.1
  0.9 0.7 fusion.4
  1.6 0.7 broadcast_add_fusion.1
  2.2 0.1 select_reduce_fusion.1
  2.3 0.8 sub.7
  3.1 16.3 %all-to-all-start = ((s32[64,1,2]{2,1,0:T(1,128)}), s32[64,1,2]{2,1,0:T(1,128)S(1)}, u32[]{:S(2)}, u32[]{:S(2)}) async-start(s32[64,1,2]{2,1,0:T(1,128)} %bitcast.3), calls=%async_computation | async-start | bytes 65536 | tf_op jit(solution)/shard_map/all_to_all | solution.py:217
  19.4 0.7 multiply_add_fusion.slot_of_ref
  20.1 0.8 dynamic-slice_convert_fusion
  20.9 5.7 %all-to-all-done.wanted_ref = s32[64,1,2]{2,1,0:T(1,128)S(1)} async-done(((s32[64,1,2]{2,1,0:T(1,128)}), s32[64,1,2]{2,1,0:T(1,128)S(1)}, u32[]{:S(2)}, u32[]{:S(2)}) %all-to-all-start) | async-done | bytes 544 | tf_op jit(solution)/shard_map/all_to_all | solution.py:217
  26.6 0.0 copy-start.3
  26.6 0.1 broadcast_in_dim.50.degree_ref
  26.6 0.8 fusion.2
  27.4 0.1 compare_reduce_fusion
  27.5 0.1 ge.16
  27.7 0.1 convert_reduce_fusion
  27.8 0.6 select_reduce_fusion.order_ref
  28.4 0.0 copy-done.3
  28.4 3.8 %shard_map.73 = bf16[128,128,128]{2,1,0:T(8,128)(2,1)} custom-call(s32[1]{0:T(128)} %bitcast.4.count_ref, s32[128]{0:T(128)} %select_reduce_fusion.order_ref, s32[64,1,2]{2,1,0:T(1,128)} %copy-done.3, bf16[16,128,128]{2,1,0:T(8,128)(2,1)} %bitcast.20), custom_call_target="tpu_custom_call" | custom-call | tf_op jit(solution)/shard_map/pallas_call | solution.py:137
  32.3 0.0 copy-start
  32.3 0.0 copy-start.1
  32.3 0.0 copy-start.2
  32.3 110.9 %all_to_all.15 = bf16[64,2,128,128]{3,2,1,0:T(8,128)(2,1)S(1)} all-to-all(bf16[64,2,128,128]{3,2,1,0:T(8,128)(2,1)} %bitcast.19), channel_id=1, replica_groups=mesh['wide'=64,'narrow'=8] {'wide'}, dimensions={0} | all-to-all | bytes 8388608 | tf_op jit(solution)/shard_map/all_to_all | solution.py:235
  143.2 0.0 copy-done
  143.2 0.0 copy-done.1
  143.2 0.0 copy-done.2
  143.2 19.2 %shard_map.74 = bf16[128,128,128]{2,1,0:T(8,128)(2,1)S(1)} custom-call(s32[16]{0:T(128)S(1)} %multiply_add_fusion.slot_of_ref, s32[128]{0:T(128)S(1)} %get-tuple-element.11.slot_tile_ref, bf16[128,128,128]{2,1,0:T(8,128)(2,1)S(1)} %bitcast.16, bf16[16,128,128]{2,1,0:T(8,128)(2,1)S(1)} %copy-done, f32[128,128]{1,0:T(8,128)S(1)} %broadcast_in_dim.50.degree_ref, ...), custom_call_target="tpu_custom_call" | custom-call | tf_op jit(solution)/shard_map/pallas_call | solution.py:93
  162.4 121.5 %all_to_all.16 = bf16[64,2,128,128]{3,2,1,0:T(8,128)(2,1)} all-to-all(bf16[64,2,128,128]{3,2,1,0:T(8,128)(2,1)S(1)} %bitcast.17), channel_id=1, replica_groups=mesh['wide'=64,'narrow'=8] {'wide'}, dimensions={0} | all-to-all | bytes 8388608 | tf_op jit(solution)/shard_map/all_to_all | solution.py:253
  283.9 4.9 %shard_map.75 = bf16[16,128,128]{2,1,0:T(8,128)(2,1)} custom-call(s32[1]{0:T(128)} %bitcast.4.count_ref, s32[128]{0:T(128)} %select_reduce_fusion.order_ref, s32[64,1,2]{2,1,0:T(1,128)} %copy-done.3, bf16[128,128,128]{2,1,0:T(8,128)(2,1)} %bitcast.18, bf16[16,128,128]{2,1,0:T(8,128)(2,1)} %bitcast.21), custom_call_target="tpu_custom_call" | custom-call | tf_op jit(solution)/shard_map/pallas_call | solution.py:174
  (1 shorter events, 0.0 us)
Async XLA Ops:
  3.1 23.5 %all-to-all-start = ((s32[64,1,2]{2,1,0:T(1,128)}), s32[64,1,2]{2,1,0:T(1,128)S(1)}, u32[]{:S(2)}, u32[]{:S(2)}) async-start(s32[64,1,2]{2,1,0:T(1,128)} %bitcast.3), calls=%async_computation | async-start | bytes 65536 | tf_op jit(solution)/shard_map/all_to_all | solution.py:217
  26.6 1.9 copy-start.3
  32.3 110.9 %copy-start = (bf16[16,128,128]{2,1,0:T(8,128)(2,1)S(1)}, bf16[16,128,128]{2,1,0:T(8,128)(2,1)}, u32[]{:S(2)}) copy-start(bf16[16,128,128]{2,1,0:T(8,128)(2,1)} %tiles_ref.1) | copy-start | bytes 1572868
  32.3 110.9 %copy-start.1 = (bf16[128,512]{1,0:T(8,128)(2,1)S(1)}, bf16[128,512]{1,0:T(8,128)(2,1)}, u32[]{:S(2)}) copy-start(bf16[128,512]{1,0:T(8,128)(2,1)} %w_in_ref.1) | copy-start | bytes 393220
  32.3 110.9 %copy-start.2 = (bf16[512,128]{1,0:T(8,128)(2,1)S(1)}, bf16[512,128]{1,0:T(8,128)(2,1)}, u32[]{:S(2)}) copy-start(bf16[512,128]{1,0:T(8,128)(2,1)} %w_out_ref.1) | copy-start | bytes 393220
